TPU v7x, 32 devices: a whole 2x2x4 slice. The times are simulated.
32 devices in a mesh: seq: 8 (over y, x, core), head: 4 (over z).
Axes of the slice: x: 2, y: 2, z: 4, core: 2. Of those that a mesh axis runs over, the one named last changes fastest.
Arguments:
- prefix_k: bfloat16 [8, 4096, 1024], P('seq', None, 'head'), may hold values from -7 to 7
- prefix_v: bfloat16 [8, 4096, 1024], P('seq', None, 'head'), may hold values from -6 to 6
- queries: bfloat16 [4096, 4096], P('seq', 'head'), may hold values from -100 to 100
- suffix_k: bfloat16 [4096, 1024], P('seq', 'head'), may hold values from -6 to 6
- suffix_v: bfloat16 [4096, 1024], P('seq', 'head'), may hold values from -6 to 6
- residual: bfloat16 [4096, 8192], P('seq', 'head'), may hold values from -12 to 12
- out_weight: bfloat16 [8192, 4096], P('seq', 'head'), may hold values from -2 to 2
- norm_gain: float32 [8192], replicated, may hold values from 0.25 to 1.75
- value_weight: float32 [8192], replicated, may hold values from -0.0029296875 to 0.0029296875
- prompt_of: int32 [8], replicated, may hold values from 0 to 7
- suffix_len: int32 [8], replicated, may hold values from 128 to 512
- return_table: float32 [512], replicated, may hold values from -4 to 4
- return_index: int32 [4096], P('seq'), may hold values from 0 to 511
Outputs:
- cache_k: bfloat16 [8, 4096, 1024], P(None, 'seq', 'head')
- cache_v: bfloat16 [8, 4096, 1024], P(None, 'seq', 'head')
- hidden: bfloat16 [4096, 8192], P('seq', 'head')
- values: float32 [4096], P('seq')
- grad_out: float32 [8192, 4096], P('seq', 'head')
All inputs are finite; a program needn't handle non-finite values.
Results may differ from a plain program's by a relative error of at most 0.014.
Values may be sent and summed in bfloat16 or wider, within the bound.
No kernel may reach another device: no remote copies, remote signals or barrier semaphores. Data moves between devices by JAX's collectives and lax.ppermute only.
A program may use at most 192 MiB of HBM per device.

v0:
```python
import jax
import jax.numpy as jnp
from jax import lax
from jax.sharding import PartitionSpec as P

D = 8192
KVH = 8
HD = 128
HQ = 32
BINS = 512


EPSILON = 1e-05
MASKED = -1e30


def attention(query_rows, prompt_keys, prompt_values, own_keys, own_values):
    row_count = query_rows.shape[0]
    kv_heads = prompt_keys.shape[1] // HD
    group_size = HQ // KVH
    prefix_count = prompt_keys.shape[0]
    key_rows = jnp.concatenate([prompt_keys, own_keys], 0)
    span_len = key_rows.shape[0]
    key_rows = key_rows.reshape(span_len, kv_heads, HD)
    value_rows = jnp.concatenate([prompt_values, own_values], 0).reshape(span_len, kv_heads, HD)
    query_block = query_rows.reshape(row_count, kv_heads, group_size, HD)
    scores = jnp.einsum(
        "skgd,lkd->kgsl", query_block, key_rows, preferred_element_type=jnp.float32
    ) * HD ** (-0.5)
    key_pos = jnp.arange(span_len)[None, :]
    query_pos = jnp.arange(row_count)[:, None]
    allowed = (key_pos < prefix_count) | (key_pos - prefix_count <= query_pos)
    scores = jnp.where(allowed, scores, MASKED)
    row_max = jnp.max(scores, -1, keepdims=True)
    weights = jnp.exp(scores - row_max)
    totals = jnp.sum(weights, -1, keepdims=True)
    mixed = jnp.einsum(
        "kgsl,lkd->skgd",
        weights.astype(jnp.bfloat16),
        value_rows,
        preferred_element_type=jnp.float32,
    )
    mixed = mixed / jnp.transpose(totals, (2, 0, 1, 3))
    return mixed.reshape(row_count, kv_heads * group_size * HD).astype(jnp.bfloat16)


def local(
    prefix_k,
    prefix_v,
    queries,
    suffix_k,
    suffix_v,
    residual,
    out_weight,
    norm_gain,
    value_weight,
    prompt_of,
    suffix_len,
    return_table,
    return_index,
):
    cache_k, cache_v = (
        lax.all_to_all(prefix_k, "seq", split_axis=1, concat_axis=0, tiled=True),
        lax.all_to_all(prefix_v, "seq", split_axis=1, concat_axis=0, tiled=True),
    )
    chosen_k = jnp.take(cache_k, prompt_of, axis=0)
    chosen_v = jnp.take(cache_v, prompt_of, axis=0)
    fetched_k, fetched_v = (
        lax.all_to_all(chosen_k, "seq", split_axis=0, concat_axis=1, tiled=True),
        lax.all_to_all(chosen_v, "seq", split_axis=0, concat_axis=1, tiled=True),
    )
    attn = attention(queries, fetched_k[0], fetched_v[0], suffix_k, suffix_v)
    partial_value = lax.dot_general(
        attn,
        lax.all_gather(out_weight, "seq", axis=0, tiled=True),
        (((1,), (1,)), ((), ())),
        preferred_element_type=jnp.float32,
    )
    row_count = residual.shape[0]
    local_width = residual.shape[1]
    head_start = lax.axis_index("head") * local_width
    gain_weight = norm_gain * value_weight
    one_hot = (return_index[:, None] == jnp.arange(BINS)[None, :]).astype(jnp.float32)
    target = jnp.dot(one_hot, return_table, precision=lax.Precision.HIGHEST)
    live = jnp.arange(row_count) < suffix_len[lax.axis_index("seq")]
    totals = lax.psum(partial_value.astype(jnp.bfloat16), "head").astype(jnp.float32)
    residual_full = lax.all_gather(residual, "head", axis=1, tiled=True)
    hidden_full = (residual_full.astype(jnp.float32) + totals).astype(jnp.bfloat16)
    hidden_wide = hidden_full.astype(jnp.float32)
    square_sum = jnp.sum(hidden_wide * hidden_wide, 1)
    weighted_sum = jnp.sum(hidden_wide * gain_weight[None, :], 1)
    inverse = lax.rsqrt(square_sum / D + EPSILON)
    value_rows = weighted_sum * inverse
    error_term = jnp.where(live, value_rows - target, 0.0)
    hidden_grad = (
        error_term[:, None]
        * (
            inverse[:, None] * gain_weight[None, :]
            - (weighted_sum * inverse * inverse * inverse)[:, None] * hidden_wide / D
        )
    ).astype(jnp.bfloat16)
    hidden_out = lax.dynamic_slice_in_dim(hidden_full, head_start, local_width, 1)
    grad_out = lax.psum_scatter(
        lax.dot_general(
            hidden_grad, attn, (((0,), (0,)), ((), ())), preferred_element_type=jnp.float32
        ).astype(jnp.bfloat16),
        "seq",
        scatter_dimension=0,
        tiled=True,
    ).astype(jnp.float32)
    return (cache_k, cache_v, hidden_out, value_rows, grad_out)


def solution(mesh):
    in_specs = (
        P("seq", None, "head"),
        P("seq", None, "head"),
        P("seq", "head"),
        P("seq", "head"),
        P("seq", "head"),
        P("seq", "head"),
        P("seq", "head"),
        P(),
        P(),
        P(),
        P(),
        P(),
        P("seq"),
    )
    out_specs = (
        P(None, "seq", "head"),
        P(None, "seq", "head"),
        P("seq", "head"),
        P("seq"),
        P("seq", "head"),
    )
    return jax.shard_map(local, mesh=mesh, in_specs=in_specs, out_specs=out_specs, check_vma=False)
```

profile of v0, /device:TPU:0, one launch (start us, length us, event | category | flops | bytes accessed | tf_op | source)
XLA Modules:
  0.0 764.6 jit_solution(6455849590809250505)
XLA Ops:
  7.9 7.5 copy.64
  15.9 21.6 %reduce.1 = bf16[4096,256]{1,0:T(8,128)(2,1)S(1)} reduce(bf16[4096,1,256]{2,1,0:T(2,128)(2,1)} %bitcast.55, bf16[]{:T(256)} %broadcast.78), dimensions={1}, to_apply=%bitcast.52.reduce_sub_computation | reduce | bytes 4194306
  40.7 5.3 all-to-all-start.1
  45.9 7.5 copy.65
  53.4 23.1 %reduce = bf16[4096,256]{1,0:T(8,128)(2,1)} reduce(bf16[4096,1,256]{2,1,0:T(2,128)(2,1)} %bitcast.56, bf16[]{:T(256)} %broadcast.78), dimensions={1}, to_apply=%bitcast.53.reduce_sub_computation | reduce | bytes 4194306
  76.4 5.8 reshape.97
  82.3 7.4 all-to-all-done.1
  89.7 4.4 all-to-all-start
  94.1 4.3 reshape.100
  101.0 39.0 %all-to-all-done = bf16[8,2,65536]{2,1,0:T(2,128)(2,1)} async-done(((bf16[8,2,65536]{2,1,0:T(2,128)(2,1)}), bf16[8,2,65536]{2,1,0:T(2,128)(2,1)}, u32[]{:S(2)}, u32[]{:S(2)}) %all-to-all-start) | async-done | bytes 2097184 | tf_op jit(solution)/shard_map/all_to_all | solution.py:63
  140.0 6.7 reshape.98
  160.5 4.5 all-to-all-start.3
  171.7 19.9 %all-to-all-done.3 = bf16[8,512,256]{2,1,0:T(8,128)(2,1)} async-done(((bf16[8,512,256]{2,1,0:T(8,128)(2,1)}), bf16[8,512,256]{2,1,0:T(8,128)(2,1)}, u32[]{:S(2)}, u32[]{:S(2)}) %all-to-all-start.3) | async-done | bytes 2097184 | tf_op jit(solution)/shard_map/all_to_all | solution.py:69
  191.6 4.4 all-to-all-start.2
  203.4 28.3 %fusion.2 = (f32[2,4,512]{2,1,0:T(4,128)S(1)}, f32[2,4608,512,4]{2,1,3,0:T(8,128)}) fusion(pred[512,4608]{0,1:T(8,128)(4,1)S(1)} %fusion.12, bf16[512,2,4,128]{3,2,1,0:T(4,128)(2,1)S(1)} %reshape.68, bf16[512,2,128]{2,0,1:T(8,128)(2,1)} %copy.47, bf16[4096,2,128]{2,0,1:T(8,128)(2,1)} %copy.46), kind=kOutput, calls=%fused_computation.6 | convolution fusion | flops 4893175808 | bytes 81281024 | tf_op jit(solution)/shard_map/skgd,lkd->kgsl/dot_general | solution.py:27
  235.7 6.1 copy.53
  241.8 24.4 %fusion = f32[2,4,512]{2,1,0:T(4,128)S(1)} fusion(f32[2,4608,512,4]{2,1,3,0:T(8,128)} %get-tuple-element.15, f32[2,4,512]{2,1,0:T(4,128)S(1)} %get-tuple-element.14, pred[512,4608]{0,1:T(8,128)(4,1)S(1)} %fusion.12), kind=kLoop, calls=%fused_computation.4 | loop fusion | flops 75493376 | bytes 77889536 | tf_op jit(solution)/shard_map/reduce_sum | solution.py:36
  266.2 29.5 %fusion.24 = bf16[512,2,4,128]{0,3,2,1:T(8,128)(2,1)} fusion(f32[2,4608,512,4]{2,1,3,0:T(8,128)} %get-tuple-element.15, f32[2,4,512]{2,1,0:T(4,128)S(1)} %get-tuple-element.14, pred[512,4608]{0,1:T(8,128)(4,1)S(1)} %fusion.12, bf16[512,2,128]{0,2,1:T(8,128)(2,1)S(1)} %bitcast.64, bf16[4096,2,128]{0,2,1:T(8,128)(2,1)} %copy.53, f32[512,2,4]{0,2,1:T(4,128)S(1)} %bitcast.65), kind=kOutput, calls=%fused_computation.36 | convolution fusion | flops 4913102848 | bytes 81297408 | tf_op jit(solution)/shard_map/kgsl,lkd->skgd/dot_general | solution.py:37
  295.7 14.8 %convolution_convert_fusion.1 = bf16[512,8192]{1,0:T(8,128)(2,1)} fusion(bf16[512,1024]{0,1:T(8,128)(2,1)} %bitcast.67, bf16[8192,1024]{1,0:T(8,128)(2,1)} %all-gather.5.cloned.1.call-done), kind=kOutput, calls=%fused_computation.20 | convolution fusion | flops 8594128896 | bytes 26214400 | tf_op jit(solution)/shard_map/dot_general | solution.py:73
  312.6 6.1 all-gather.3.cloned.1.call-done
  318.7 291.5 %all-reduce.2.cloned.1.call-done = bf16[512,8192]{1,0:T(8,128)(2,1)} async-done(((bf16[512,8192]{1,0:T(8,128)(2,1)}), bf16[512,8192]{1,0:T(8,128)(2,1)}) %all-reduce.2.cloned.1.call-update) | async-done | bytes 8388624 | tf_op jit(solution)/shard_map/psum | solution.py:86
  610.2 10.7 %fusion.7 = (f32[512]{0:T(512)S(1)}, f32[512]{0:T(512)S(1)}, bf16[512,8192]{1,0:T(8,128)(2,1)}) fusion(f32[8192]{0:T(1024)S(1)} %mul.79, bf16[512,8192]{1,0:T(8,128)(2,1)} %all-reduce.2.cloned.1.call-done, bf16[512,8192]{1,0:T(8,128)(2,1)} %all-gather.3.cloned.1.call-done), kind=kLoop, calls=%fused_computation.13 | loop fusion | flops 37747712 | bytes 25202688 | tf_op jit(solution)/shard_map/reduce_sum | solution.py:90
  621.7 17.0 %convolution_convert_fusion = bf16[8192,1024]{1,0:T(8,128)(2,1)} fusion(bf16[512,1024]{0,1:T(8,128)(2,1)S(1)} %bitcast.68, bf16[512,8192]{1,0:T(8,128)(2,1)} %get-tuple-element.10, f32[512]{0:T(512)S(1)} %multiply_multiply_fusion, f32[512]{0:T(512)S(1)} %get-tuple-element.11, f32[512]{0:T(512)S(1)} %get-tuple-element.8, f32[8192]{0:T(1024)S(1)} %mul.79), kind=kOutput, calls=%fused_computation.19 | convolution fusion | flops 8627683328 | bytes 26253312 | tf_op jit(solution)/shard_map/dot_general | solution.py:104
  641.8 112.2 %reduce-scatter.2.cloned.1.call-done = bf16[1024,1024]{1,0:T(8,128)(2,1)} async-done(((bf16[8192,1024]{1,0:T(8,128)(2,1)}), bf16[1024,1024]{1,0:T(8,128)(2,1)}) %reduce-scatter.2.cloned.1.call-update) | async-done | bytes 2097168 | tf_op jit(solution)/shard_map/reduce_scatter | solution.py:103
  (65 shorter events, 48.6 us)
Async XLA Ops:
  7.2 304.7 %copy-start = (f32[512]{0:T(512)S(1)}, f32[512]{0:T(512)}, u32[]{:S(2)}) copy-start(f32[512]{0:T(512)} %param.26) | copy-start | bytes 6148
  7.2 288.5 %all-gather.5.cloned.1.call-start = ((), (), s32[]{:S(2)}) async-start(), calls=%async_computation.6 | async-start | bytes 18874368 | tf_op jit(solution)/shard_map/all_gather | solution.py:75
  40.7 49.0 %all-to-all-start.1 = ((bf16[8,2,65536]{2,1,0:T(2,128)(2,1)}), bf16[8,2,65536]{2,1,0:T(2,128)(2,1)S(1)}, u32[]{:S(2)}, u32[]{:S(2)}) async-start(bf16[8,2,65536]{2,1,0:T(2,128)(2,1)} %reshape.99), calls=%async_computation.1 | async-start | bytes 4194304 | tf_op jit(solution)/shard_map/all_to_all | solution.py:64
  76.4 17.6 %copy-start.11 = (s32[8]{0:T(128)S(1)}, s32[8]{0:T(128)}, u32[]{:S(2)}) copy-start(s32[8]{0:T(128)} %param.24) | copy-start | bytes 100
  89.7 50.3 %all-to-all-start = ((bf16[8,2,65536]{2,1,0:T(2,128)(2,1)}), bf16[8,2,65536]{2,1,0:T(2,128)(2,1)}, u32[]{:S(2)}, u32[]{:S(2)}) async-start(bf16[8,2,65536]{2,1,0:T(2,128)(2,1)} %reshape.97), calls=%async_computation | async-start | bytes 4194304 | tf_op jit(solution)/shard_map/all_to_all | solution.py:63
  101.0 49.6 %copy-start.1 = (bf16[1,4096,256]{2,1,0:T(8,128)(2,1)}, bf16[1,4096,256]{2,1,0:T(8,128)(2,1)S(1)}, u32[]{:S(2)}) copy-start(bf16[1,4096,256]{2,1,0:T(8,128)(2,1)S(1)} %copy.57) | copy-start | bytes 6291460
  152.6 3.7 copy-start.2
  160.5 5.3 copy-start.3
  160.5 6.0 copy-start.4
  160.5 7.0 copy-start.5
  160.5 31.1 %all-to-all-start.3 = ((bf16[8,512,256]{2,1,0:T(8,128)(2,1)}), bf16[8,512,256]{2,1,0:T(8,128)(2,1)}, u32[]{:S(2)}, u32[]{:S(2)}) async-start(bf16[8,512,256]{2,1,0:T(8,128)(2,1)} %get-tuple-element.13), calls=%async_computation.3 | async-start | bytes 4194304 | tf_op jit(solution)/shard_map/all_to_all | solution.py:69
  165.0 153.7 %all-gather.3.cloned.1.call-start = ((), (), s32[]{:S(2)}) async-start(), calls=%async_computation.5 | async-start | bytes 10485760 | tf_op jit(solution)/shard_map/all_gather | solution.py:87
  191.6 40.1 %all-to-all-start.2 = ((bf16[8,512,256]{2,1,0:T(8,128)(2,1)}), bf16[8,512,256]{2,1,0:T(8,128)(2,1)}, u32[]{:S(2)}, u32[]{:S(2)}) async-start(bf16[8,512,256]{2,1,0:T(8,128)(2,1)} %get-tuple-element.12), calls=%async_computation.2 | async-start | bytes 4194304 | tf_op jit(solution)/shard_map/all_to_all | solution.py:70
  196.0 414.2 %all-reduce.2.cloned.1.call-start = ((), (), s32[]{:S(2)}) async-start(), calls=%async_computation.7 | async-start | bytes 16777216 | tf_op jit(solution)/shard_map/psum | solution.py:86
  241.8 24.4 %copy-start.6 = (bf16[512,256]{0,1:T(8,128)(2,1)S(1)}, bf16[512,256]{0,1:T(8,128)(2,1)}, u32[]{:S(2)}) copy-start(bf16[512,256]{0,1:T(8,128)(2,1)} %copy.43) | copy-start | bytes 786436
  310.5 0.8 copy-start.7
  310.5 0.8 copy-start.8
  310.5 0.8 copy-start.12
  310.5 1.4 copy-start.10
  310.6 443.4 %reduce-scatter.2.cloned.1.call-start = ((), (), s32[]{:S(2)}) async-start(), calls=%async_computation.8 | async-start | bytes 18874368 | tf_op jit(solution)/shard_map/reduce_scatter | solution.py:103
  312.5 309.1 %copy-start.13 = (bf16[512,2,4,128]{0,3,2,1:T(8,128)(2,1)S(1)}, bf16[512,2,4,128]{0,3,2,1:T(8,128)(2,1)}, u32[]{:S(2)}) copy-start(bf16[512,2,4,128]{0,3,2,1:T(8,128)(2,1)} %fusion.24) | copy-start | bytes 3145732
  621.6 17.0 %copy-start.9 = (f32[512]{0:T(512)}, f32[512]{0:T(512)S(1)}, u32[]{:S(2)}) copy-start(f32[512]{0:T(512)S(1)} %get-tuple-element.9) | copy-start | bytes 6148
Sparse Core Ops, SparseCore 0:
  9.9 127.5 all-gather.4
  167.4 151.2 all-gather.2
  321.2 289.0 all-reduce.1
  638.8 115.1 reduce-scatter.1
where the time goes:
time: 766 us; the launch traced here: 765 us
  waiting for transfers between devices  478 us (62%)
  other arithmetic  92 us (12%)
  matrix products  90.3 us (12%)
  local copies, waits for them, and re-layouts  72 us (9%)
  starting transfers between devices  18.8 us (2%)
  between operations  14 us (2%)
    psum x1, waiting for transfers between devices, local(): lax.psum(partial_value.astype(jnp.bfloat16), 'head').astype(jnp.float32)  292 us
    reduce_scatter x1, waiting for transfers between devices, local(): lax.psum_scatter(lax.dot_general(hidden_grad, attn, (((0,), (0,)), ((), (...  112 us
    unnamed x2, other arithmetic  44.7 us
    unnamed x39, local copies, waits for them, and re-layouts  43.6 us
    all_to_all x1, waiting for transfers between devices, local(): lax.all_to_all(prefix_k, 'seq', split_axis=1, concat_axis=0, tiled=True)  39 us
    dot_general x1, matrix products, attention(): jnp.einsum('kgsl,lkd->skgd', weights.astype(jnp.bfloat16), value_rows, pr...  29.5 us
    dot_general x1, matrix products, attention(): jnp.einsum('skgd,lkd->kgsl', query_block, key_rows, preferred_element_typ...  28.3 us
    reduce_sum x1, other arithmetic, attention(): totals = jnp.sum(weights, -1, keepdims=True)  24.4 us
  transfers between devices with their start and end apart: 8, of which 6 were waited for; matrix products, arithmetic and copies ran while one was open for 29% of the time, Pallas kernels for 0%

commit v1 on v0

v1 whole, which is shorter than its diff:
```python
import functools
import math

import jax
import jax.numpy as jnp
from jax import lax
from jax.experimental import pallas as pl
from jax.experimental.pallas import tpu as pltpu
from jax.sharding import PartitionSpec as P


HD = 128
EPSILON = 1e-05
MASKED = -1e30
BF = jnp.bfloat16
F32 = jnp.float32
VMEM_LIMIT = 60 * 1024 * 1024


def tie(x, *deps):
    return lax.optimization_barrier((x, *deps))[0]


def shift_perm(count, step):
    return [(i, (i + step) % count) for i in range(count)]


def xor_perm(count, mask):
    return [(i, i ^ mask) for i in range(count)]


def dot_t(a, b):
    return lax.dot_general(a, b, (((1,), (1,)), ((), ())), preferred_element_type=F32)


def dot(a, b):
    return lax.dot_general(a, b, (((1,), (0,)), ((), ())), preferred_element_type=F32)


def attention_kernel(blocks, *refs):
    q_ref = refs[0]
    kv = refs[1 : 1 + blocks]
    sk_ref, sv_ref = refs[1 + blocks : 3 + blocks]
    o_ref, v_wide, scores = refs[-3:]
    tile = q_ref.shape[0]
    block_len = kv[0].shape[1]
    own_len = sk_ref.shape[0]
    prefix_len = blocks * block_len
    scale = HD ** (-0.5) / math.log(2.0)

    @pl.when((pl.program_id(0) == 0) & (pl.program_id(1) == 0))
    def _():
        for b in range(blocks):
            v_wide[b * block_len : (b + 1) * block_len, :HD] = kv[b][1]
        v_wide[prefix_len:, :HD] = sv_ref[...]
        v_wide[:, HD:] = jnp.ones((prefix_len + own_len, HD), BF)

    q = q_ref[...]
    spans = [(b * block_len, block_len) for b in range(blocks)]
    top = jnp.full((tile, HD), MASKED, F32)
    for b, (start, size) in enumerate(spans):
        s = dot_t(q, kv[b][0])
        scores[:, start : start + size] = s
        for lane in range(0, size, HD):
            top = jnp.maximum(top, s[:, lane : lane + HD])
    s = dot_t(q, sk_ref[...])
    row = lax.broadcasted_iota(jnp.int32, (tile, own_len), 0) + pl.program_id(1) * tile
    col = lax.broadcasted_iota(jnp.int32, (tile, own_len), 1)
    s = jnp.where(col <= row, s, MASKED)
    scores[:, prefix_len:] = s
    for lane in range(0, own_len, HD):
        top = jnp.maximum(top, s[:, lane : lane + HD])
    row_max = jnp.max(top, 1, keepdims=True)
    mixed = jnp.zeros((tile, 2 * HD), F32)
    for start, size in spans + [(prefix_len, own_len)]:
        p = jnp.exp2((scores[:, start : start + size] - row_max) * scale)
        mixed = mixed + dot(p.astype(BF), v_wide[start : start + size, :])
    o_ref[...] = (mixed[:, :HD] / mixed[:, HD:]).astype(BF)


def attention(queries, kv, suffix_k, suffix_v, head, group, first, count, before=None):
    rows = queries.shape[0]
    tile = 256
    blocks = len(kv)
    block_len = kv[0].shape[1]
    span = blocks * block_len + rows
    extra = [] if before is None else [before]
    return pl.pallas_call(
        functools.partial(attention_kernel, blocks),
        out_shape=jax.ShapeDtypeStruct((rows, group * HD), BF),
        grid=(count, rows // tile),
        in_specs=[pl.BlockSpec((tile, HD), lambda j, i: (i, head * group + first + j))]
        + [pl.BlockSpec(kv[0].shape, lambda j, i: (0, 0, 0))] * blocks
        + [pl.BlockSpec((rows, HD), lambda j, i: (0, head))] * 2
        + [pl.BlockSpec(memory_space=pl.ANY)] * len(extra),
        out_specs=pl.BlockSpec((tile, HD), lambda j, i: (i, first + j)),
        scratch_shapes=[pltpu.VMEM((span, 2 * HD), BF), pltpu.VMEM((tile, span), F32)],
        input_output_aliases={3 + blocks: 0} if extra else {},
        compiler_params=pltpu.CompilerParams(vmem_limit_bytes=VMEM_LIMIT),
        cost_estimate=pl.CostEstimate(
            flops=4 * rows * count * span * HD, bytes_accessed=4 * span * HD, transcendentals=rows * count * span
        ),
        name="attend",
    )(queries, *kv, suffix_k, suffix_v, *extra)


def route_kernel(count, head, *refs):
    pick, slot = refs[0], refs[1]
    came = refs[2 : 2 + count]
    outs = refs[-(count + 5) : -5]
    cache_k, cache_v, held, in_sem, out_sem = refs[-5:]
    for m in range(count):
        pltpu.make_async_copy(came[m], held.at[m], in_sem.at[m]).start()
    for m in range(count):
        pltpu.make_async_copy(came[m], held.at[m], in_sem.at[m]).wait()
    copies = [pltpu.make_async_copy(held.at[pick[m]], outs[m], out_sem.at[0, m]) for m in range(count)]
    cut = pl.ds(head * HD, HD)
    for which, cache in enumerate((cache_k, cache_v)):
        for m in range(count):
            copies.append(
                pltpu.make_async_copy(held.at[m, which], cache.at[slot[m], :, cut], out_sem.at[1 + which, m])
            )
    for copy in copies:
        copy.start()
    for copy in copies:
        copy.wait()


def route(pick, slot, came, head, kv_heads, caches):
    count = len(came)
    _, block_len, _ = came[0].shape
    cache = jax.ShapeDtypeStruct((count, block_len, kv_heads * HD), BF)
    smem_spec = pl.BlockSpec(memory_space=pltpu.SMEM)
    any_spec = pl.BlockSpec(memory_space=pl.ANY)
    extra = list(caches)
    outs = pl.pallas_call(
        functools.partial(route_kernel, count, head),
        out_shape=(jax.ShapeDtypeStruct(came[0].shape, BF),) * count + (cache, cache),
        in_specs=[smem_spec] * 2 + [any_spec] * (count + len(extra)),
        out_specs=(any_spec,) * (count + 2),
        scratch_shapes=[
            pltpu.VMEM((count, *came[0].shape), BF),
            pltpu.SemaphoreType.DMA((count,)),
            pltpu.SemaphoreType.DMA((3, count)),
        ],
        input_output_aliases={2 + count: count, 3 + count: count + 1} if extra else {},
        compiler_params=pltpu.CompilerParams(vmem_limit_bytes=VMEM_LIMIT),
        cost_estimate=pl.CostEstimate(flops=0, bytes_accessed=8 * 1024 * 1024, transcendentals=0),
        name="route",
    )(pick, slot, *came, *extra)
    return outs[:count], outs[count:]


def project_kernel(planes, parts, chips, *refs):
    pieces = planes * parts
    where_ref = refs[0]
    own = refs[1 : 1 + pieces]
    other = refs[1 + pieces : 1 + 2 * pieces]
    weights = refs[1 + 2 * pieces : 1 + 2 * pieces + 2 * chips]
    res_own, res_other, gain, h_own, h_other, h_flip, sums, a_buf, w_buf, a_sem, w_sem = refs[-11:]
    half = planes // 2
    width = own[0].shape[1]
    block = width * parts
    rows = own[0].shape[0]
    chip = where_ref[0]
    plane = where_ref[1]

    def a_copy(side, p):
        src = (own, other)[side][p]
        return pltpu.make_async_copy(src, a_buf.at[side, :, p * width : (p + 1) * width], a_sem.at[side, p])

    def w_copy(e, t):
        return pltpu.make_async_copy(
            weights[2 * e + t // half].at[t % half], w_buf.at[e, :, t * block : (t + 1) * block], w_sem.at[e, t]
        )

    for p in range(pieces):
        a_copy(0, p).start()
    for t in range(planes):
        w_copy(0, t).start()
    for p in range(pieces):
        a_copy(1, p).start()
    for e in range(1, chips):
        for t in range(planes):
            w_copy(e, t).start()
    for p in range(pieces):
        a_copy(0, p).wait()
    for p in range(pieces):
        a_copy(1, p).wait()
    sums[...] = jnp.zeros_like(sums)

    @pl.loop(0, chips)
    def _(e):
        for t in range(planes):
            landed = w_buf.at[e, :, t * block : (t + 1) * block]
            pltpu.make_async_copy(landed, landed, w_sem.at[e, t]).wait()
        home = jnp.bitwise_xor(chip, e)
        gain_col = gain[home]
        came = lax.rem(plane - home + planes, planes)
        goes = lax.rem(home - plane + planes, planes)
        for side, (res, out) in enumerate(((res_own, h_own), (res_other, h_other))):
            total = dot_t(a_buf[side], w_buf[e])
            h = (res[came].astype(F32) + total).astype(BF)
            out[goes] = h
            flip = h.astype(F32).T
            h_flip[e, :, side * rows : (side + 1) * rows] = flip.astype(BF)
            sums[2 * side : 2 * side + 1, :] += jnp.sum(flip * flip, 0, keepdims=True)
            sums[2 * side + 1 : 2 * side + 2, :] += jnp.sum(flip * gain_col, 0, keepdims=True)


def project(where, own, other, weights, res_own, res_other, gain, planes, parts):
    chips = len(weights) // 2
    rows, width = own[0].shape
    features = weights[0].shape[1]
    depth = planes * parts * width
    shape = jax.ShapeDtypeStruct
    any_spec = pl.BlockSpec(memory_space=pl.ANY)
    vmem_spec = pl.BlockSpec(memory_space=pltpu.VMEM)
    return pl.pallas_call(
        functools.partial(project_kernel, planes, parts, chips),
        out_shape=(
            shape((chips, rows, features), BF),
            shape((chips, rows, features), BF),
            shape((chips, features, 2 * rows), BF),
            shape((8, rows), F32),
        ),
        in_specs=[pl.BlockSpec(memory_space=pltpu.SMEM)]
        + [any_spec] * (2 * planes * parts + 2 * chips)
        + [vmem_spec] * 3,
        out_specs=(vmem_spec,) * 4,
        scratch_shapes=[
            pltpu.VMEM((2, rows, depth), BF),
            pltpu.VMEM((chips, features, depth), BF),
            pltpu.SemaphoreType.DMA((2, planes * parts)),
            pltpu.SemaphoreType.DMA((chips, planes)),
        ],
        compiler_params=pltpu.CompilerParams(vmem_limit_bytes=VMEM_LIMIT),
        cost_estimate=pl.CostEstimate(
            flops=4 * rows * features * chips * depth, bytes_accessed=24 * 1024 * 1024, transcendentals=0
        ),
        name="project",
    )(where, *own, *other, *weights, res_own, res_other, gain)


def gradient_kernel(parts, chips, *refs):
    grad = refs[0]
    own = refs[1 : 1 + parts]
    other = refs[1 + parts : 1 + 2 * parts]
    outs = refs[1 + 2 * parts :]
    rows, width = own[0].shape
    for e in range(chips):
        for g in range(parts):
            total = dot(grad[e, :, :rows], own[g][...]) + dot(grad[e, :, rows:], other[g][...])
            outs[e][:, g * width : (g + 1) * width] = total.astype(BF)


def gradient(grad, own, other):
    chips, features, tokens = grad.shape
    parts = len(own)
    width = own[0].shape[1]
    vmem_spec = pl.BlockSpec(memory_space=pltpu.VMEM)
    return pl.pallas_call(
        functools.partial(gradient_kernel, parts, chips),
        out_shape=(jax.ShapeDtypeStruct((features, parts * width), BF),) * chips,
        in_specs=[vmem_spec] * (1 + 2 * parts),
        out_specs=(vmem_spec,) * chips,
        compiler_params=pltpu.CompilerParams(vmem_limit_bytes=VMEM_LIMIT),
        cost_estimate=pl.CostEstimate(
            flops=2 * chips * features * tokens * parts * width, bytes_accessed=8 * 1024 * 1024, transcendentals=0
        ),
        name="gradient",
    )(grad, *own, *other)


def place_kernel(count, axis, size, *refs):
    where_ref = refs[0]
    out = refs[-1]
    for i in range(count):
        start = pl.multiple_of(where_ref[i] * size, size)
        piece = refs[1 + i][...].astype(out.dtype)
        if axis == 0:
            out[pl.ds(start, size), :] = piece
        else:
            out[:, pl.ds(start, size)] = piece


def place(slots, pieces, axis, dtype):
    shape = list(pieces[0].shape)
    size = shape[axis]
    if axis == 1 and size % HD:
        order = jnp.argsort(slots)
        stacked = jnp.take(jnp.stack(pieces, 0), order, axis=0, mode="clip")
        return jnp.concatenate([stacked[i] for i in range(len(pieces))], 1).astype(dtype)
    shape[axis] *= len(pieces)
    vmem_spec = pl.BlockSpec(memory_space=pltpu.VMEM)
    return pl.pallas_call(
        functools.partial(place_kernel, len(pieces), axis, size),
        out_shape=jax.ShapeDtypeStruct(tuple(shape), dtype),
        in_specs=[pl.BlockSpec(memory_space=pltpu.SMEM)] + [vmem_spec] * len(pieces),
        out_specs=vmem_spec,
        compiler_params=pltpu.CompilerParams(vmem_limit_bytes=VMEM_LIMIT),
        cost_estimate=pl.CostEstimate(flops=0, bytes_accessed=6 * 1024 * 1024, transcendentals=0),
        name="place",
    )(slots.astype(jnp.int32), *pieces)


def local(n_seq, n_head, prefix_k, prefix_v, queries, suffix_k, suffix_v, residual, out_weight,
          norm_gain, value_weight, prompt_of, suffix_len, return_table, return_index):
    chips = n_seq // 2
    bits = [1 << b for b in range(chips.bit_length() - 1)]
    rows = queries.shape[0]
    local_width = residual.shape[1]
    model = local_width * n_head
    kv_heads = prefix_k.shape[2] // HD
    group = queries.shape[1] // (kv_heads * HD)
    positions = prefix_k.shape[1]
    block_len = positions // n_seq
    seq = lax.axis_index("seq")
    plane = lax.axis_index("head")
    chip, core = seq // 2, seq % 2

    def seq_send(x, mask):
        return lax.ppermute(x, "seq", xor_perm(n_seq, mask))

    def partner(x):
        return seq_send(x, 1)

    def chip_send(x, bit):
        return seq_send(x, 2 * bit)

    def plane_send(x, step):
        return lax.ppermute(x, "head", shift_perm(n_head, step))

    def next_plane(step):
        return (plane + step) % n_head

    def plane_send(x, step):
        return lax.ppermute(x, "head", shift_perm(n_head, step))

    def next_plane(step):
        return (plane + step) % n_head

    peers = [seq ^ m for m in range(n_seq)]
    moved = []
    for head in range(kv_heads):
        cut = slice(head * HD, (head + 1) * HD)
        came = []
        for m, peer in enumerate(peers):
            k, v = (
                lax.dynamic_slice_in_dim(source[0, :, cut], peer * block_len, block_len, 0)
                for source in (prefix_k, prefix_v)
            )
            piece = jnp.stack([k, v], 0)
            came.append(seq_send(piece, m) if m else piece)
        moved.append(came)

    weight_rows = out_weight.shape[0] // n_head
    w_own = []
    for t in range(n_head):
        piece = lax.dynamic_slice_in_dim(out_weight, next_plane(t) * weight_rows, weight_rows, 0)
        w_own.append(plane_send(piece, t) if t else piece)
    w_own = [jnp.stack(w_own[: n_head // 2], 0), jnp.stack(w_own[n_head // 2 :], 0)]

    res = residual.reshape(rows, 2, n_head, weight_rows)
    res_own, res_other = [], []
    for t in range(n_head):
        piece = lax.dynamic_index_in_dim(res, next_plane(t), 2, keepdims=False)
        mine = lax.dynamic_index_in_dim(piece, core, 1, keepdims=False)
        yours = lax.dynamic_index_in_dim(piece, 1 - core, 1, keepdims=False)
        if t:
            both = tie(jnp.stack([mine, yours], 0), *w_own)
            both = plane_send(both, t)
            mine, yours = both[0], both[1]
        res_own.append(mine)
        res_other.append(yours)
    res_own = jnp.stack(res_own, 0)
    res_other = partner(jnp.stack(res_other, 0))

    gain_weight = norm_gain * value_weight
    gain = gain_weight.reshape(chips, 2, n_head, weight_rows)
    gain = lax.dynamic_index_in_dim(gain, core, 1, keepdims=False)
    gain = lax.dynamic_index_in_dim(gain, plane, 1, keepdims=False)

    bins = return_table.shape[0]
    one_hot = return_index[:, None] == jnp.arange(bins)[None, :]
    target = jnp.sum(jnp.where(one_hot, return_table[None, :], 0.0), 1)
    target_other = partner(target)

    slot = jnp.stack(peers).astype(jnp.int32)
    pick = (jnp.take(prompt_of, slot, mode="clip") ^ seq).astype(jnp.int32)
    attn = []
    caches = ()
    begun = None
    count = max(group // 2, 1)
    for head in range(kv_heads):
        came = moved[head]
        if begun is not None:
            came = list(lax.optimization_barrier((*came, begun))[:-1])
        chosen, caches = route(pick, slot, came, head, kv_heads, caches)
        kv = [chosen[0]] + [seq_send(c, m) for m, c in enumerate(chosen) if m]
        part = None
        for step, first in enumerate(range(0, group, count)):
            part = attention(queries, kv, suffix_k, suffix_v, head, group, first, count, part)
            if not step:
                begun = part
        attn.append(part)
    cache_k, cache_v = caches

    w_own = list(lax.optimization_barrier((*w_own, *kv))[:2])
    weights = [w_own] + [None] * (chips - 1)
    for e in sorted(range(1, chips), key=lambda v: bin(v).count("1")):
        low, high = e & -e, 1 << (e.bit_length() - 1)
        if low == high:
            pair = [None, None]
            for part in (1, 0) if low == 1 else (0, 1):
                pair[part] = chip_send(w_own[part], e)
            weights[e] = pair
        else:
            weights[e] = [chip_send(weights[e ^ low][0], low), chip_send(weights[e ^ high][1], high)]

    own = [[None] * kv_heads for _ in range(n_head)]
    other = [[None] * kv_heads for _ in range(n_head)]
    for g in range(kv_heads):
        piece = attn[g]
        for t in range(n_head):
            own[t][g] = piece
            other[t][g] = partner(piece)
            if t + 1 < n_head:
                piece = plane_send(piece, 1)

    where = jnp.stack([chip, plane]).astype(jnp.int32)
    h_own, h_other, h_flip, sums = project(
        where, sum(own, []), sum(other, []), sum(weights, []), res_own, res_other, gain[:, :, None], n_head, kv_heads
    )

    h_rest = partner(h_other)
    back, slots = [], []
    for side, source in ((core, h_own), (1 - core, h_rest)):
        for t in range(n_head):
            back.append(plane_send(source[t], t) if t else source[0])
            slots.append(side * n_head + next_plane(-t))
    hidden = place(jnp.stack(slots), back, 1, BF)

    mine, yours = sums[:4], partner(sums[:4])
    totals = mine + jnp.concatenate([yours[2:], yours[:2]], 0)
    step = 1
    while step < n_head:
        totals = totals + lax.ppermute(totals, "head", xor_perm(n_head, step))
        step *= 2
    square_sum = jnp.concatenate([totals[0], totals[2]])
    weighted_sum = jnp.concatenate([totals[1], totals[3]])
    inverse = lax.rsqrt(square_sum / model + EPSILON)
    value_rows = weighted_sum * inverse
    targets = jnp.concatenate([target, target_other])
    position = jnp.arange(rows)
    live = jnp.concatenate([position < suffix_len[seq], position < suffix_len[seq ^ 1]])
    error = jnp.where(live, value_rows - targets, 0.0)
    first_term = error * inverse
    second_term = error * (weighted_sum * inverse * inverse * inverse) / model
    gain_near = jnp.take(gain, chip ^ jnp.arange(chips), axis=0, mode="clip")
    grad = (
        first_term[None, None, :] * gain_near[:, :, None] - second_term[None, None, :] * h_flip.astype(F32)
    ).astype(BF)

    final = []
    for t in [*range(1, n_head), 0]:
        terms = list(gradient(grad, own[t], other[t]))
        order = bits if t % 2 else bits[::-1]
        alive = list(range(chips))
        for bit in order:
            got = {}
            for e in alive:
                if e & bit:
                    got[e ^ bit] = chip_send(terms[e], bit)
            alive = [e for e in alive if not e & bit]
            for e in alive:
                terms[e] = (terms[e].astype(F32) + got[e].astype(F32)).astype(BF)
        final.append(plane_send(terms[0], -t) if t else terms[0])
    final = final[-1:] + final[:-1]
    grad_out = place(jnp.stack([next_plane(t) for t in range(n_head)]), final, 0, F32)
    return (cache_k, cache_v, hidden, value_rows[:rows], grad_out)


def solution(mesh):
    in_specs = (
        P("seq", None, "head"),
        P("seq", None, "head"),
        P("seq", "head"),
        P("seq", "head"),
        P("seq", "head"),
        P("seq", "head"),
        P("seq", "head"),
        P(),
        P(),
        P(),
        P(),
        P(),
        P("seq"),
    )
    out_specs = (
        P(None, "seq", "head"),
        P(None, "seq", "head"),
        P("seq", "head"),
        P("seq"),
        P("seq", "head"),
    )
    body = functools.partial(local, mesh.shape["seq"], mesh.shape["head"])

    return jax.shard_map(body, mesh=mesh, in_specs=in_specs, out_specs=out_specs, check_vma=False)
```

time: 766 us -> 516 us (0.67)
  waiting for transfers between devices: 478 us -> 243 us
  Pallas kernels: 0 us -> 113 us
  matrix products: 90.3 us -> 0 us
  starting transfers between devices: 18.8 us -> 79.5 us
  other arithmetic: 92 us -> 36.1 us
  local copies, waits for them, and re-layouts: 72 us -> 34.7 us
  between operations: 14 us -> 1.84 us
    psum x1 -> x0, waiting for transfers between devices: 292 us -> none  [local(): lax.psum(partial_value.astype(jnp.bfloat16), 'head').astype(jnp.float32)]
    ppermute x0 -> x81, waiting for transfers between devices: none -> 243 us  [the longest x21 130 us: plane_send(): return lax.ppermute(x, 'head', shift_perm(n_head, step))]
    pallas_call x0 -> x13, Pallas kernels: none -> 113 us  [the longest x4 55.8 us: attention(): pl.pallas_call(functools.partial(attention_kernel, blocks), out_shape=jax...]
    reduce_scatter x1 -> x0, waiting for transfers between devices: 112 us -> none  [local(): lax.psum_scatter(lax.dot_general(hidden_grad, attn, (((0,), (0,)), ((), (...]
    dot_general x5 -> x0, matrix products: 90.3 us -> none  [the longest x1 29.5 us: attention(): jnp.einsum('kgsl,lkd->skgd', weights.astype(jnp.bfloat16), value_rows, pr...]
    ppermute x0 -> x81, starting transfers between devices: none -> 79.5 us  [the longest x58 47.3 us: seq_send(): return lax.ppermute(x, 'seq', xor_perm(n_seq, mask))]
    all_to_all x4 -> x0, waiting for transfers between devices: 66.4 us -> none  [the longest x1 39 us: local(): lax.all_to_all(prefix_k, 'seq', split_axis=1, concat_axis=0, tiled=True)]
    unnamed x2 -> x0, other arithmetic: 44.7 us -> none
  transfers between devices with their start and end apart: 8 -> 81, of which waited for: 6 -> 24; matrix products, arithmetic and copies ran while one was open for 29% -> 12% of each run, Pallas kernels for 0% -> 21%
where the time goes in v1:
time: 516 us; the launch traced here: 508 us
  waiting for transfers between devices  243 us (47%)
  Pallas kernels  113 us (22%)
  starting transfers between devices  79.5 us (15%)
  other arithmetic  36.1 us (7%)
  local copies, waits for them, and re-layouts  34.7 us (7%)
    ppermute x21, waiting for transfers between devices, plane_send(): return lax.ppermute(x, 'head', shift_perm(n_head, step))  130 us
    ppermute x58, waiting for transfers between devices, seq_send(): return lax.ppermute(x, 'seq', xor_perm(n_seq, mask))  111 us
    pallas_call x4, Pallas kernels, attention(): pl.pallas_call(functools.partial(attention_kernel, blocks), out_shape=jax...  55.8 us
    ppermute x58, starting transfers between devices, seq_send(): return lax.ppermute(x, 'seq', xor_perm(n_seq, mask))  47.3 us
    ppermute x21, starting transfers between devices, plane_send(): return lax.ppermute(x, 'head', shift_perm(n_head, step))  29 us
    pallas_call x4, Pallas kernels, gradient(): pl.pallas_call(functools.partial(gradient_kernel, parts, chips), out_shap...  21.3 us
    pallas_call x1, Pallas kernels, project(): pl.pallas_call(functools.partial(project_kernel, planes, parts, chips), o...  19.8 us
    another operation x16, other arithmetic, local(): piece = jnp.stack([k, v], 0)  15.9 us
  transfers between devices with their start and end apart: 81, of which 24 were waited for; matrix products, arithmetic and copies ran while one was open for 12% of the time, Pallas kernels for 21%

profile of v1, /device:TPU:0, one launch (start us, length us, event | category | flops | bytes accessed | tf_op | source)
XLA Modules:
  0.0 508.0 jit_solution(2179537088090342186)
XLA Ops:
  28.2 5.3 %constant_dynamic-slice_fusion.1 = (bf16[512,1,1,256]{3,2,1,0:T(2,128)(2,1)}, bf16[512,1,1,256]{3,2,1,0:T(2,128)(2,1)}, bf16[512,1,1,256]{3,2,1,0:T(2,128)(2,1)}...) fusion(bf16[512,2,4,256]{3,2,1,0:T(4,128)(2,1)S(1)} %reshape.22, ...), kind=kLoop, calls=%fused_computation.58 | loop fusion | bytes 4194328 | tf_op jit(solution)/shard_map/jit(dynamic_index_in_dim)/dynamic_slice | solution.py:369
  42.2 13.7 %collective-permute-done.11.refs_7_ = bf16[2,512,128]{2,1,0:T(8,128)(2,1)S(1)} collective-permute-done((bf16[2,512,128]{2,1,0:T(8,128)(2,1)}, bf16[2,512,128]{2,1,0:T(8,128)(2,1)S(1)}, u32[]{:S(2)}, u32[]{:S(2)}) %collective-permute-start.11) | collective-permute-done | bytes 262176 | tf_op jit(solution)/shard_map/ppermute | solution.py:323
  80.3 18.0 %collective-permute-done.18.refs_6_ = bf16[2,512,128]{2,1,0:T(8,128)(2,1)S(1)} collective-permute-done((bf16[2,512,128]{2,1,0:T(8,128)(2,1)}, bf16[2,512,128]{2,1,0:T(8,128)(2,1)S(1)}, u32[]{:S(2)}, u32[]{:S(2)}) %collective-permute-start.18) | collective-permute-done | bytes 262176 | tf_op jit(solution)/shard_map/ppermute | solution.py:323
  104.2 13.8 %attend.4.refs_11_ = bf16[512,512]{1,0:T(8,128)(2,1)} custom-call(bf16[512,1024]{1,0:T(8,128)(2,1)} %refs_0_.7, bf16[2,512,128]{2,1,0:T(8,128)(2,1)} %get-tuple-element.58.refs_1_, bf16[2,512,128]{2,1,0:T(8,128)(2,1)} %collective-permute-done.14.refs_2_, bf16[2,512,128]{2,1,0:T(8,128)(2,1)} %collective-permute-done.15.refs_3_, ...), custom_call_target="tpu_custom_call" | custom-call | flops 2415919104 | bytes 2359296 | tf_op jit(solution)/shard_map/attend/pallas_call | solution.py:88
  127.3 10.2 %collective-permute-done.43 = bf16[256,1024]{1,0:T(8,128)(2,1)} collective-permute-done((bf16[256,1024]{1,0:T(8,128)(2,1)}, bf16[256,1024]{1,0:T(8,128)(2,1)}, u32[]{:S(2)}, u32[]{:S(2)}) %collective-permute-start.43) | collective-permute-done | bytes 524320 | tf_op jit(solution)/shard_map/ppermute | solution.py:338
  143.0 14.2 %attend.5.refs_1_ = bf16[512,512]{1,0:T(8,128)(2,1)} custom-call(bf16[512,1024]{1,0:T(8,128)(2,1)} %refs_0_.7, bf16[2,512,128]{2,1,0:T(8,128)(2,1)} %get-tuple-element.58.refs_1_, bf16[2,512,128]{2,1,0:T(8,128)(2,1)} %collective-permute-done.14.refs_2_, bf16[2,512,128]{2,1,0:T(8,128)(2,1)} %collective-permute-done.15.refs_3_, ...), custom_call_target="tpu_custom_call", output_to_operand_aliasing={{}: (11, {})} | custom-call | flops 2415919104 | bytes 2359296 | tf_op jit(solution)/shard_map/attend/pallas_call | solution.py:88
  161.8 13.9 %attend.6.refs_11_ = bf16[512,512]{1,0:T(8,128)(2,1)} custom-call(bf16[512,1024]{1,0:T(8,128)(2,1)} %refs_0_.7, bf16[2,512,128]{2,1,0:T(8,128)(2,1)} %get-tuple-element.78.refs_1_, bf16[2,512,128]{2,1,0:T(8,128)(2,1)} %copy-done.71, bf16[2,512,128]{2,1,0:T(8,128)(2,1)} %copy-done.72, bf16[2,512,128]{2,1,0:T(8,128)(2,1)} %collective-permute-done.23.refs_4_, ...), custom_call_target="tpu_custom_call" | custom-call | flops 2415919104 | bytes 2359296 | tf_op jit(solution)/shard_map/attend/pallas_call | solution.py:88
  175.7 13.9 %attend.7.refs_2_ = bf16[512,512]{1,0:T(8,128)(2,1)} custom-call(bf16[512,1024]{1,0:T(8,128)(2,1)} %refs_0_.7, bf16[2,512,128]{2,1,0:T(8,128)(2,1)} %get-tuple-element.78.refs_1_, bf16[2,512,128]{2,1,0:T(8,128)(2,1)} %copy-done.71, bf16[2,512,128]{2,1,0:T(8,128)(2,1)} %copy-done.72, ...), custom_call_target="tpu_custom_call", output_to_operand_aliasing={{}: (11, {})} | custom-call | flops 2415919104 | bytes 2359296 | tf_op jit(solution)/shard_map/attend/pallas_call | solution.py:88
  193.0 47.4 %collective-permute-done.52 = bf16[2,512,256]{2,1,0:T(8,128)(2,1)} collective-permute-done((bf16[2,512,256]{2,1,0:T(8,128)(2,1)}, bf16[2,512,256]{2,1,0:T(8,128)(2,1)}, u32[]{:S(2)}, u32[]{:S(2)}) %collective-permute-start.52) | collective-permute-done | bytes 524320 | tf_op jit(solution)/shard_map/ppermute | solution.py:338
  245.9 10.7 %collective-permute-done.31.refs_6_.refs_2_ = bf16[512,512]{1,0:T(8,128)(2,1)} collective-permute-done((bf16[512,512]{1,0:T(8,128)(2,1)S(1)}, bf16[512,512]{1,0:T(8,128)(2,1)}, u32[]{:S(2)}, u32[]{:S(2)}) %collective-permute-start.31) | collective-permute-done | bytes 524320 | tf_op jit(solution)/shard_map/ppermute | solution.py:338
  260.1 6.4 %collective-permute-done.45.refs_19_ = bf16[2,256,1024]{2,1,0:T(8,128)(2,1)S(1)} collective-permute-done((bf16[2,256,1024]{2,1,0:T(8,128)(2,1)S(1)}, bf16[2,256,1024]{2,1,0:T(8,128)(2,1)S(1)}, u32[]{:S(2)}, u32[]{:S(2)}) %collective-permute-start.45) | collective-permute-done | bytes 1048608 | tf_op jit(solution)/shard_map/ppermute | solution.py:323
  266.6 22.0 %collective-permute-done.46.refs_20_ = bf16[2,256,1024]{2,1,0:T(8,128)(2,1)} collective-permute-done((bf16[2,256,1024]{2,1,0:T(8,128)(2,1)S(1)}, bf16[2,256,1024]{2,1,0:T(8,128)(2,1)}, u32[]{:S(2)}, u32[]{:S(2)}) %collective-permute-start.46) | collective-permute-done | bytes 1048608 | tf_op jit(solution)/shard_map/ppermute | solution.py:323
  294.0 11.0 %collective-permute-done.33.refs_8_.refs_2_ = bf16[512,512]{1,0:T(8,128)(2,1)} collective-permute-done((bf16[512,512]{1,0:T(8,128)(2,1)}, bf16[512,512]{1,0:T(8,128)(2,1)}, u32[]{:S(2)}, u32[]{:S(2)}) %collective-permute-start.33) | collective-permute-done | bytes 524320 | tf_op jit(solution)/shard_map/ppermute | solution.py:338
  316.8 19.8 %project.1 = (bf16[4,512,256]{2,1,0:T(8,128)(2,1)}, bf16[4,512,256]{2,1,0:T(8,128)(2,1)}, bf16[4,256,1024]{2,1,0:T(8,128)(2,1)}, f32[8,512]{1,0:T(8,128)}) custom-call(s32[2]{0:T(128)} %pad_add_fusion.refs_0_, bf16[512,512]{1,0:T(8,128)(2,1)} %attend.5.refs_1_, bf16[512,512]{1,0:T(8,128)(2,1)} %attend.7.refs_2_, ...), custom_call_target="tpu_custom_call" | custom-call | flops 8589934592 | bytes 25165824 | tf_op jit(solution)/shard_map/project/pallas_call | solution.py:219
  351.3 5.3 %gradient.4 = (bf16[256,1024]{1,0:T(8,128)(2,1)}, bf16[256,1024]{1,0:T(8,128)(2,1)}, bf16[256,1024]{1,0:T(8,128)(2,1)}, bf16[256,1024]{1,0:T(8,128)(2,1)}) custom-call(bf16[4,256,1024]{2,1,0:T(8,128)(2,1)} %subtract_convert_fusion.refs_0_, bf16[512,512]{1,0:T(8,128)(2,1)} %attend.5.refs_1_, bf16[512,512]{1,0:T(8,128)(2,1)} %attend.7.refs_2_, ...), custom_call_target="tpu_custom_call" | custom-call | flops 2147483648 | bytes 8388608 | tf_op jit(solution)/shard_map/gradient/pallas_call | solution.py:262
  357.7 5.3 %gradient.5 = (bf16[256,1024]{1,0:T(8,128)(2,1)}, bf16[256,1024]{1,0:T(8,128)(2,1)}, bf16[256,1024]{1,0:T(8,128)(2,1)}, bf16[256,1024]{1,0:T(8,128)(2,1)}) custom-call(bf16[4,256,1024]{2,1,0:T(8,128)(2,1)} %subtract_convert_fusion.refs_0_, bf16[512,512]{1,0:T(8,128)(2,1)} %collective-permute-done.28.refs_3_.refs_1_, bf16[512,512]{1,0:T(8,128)(2,1)} %copy-done.55, ...), custom_call_target="tpu_custom_call" | custom-call | flops 2147483648 | bytes 8388608 | tf_op jit(solution)/shard_map/gradient/pallas_call | solution.py:262
  365.0 5.3 %gradient.6 = (bf16[256,1024]{1,0:T(8,128)(2,1)}, bf16[256,1024]{1,0:T(8,128)(2,1)}, bf16[256,1024]{1,0:T(8,128)(2,1)}, bf16[256,1024]{1,0:T(8,128)(2,1)}) custom-call(bf16[4,256,1024]{2,1,0:T(8,128)(2,1)} %subtract_convert_fusion.refs_0_, bf16[512,512]{1,0:T(8,128)(2,1)} %collective-permute-done.30.refs_5_.refs_1_, ...), custom_call_target="tpu_custom_call" | custom-call | flops 2147483648 | bytes 8388608 | tf_op jit(solution)/shard_map/gradient/pallas_call | solution.py:262
  370.3 5.4 %gradient.7 = (bf16[256,1024]{1,0:T(8,128)(2,1)}, bf16[256,1024]{1,0:T(8,128)(2,1)}, bf16[256,1024]{1,0:T(8,128)(2,1)}, bf16[256,1024]{1,0:T(8,128)(2,1)}) custom-call(bf16[4,256,1024]{2,1,0:T(8,128)(2,1)} %subtract_convert_fusion.refs_0_, bf16[512,512]{1,0:T(8,128)(2,1)} %copy-done.59, bf16[512,512]{1,0:T(8,128)(2,1)} %collective-permute-done.33.refs_8_.refs_2_, ...), custom_call_target="tpu_custom_call" | custom-call | flops 2147483648 | bytes 8388608 | tf_op jit(solution)/shard_map/gradient/pallas_call | solution.py:262
  380.4 9.1 %collective-permute-done.74 = bf16[256,1024]{1,0:T(8,128)(2,1)S(1)} collective-permute-done((bf16[256,1024]{1,0:T(8,128)(2,1)}, bf16[256,1024]{1,0:T(8,128)(2,1)S(1)}, u32[]{:S(2)}, u32[]{:S(2)}) %collective-permute-start.74) | collective-permute-done | bytes 524320 | tf_op jit(solution)/shard_map/ppermute | solution.py:323
  390.6 9.2 %collective-permute-done.78 = bf16[256,1024]{1,0:T(8,128)(2,1)S(1)} collective-permute-done((bf16[256,1024]{1,0:T(8,128)(2,1)}, bf16[256,1024]{1,0:T(8,128)(2,1)S(1)}, u32[]{:S(2)}, u32[]{:S(2)}) %collective-permute-start.78) | collective-permute-done | bytes 524320 | tf_op jit(solution)/shard_map/ppermute | solution.py:323
  406.5 8.0 %collective-permute-done.73 = bf16[256,1024]{1,0:T(8,128)(2,1)S(1)} collective-permute-done((bf16[256,1024]{1,0:T(8,128)(2,1)S(1)}, bf16[256,1024]{1,0:T(8,128)(2,1)S(1)}, u32[]{:S(2)}, u32[]{:S(2)}) %collective-permute-start.73) | collective-permute-done | bytes 524320 | tf_op jit(solution)/shard_map/ppermute | solution.py:323
  418.0 9.0 %collective-permute-done.77 = bf16[256,1024]{1,0:T(8,128)(2,1)S(1)} collective-permute-done((bf16[256,1024]{1,0:T(8,128)(2,1)S(1)}, bf16[256,1024]{1,0:T(8,128)(2,1)S(1)}, u32[]{:S(2)}, u32[]{:S(2)}) %collective-permute-start.77) | collective-permute-done | bytes 524320 | tf_op jit(solution)/shard_map/ppermute | solution.py:323
  435.1 5.7 %collective-permute-done.57.refs_4_ = bf16[512,256]{1,0:T(8,128)(2,1)S(1)} collective-permute-done((bf16[512,256]{1,0:T(8,128)(2,1)S(1)}, bf16[512,256]{1,0:T(8,128)(2,1)S(1)}, u32[]{:S(2)}, u32[]{:S(2)}) %collective-permute-start.57) | collective-permute-done | bytes 262176 | tf_op jit(solution)/shard_map/ppermute | solution.py:338
  453.2 45.1 %collective-permute-done.60.refs_7_ = bf16[512,256]{1,0:T(8,128)(2,1)S(1)} collective-permute-done((bf16[512,256]{1,0:T(8,128)(2,1)}, bf16[512,256]{1,0:T(8,128)(2,1)S(1)}, u32[]{:S(2)}, u32[]{:S(2)}) %collective-permute-start.60) | collective-permute-done | bytes 262176 | tf_op jit(solution)/shard_map/ppermute | solution.py:338
  (373 shorter events, 178.7 us)
Async XLA Ops:
  7.8 54.8 %collective-permute-start = (bf16[2,512,128]{2,1,0:T(8,128)(2,1)}, bf16[2,512,128]{2,1,0:T(8,128)(2,1)}, u32[]{:S(2)}, u32[]{:S(2)}) collective-permute-start(bf16[2,512,128]{2,1,0:T(8,128)(2,1)} %pad_maximum_fusion.8), channel_id=1, source_target_pairs={{0,4},{4,0},{8,12},{12,8},{16,20},{20,16},{24,28},{28,24},{1,5},{5... | collective-permute-start | bytes 786440 | tf_op jit(solution)/shard_map/ppermute | solution.py:323
  77.0 47.4 %collective-permute-start.42 = (bf16[256,1024]{1,0:T(8,128)(2,1)}, bf16[256,1024]{1,0:T(8,128)(2,1)S(1)}, u32[]{:S(2)}, u32[]{:S(2)}) collective-permute-start(bf16[256,1024]{1,0:T(8,128)(2,1)} %get-tuple-element.122), channel_id=1, source_target_pairs={{0,1},{1,2},{2,3},{3,0},{4,5},{5,6},{6,7},{7,4},{8,9},{9,10},{10,1... | collective-permute-start | bytes 1572872 | tf_op jit(solution)/shard_map/ppermute | solution.py:338
  79.4 38.7 %collective-permute-start.5 = (bf16[2,512,128]{2,1,0:T(8,128)(2,1)S(1)}, bf16[2,512,128]{2,1,0:T(8,128)(2,1)}, u32[]{:S(2)}, u32[]{:S(2)}) collective-permute-start(bf16[2,512,128]{2,1,0:T(8,128)(2,1)S(1)} %pad_maximum_fusion.13), channel_id=1, source_target_pairs={{0,24},{4,28},{8,16},{12,20},{16,8},{20,12},{24,0},{28,4},{1,25},{... | collective-permute-start | bytes 786440 | tf_op jit(solution)/shard_map/ppermute | solution.py:323
  103.4 34.1 %collective-permute-start.43 = (bf16[256,1024]{1,0:T(8,128)(2,1)}, bf16[256,1024]{1,0:T(8,128)(2,1)}, u32[]{:S(2)}, u32[]{:S(2)}) collective-permute-start(bf16[256,1024]{1,0:T(8,128)(2,1)} %get-tuple-element.121), channel_id=1, source_target_pairs={{0,2},{1,3},{2,0},{3,1},{4,6},{5,7},{6,4},{7,5},{8,10},{9,11},{10,... | collective-permute-start | bytes 1572872 | tf_op jit(solution)/shard_map/ppermute | solution.py:338
  157.2 34.5 %collective-permute-start.28 = (bf16[512,512]{1,0:T(8,128)(2,1)}, bf16[512,512]{1,0:T(8,128)(2,1)}, u32[]{:S(2)}, u32[]{:S(2)}) collective-permute-start(bf16[512,512]{1,0:T(8,128)(2,1)} %attend.5.refs_1_), channel_id=1, source_target_pairs={{0,1},{1,2},{2,3},{3,0},{4,5},{5,6},{6,7},{7,4},{8,9},{9,10},{10,1... | collective-permute-start | bytes 1572872 | tf_op jit(solution)/shard_map/ppermute | solution.py:338
  158.1 34.7 %collective-permute-start.34 = (bf16[512,512]{1,0:T(8,128)(2,1)}, bf16[512,512]{1,0:T(8,128)(2,1)}, u32[]{:S(2)}, u32[]{:S(2)}) collective-permute-start(bf16[512,512]{1,0:T(8,128)(2,1)} %attend.5.refs_1_), channel_id=1, source_target_pairs={{0,4},{4,0},{8,12},{12,8},{16,20},{20,16},{24,28},{28,24},{1,5},{5... | collective-permute-start | bytes 1572872 | tf_op jit(solution)/shard_map/ppermute | solution.py:323
  158.1 34.7 %collective-permute-start.53 = (bf16[2,512,256]{2,1,0:T(8,128)(2,1)S(1)}, bf16[2,512,256]{2,1,0:T(8,128)(2,1)}, u32[]{:S(2)}, u32[]{:S(2)}) collective-permute-start(bf16[2,512,256]{2,1,0:T(8,128)(2,1)S(1)} %copy-done.17), channel_id=1, source_target_pairs={{0,3},{1,0},{2,1},{3,2},{4,7},{5,4},{6,5},{7,6},{8,11},{9,8},{10,9... | collective-permute-start | bytes 1572872 | tf_op jit(solution)/shard_map/ppermute | solution.py:338
  161.3 79.0 %collective-permute-start.52 = (bf16[2,512,256]{2,1,0:T(8,128)(2,1)}, bf16[2,512,256]{2,1,0:T(8,128)(2,1)}, u32[]{:S(2)}, u32[]{:S(2)}) collective-permute-start(bf16[2,512,256]{2,1,0:T(8,128)(2,1)} %pad_maximum_fusion.5), channel_id=1, source_target_pairs={{0,2},{1,3},{2,0},{3,1},{4,6},{5,7},{6,4},{7,5},{8,10},{9,11},{10,... | collective-permute-start | bytes 1572872 | tf_op jit(solution)/shard_map/ppermute | solution.py:338
  189.5 50.9 %collective-permute-start.29 = (bf16[512,512]{1,0:T(8,128)(2,1)}, bf16[512,512]{1,0:T(8,128)(2,1)S(1)}, u32[]{:S(2)}, u32[]{:S(2)}) collective-permute-start(bf16[512,512]{1,0:T(8,128)(2,1)} %attend.7.refs_2_), channel_id=1, source_target_pairs={{0,1},{1,2},{2,3},{3,0},{4,5},{5,6},{6,7},{7,4},{8,9},{9,10},{10,1... | collective-permute-start | bytes 1572872 | tf_op jit(solution)/shard_map/ppermute | solution.py:338
  191.7 48.8 %collective-permute-start.51 = (bf16[2,512,256]{2,1,0:T(8,128)(2,1)S(1)}, bf16[2,512,256]{2,1,0:T(8,128)(2,1)S(1)}, u32[]{:S(2)}, u32[]{:S(2)}) collective-permute-start(bf16[2,512,256]{2,1,0:T(8,128)(2,1)S(1)} %pad_maximum_fusion.4), channel_id=1, source_target_pairs={{0,1},{1,2},{2,3},{3,0},{4,5},{5,6},{6,7},{7,4},{8,9},{9,10},{10,1... | collective-permute-start | bytes 1572872 | tf_op jit(solution)/shard_map/ppermute | solution.py:338
  192.8 49.8 %collective-permute-start.35 = (bf16[512,512]{1,0:T(8,128)(2,1)S(1)}, bf16[512,512]{1,0:T(8,128)(2,1)S(1)}, u32[]{:S(2)}, u32[]{:S(2)}) collective-permute-start(bf16[512,512]{1,0:T(8,128)(2,1)S(1)} %copy-done.64), channel_id=1, source_target_pairs={{0,4},{4,0},{8,12},{12,8},{16,20},{20,16},{24,28},{28,24},{1,5},{5... | collective-permute-start | bytes 1572872 | tf_op jit(solution)/shard_map/ppermute | solution.py:323
  192.8 51.0 %collective-permute-start.30 = (bf16[512,512]{1,0:T(8,128)(2,1)}, bf16[512,512]{1,0:T(8,128)(2,1)}, u32[]{:S(2)}, u32[]{:S(2)}) collective-permute-start(bf16[512,512]{1,0:T(8,128)(2,1)} %collective-permute-done.28.refs_3_.refs_1_), channel_id=1, source_target_pairs={{0,1},{1,2},{2,3},{3,0},{4,5},{5,6},{6,7},{7,4},{8,9},{9,10},{10,1... | collective-permute-start | bytes 1572872 | tf_op jit(solution)/shard_map/ppermute | solution.py:338
  242.6 45.9 %collective-permute-start.47 = (bf16[2,256,1024]{2,1,0:T(8,128)(2,1)S(1)}, bf16[2,256,1024]{2,1,0:T(8,128)(2,1)}, u32[]{:S(2)}, u32[]{:S(2)}) collective-permute-start(bf16[2,256,1024]{2,1,0:T(8,128)(2,1)S(1)} %pad_maximum_fusion.refs_17_), channel_id=1, source_target_pairs={{0,16},{4,20},{8,24},{12,28},{16,0},{20,4},{24,8},{28,12},{1,17},{... | collective-permute-start | bytes 3145736 | tf_op jit(solution)/shard_map/ppermute | solution.py:323
  243.8 44.8 %collective-permute-start.46 = (bf16[2,256,1024]{2,1,0:T(8,128)(2,1)S(1)}, bf16[2,256,1024]{2,1,0:T(8,128)(2,1)}, u32[]{:S(2)}, u32[]{:S(2)}) collective-permute-start(bf16[2,256,1024]{2,1,0:T(8,128)(2,1)S(1)} %pad_maximum_fusion.1.refs_18_), channel_id=1, source_target_pairs={{0,8},{4,12},{8,0},{12,4},{16,24},{20,28},{24,16},{28,20},{1,9},{5... | collective-permute-start | bytes 3145736 | tf_op jit(solution)/shard_map/ppermute | solution.py:323
  244.9 45.4 %collective-permute-start.48 = (bf16[2,256,1024]{2,1,0:T(8,128)(2,1)S(1)}, bf16[2,256,1024]{2,1,0:T(8,128)(2,1)S(1)}, u32[]{:S(2)}, u32[]{:S(2)}) collective-permute-start(bf16[2,256,1024]{2,1,0:T(8,128)(2,1)S(1)} %pad_maximum_fusion.1.refs_18_), channel_id=1, source_target_pairs={{0,16},{4,20},{8,24},{12,28},{16,0},{20,4},{24,8},{28,12},{1,17},{... | collective-permute-start | bytes 3145736 | tf_op jit(solution)/shard_map/ppermute | solution.py:323
  309.1 40.1 %collective-permute-start.65 = (f32[512]{0:T(512)S(1)}, f32[512]{0:T(512)S(1)}, u32[]{:S(2)}, u32[]{:S(2)}) collective-permute-start(f32[512]{0:T(512)S(1)} %select_reduce_fusion), channel_id=1, source_target_pairs={{0,4},{4,0},{8,12},{12,8},{16,20},{20,16},{24,28},{28,24},{1,5},{5... | collective-permute-start | bytes 6152 | tf_op jit(solution)/shard_map/ppermute | solution.py:323
  348.5 69.4 %collective-permute-start.55 = (bf16[512,256]{1,0:T(8,128)(2,1)}, bf16[512,256]{1,0:T(8,128)(2,1)S(1)}, u32[]{:S(2)}, u32[]{:S(2)}) collective-permute-start(bf16[512,256]{1,0:T(8,128)(2,1)} %get-tuple-element.135), channel_id=1, source_target_pairs={{0,1},{1,2},{2,3},{3,0},{4,5},{5,6},{6,7},{7,4},{8,9},{9,10},{10,1... | collective-permute-start | bytes 786440 | tf_op jit(solution)/shard_map/ppermute | solution.py:338
  349.2 51.6 %collective-permute-start.58 = (bf16[4,512,256]{2,1,0:T(8,128)(2,1)}, bf16[4,512,256]{2,1,0:T(8,128)(2,1)S(1)}, u32[]{:S(2)}, u32[]{:S(2)}) collective-permute-start(bf16[4,512,256]{2,1,0:T(8,128)(2,1)} %get-tuple-element.92), channel_id=1, source_target_pairs={{0,4},{4,0},{8,12},{12,8},{16,20},{20,16},{24,28},{28,24},{1,5},{5... | collective-permute-start | bytes 3145736 | tf_op jit(solution)/shard_map/ppermute | solution.py:323
  364.1 38.9 %collective-permute-start.69 = (bf16[256,1024]{1,0:T(8,128)(2,1)}, bf16[256,1024]{1,0:T(8,128)(2,1)}, u32[]{:S(2)}, u32[]{:S(2)}) collective-permute-start(bf16[256,1024]{1,0:T(8,128)(2,1)} %get-tuple-element.100), channel_id=1, source_target_pairs={{0,8},{4,12},{8,0},{12,4},{16,24},{20,28},{24,16},{28,20},{1,9},{5... | collective-permute-start | bytes 1572872 | tf_op jit(solution)/shard_map/ppermute | solution.py:323
  431.3 70.9 %collective-permute-start.72 = (bf16[256,1024]{1,0:T(8,128)(2,1)S(1)}, bf16[256,1024]{1,0:T(8,128)(2,1)S(1)}, u32[]{:S(2)}, u32[]{:S(2)}) collective-permute-start(bf16[256,1024]{1,0:T(8,128)(2,1)S(1)} %add_convert_fusion.6), channel_id=1, source_target_pairs={{0,3},{1,0},{2,1},{3,2},{4,7},{5,4},{6,5},{7,6},{8,11},{9,8},{10,9... | collective-permute-start | bytes 1572872 | tf_op jit(solution)/shard_map/ppermute | solution.py:338
  440.9 61.4 %collective-permute-start.76 = (bf16[256,1024]{1,0:T(8,128)(2,1)}, bf16[256,1024]{1,0:T(8,128)(2,1)S(1)}, u32[]{:S(2)}, u32[]{:S(2)}) collective-permute-start(bf16[256,1024]{1,0:T(8,128)(2,1)} %add_convert_fusion.3), channel_id=1, source_target_pairs={{0,2},{1,3},{2,0},{3,1},{4,6},{5,7},{6,4},{7,5},{8,10},{9,11},{10,... | collective-permute-start | bytes 1572872 | tf_op jit(solution)/shard_map/ppermute | solution.py:338
  441.6 60.7 %collective-permute-start.80 = (bf16[256,1024]{1,0:T(8,128)(2,1)}, bf16[256,1024]{1,0:T(8,128)(2,1)S(1)}, u32[]{:S(2)}, u32[]{:S(2)}) collective-permute-start(bf16[256,1024]{1,0:T(8,128)(2,1)} %add_convert_fusion), channel_id=1, source_target_pairs={{0,1},{1,2},{2,3},{3,0},{4,5},{5,6},{6,7},{7,4},{8,9},{9,10},{10,1... | collective-permute-start | bytes 1572872 | tf_op jit(solution)/shard_map/ppermute | solution.py:338
  444.4 53.9 %collective-permute-start.60 = (bf16[512,256]{1,0:T(8,128)(2,1)}, bf16[512,256]{1,0:T(8,128)(2,1)S(1)}, u32[]{:S(2)}, u32[]{:S(2)}) collective-permute-start(bf16[512,256]{1,0:T(8,128)(2,1)} %get-tuple-element.130), channel_id=1, source_target_pairs={{0,2},{1,3},{2,0},{3,1},{4,6},{5,7},{6,4},{7,5},{8,10},{9,11},{10,... | collective-permute-start | bytes 786440 | tf_op jit(solution)/shard_map/ppermute | solution.py:338
  446.7 51.6 %collective-permute-start.61 = (bf16[512,256]{1,0:T(8,128)(2,1)}, bf16[512,256]{1,0:T(8,128)(2,1)S(1)}, u32[]{:S(2)}, u32[]{:S(2)}) collective-permute-start(bf16[512,256]{1,0:T(8,128)(2,1)} %get-tuple-element.129), channel_id=1, source_target_pairs={{0,3},{1,0},{2,1},{3,2},{4,7},{5,4},{6,5},{7,6},{8,11},{9,8},{10,9... | collective-permute-start | bytes 786440 | tf_op jit(solution)/shard_map/ppermute | solution.py:338
  (130 other events, 2391.7 us)

commit v2 on v1

v2 whole, which is shorter than its diff:
```python
import functools
import math

import jax
import jax.numpy as jnp
from jax import lax
from jax.experimental import pallas as pl
from jax.experimental.pallas import tpu as pltpu
from jax.sharding import PartitionSpec as P


HD = 128
EPSILON = 1e-05
MASKED = -1e30
BF = jnp.bfloat16
F32 = jnp.float32
TILE = 256
VMEM_LIMIT = 60 * 1024 * 1024


def tie(x, *deps):
    return lax.optimization_barrier((x, *deps))[0]


def shift_perm(count, step):
    return [(i, (i + step) % count) for i in range(count)]


def xor_perm(count, mask):
    return [(i, i ^ mask) for i in range(count)]


def dot_t(a, b):
    return lax.dot_general(a, b, (((1,), (1,)), ((), ())), preferred_element_type=F32)


def dot(a, b):
    return lax.dot_general(a, b, (((1,), (0,)), ((), ())), preferred_element_type=F32)


def attention_kernel(q_ref, kv, sk_ref, sv_ref, o_ref, v_wide, scores):
    blocks = kv.shape[0]
    tile = q_ref.shape[0]
    block_len = kv.shape[2]
    own_len = sk_ref.shape[0]
    prefix_len = blocks * block_len
    scale = HD ** (-0.5) / math.log(2.0)

    @pl.when((pl.program_id(0) == 0) & (pl.program_id(1) == 0))
    def _():
        for b in range(blocks):
            v_wide[b * block_len : (b + 1) * block_len, :HD] = kv[b, 1]
        v_wide[prefix_len:, :HD] = sv_ref[...]
        v_wide[:, HD:] = jnp.ones((prefix_len + own_len, HD), BF)

    q = q_ref[...]
    spans = [(b * block_len, block_len) for b in range(blocks)]
    top = jnp.full((tile, HD), MASKED, F32)
    for b, (start, size) in enumerate(spans):
        s = dot_t(q, kv[b, 0])
        scores[:, start : start + size] = s
        for lane in range(0, size, HD):
            top = jnp.maximum(top, s[:, lane : lane + HD])
    s = dot_t(q, sk_ref[...])
    row = lax.broadcasted_iota(jnp.int32, (tile, own_len), 0) + pl.program_id(1) * tile
    col = lax.broadcasted_iota(jnp.int32, (tile, own_len), 1)
    s = jnp.where(col <= row, s, MASKED)
    scores[:, prefix_len:] = s
    for lane in range(0, own_len, HD):
        top = jnp.maximum(top, s[:, lane : lane + HD])
    row_max = jnp.max(top, 1, keepdims=True)
    mixed = jnp.zeros((tile, 2 * HD), F32)
    for start, size in spans + [(prefix_len, own_len)]:
        p = jnp.exp2((scores[:, start : start + size] - row_max) * scale)
        mixed = mixed + dot(p.astype(BF), v_wide[start : start + size, :])
    o_ref[...] = (mixed[:, :HD] / mixed[:, HD:]).astype(BF)


def attention(queries, kv, suffix_k, suffix_v, head, group, first, count):
    rows = queries.shape[0]
    tile = TILE
    blocks, _, block_len, _ = kv.shape
    span = blocks * block_len + rows
    return pl.pallas_call(
        attention_kernel,
        out_shape=jax.ShapeDtypeStruct((rows, count * HD), BF),
        grid=(count, rows // tile),
        in_specs=[pl.BlockSpec((tile, HD), lambda j, i: (i, head * group + first + j))]
        + [pl.BlockSpec(kv.shape, lambda j, i: (0, 0, 0, 0))]
        + [pl.BlockSpec((rows, HD), lambda j, i: (0, head))] * 2,
        out_specs=pl.BlockSpec((tile, HD), lambda j, i: (i, j)),
        scratch_shapes=[pltpu.VMEM((span, 2 * HD), BF), pltpu.VMEM((tile, span), F32)],
        compiler_params=pltpu.CompilerParams(vmem_limit_bytes=VMEM_LIMIT),
        cost_estimate=pl.CostEstimate(
            flops=4 * rows * count * span * HD, bytes_accessed=4 * span * HD, transcendentals=rows * count * span
        ),
        name="attend",
    )(queries, kv, suffix_k, suffix_v)


def route_kernel(head, *refs):
    pick, came = refs[:2]
    chosen, cache_k, cache_v, held, in_sem, out_sem, cache_sem = refs[-7:]
    count = held.shape[0]
    load = pltpu.make_async_copy(came, held, in_sem)
    load.start()
    load.wait()
    cut = pl.ds(head * HD, HD)
    copies = [pltpu.make_async_copy(held.at[pick[n]], chosen.at[n], out_sem.at[n]) for n in range(count)]
    for which, cache in enumerate((cache_k, cache_v)):
        copies.append(pltpu.make_async_copy(held.at[:, which], cache.at[:, :, cut], cache_sem.at[which]))
    for copy in copies:
        copy.start()
    for copy in copies:
        copy.wait()


def route(pick, came, head, kv_heads, caches):
    count, _, block_len, _ = came.shape
    cache = jax.ShapeDtypeStruct((count, block_len, kv_heads * HD), BF)
    any_spec = pl.BlockSpec(memory_space=pl.ANY)
    extra = list(caches)
    chosen, *caches = pl.pallas_call(
        functools.partial(route_kernel, head),
        out_shape=(jax.ShapeDtypeStruct(came.shape, BF), cache, cache),
        in_specs=[pl.BlockSpec(memory_space=pltpu.SMEM)] + [any_spec] * (1 + len(extra)),
        out_specs=(any_spec,) * 3,
        scratch_shapes=[
            pltpu.VMEM(came.shape, BF),
            pltpu.SemaphoreType.DMA,
            pltpu.SemaphoreType.DMA((count,)),
            pltpu.SemaphoreType.DMA((2,)),
        ],
        input_output_aliases={2: 1, 3: 2} if extra else {},
        compiler_params=pltpu.CompilerParams(vmem_limit_bytes=VMEM_LIMIT),
        cost_estimate=pl.CostEstimate(flops=0, bytes_accessed=8 * 1024 * 1024, transcendentals=0),
        name="route",
    )(pick, came, *extra)
    return chosen, caches


def fill(planes, widths, sides, weights, a_buf, w_buf, a_sem, w_sem, more):
    parts = len(widths)
    block = sum(widths)
    chips = len(weights) // planes
    copies = []
    for side in range(2):
        for t in range(planes):
            for g in range(parts):
                start = t * block + sum(widths[:g])
                copies.append(
                    pltpu.make_async_copy(
                        sides[side][t * parts + g],
                        a_buf.at[side, :, start : start + widths[g]],
                        a_sem.at[side, t * parts + g],
                    )
                )
    for copy in copies:
        copy.start()
    for e in range(chips):
        for t in range(planes):
            pltpu.make_async_copy(
                weights[e * planes + t],
                w_buf.at[e, :, t * block : (t + 1) * block],
                w_sem.at[e, t],
            ).start()
        if not e:
            for copy in more:
                copy.start()
    for copy in copies:
        copy.wait()


def weights_landed(planes, block, w_buf, w_sem, e):
    for t in range(planes):
        landed = w_buf.at[e, :, t * block : (t + 1) * block]
        pltpu.make_async_copy(landed, landed, w_sem.at[e, t]).wait()


def project_kernel(planes, widths, chips, *refs):
    pieces = planes * len(widths)
    where_ref, refs = refs[0], refs[1:]
    sides, refs = (refs[:pieces], refs[pieces : 2 * pieces]), refs[2 * pieces :]
    weights, refs = refs[: planes * chips], refs[planes * chips :]
    res, refs = refs[:planes], refs[planes:]
    gain, refs = refs[0], refs[1:]
    h_outs, refs = refs[:planes], refs[planes:]
    h_flip, sums, a_buf, w_buf, r_buf, h_buf, a_sem, w_sem, r_sem, h_sem = refs
    rows = a_buf.shape[1]
    chip = where_ref[0]
    plane = where_ref[1]
    more = [pltpu.make_async_copy(res[r], r_buf.at[r], r_sem.at[r]) for r in range(planes)]
    fill(planes, widths, sides, weights, a_buf, w_buf, a_sem, w_sem, more)
    for copy in more:
        copy.wait()
    sums[...] = jnp.zeros_like(sums)

    @pl.loop(0, chips)
    def _(e):
        weights_landed(planes, sum(widths), w_buf, w_sem, e)
        home = jnp.bitwise_xor(chip, e)
        gain_col = gain[home]
        came = lax.rem(plane - home + planes, planes)
        goes = lax.rem(home - plane + planes, planes)
        for side in range(2):
            total = dot_t(a_buf[side], w_buf[e])
            h = (r_buf[came, side].astype(F32) + total).astype(BF)
            h_buf[e, side] = h
            flip = h.astype(F32).T
            h_flip[e, :, side * rows : (side + 1) * rows] = flip.astype(BF)
            sums[2 * side : 2 * side + 1, :] += jnp.sum(flip * flip, 0, keepdims=True)
            sums[2 * side + 1 : 2 * side + 2, :] += jnp.sum(flip * gain_col, 0, keepdims=True)
        for r in range(planes):

            @pl.when(goes == r)
            def _(r=r):
                pltpu.make_async_copy(h_buf.at[e], h_outs[r], h_sem.at[r]).start()

    for r in range(planes):
        pltpu.make_async_copy(h_buf.at[0], h_outs[r], h_sem.at[r]).wait()


def project(where, own, other, weights, res, gain):
    planes = len(own)
    widths = tuple(a.shape[1] for a in own[0])
    chips = len(weights) // planes
    rows = own[0][0].shape[0]
    features = weights[0].shape[0]
    depth = planes * sum(widths)
    shape = jax.ShapeDtypeStruct
    any_spec = pl.BlockSpec(memory_space=pl.ANY)
    vmem_spec = pl.BlockSpec(memory_space=pltpu.VMEM)
    own, other = sum(own, []), sum(other, [])
    buffers = [pltpu.VMEM((2, rows, depth), BF), pltpu.VMEM((chips, features, depth), BF)]
    semaphores = [pltpu.SemaphoreType.DMA((2, len(own))), pltpu.SemaphoreType.DMA((chips, planes))]
    params = pltpu.CompilerParams(vmem_limit_bytes=VMEM_LIMIT)
    cost = pl.CostEstimate(
        flops=4 * rows * features * chips * depth, bytes_accessed=16 * 1024 * 1024, transcendentals=0
    )
    return pl.pallas_call(
        functools.partial(project_kernel, planes, widths, chips),
        out_shape=(
            *(shape((2, rows, features), BF),) * planes,
            shape((chips, features, 2 * rows), BF),
            shape((8, rows), F32),
        ),
        in_specs=[pl.BlockSpec(memory_space=pltpu.SMEM)]
        + [any_spec] * (2 * len(own) + planes * chips + planes)
        + [vmem_spec],
        out_specs=(any_spec,) * planes + (vmem_spec,) * 2,
        scratch_shapes=buffers
        + [
            pltpu.VMEM((planes, 2, rows, features), BF),
            pltpu.VMEM((chips, 2, rows, features), BF),
        ]
        + semaphores
        + [pltpu.SemaphoreType.DMA((n,)) for n in (planes, planes)],
        compiler_params=params,
        cost_estimate=cost,
        name="project",
    )(where, *own, *other, *weights, *res, gain)


def gradient_kernel(parts, order, *refs):
    grad = refs[0]
    own = refs[1 : 1 + parts]
    other = refs[1 + parts : 1 + 2 * parts]
    outs = refs[1 + 2 * parts :]
    rows = own[0].shape[0]
    count = len(order) // 2
    step = order[count]
    for out, base in zip(outs, (step, 0)):

        @pl.loop(0, count)
        def _(i):
            e = base + chip_index(order, i)
            start = 0
            for a, b in zip(own, other):
                total = dot(grad[e, :, :rows], a[...]) + dot(grad[e, :, rows:], b[...])
                out[i, :, start : start + a.shape[1]] = total.astype(BF)
                start += a.shape[1]


def chip_index(order, i):
    value = 0
    bit = 1
    while bit < len(order) // 2:
        value = value + jnp.where(jnp.bitwise_and(i, bit) != 0, order[bit], 0)
        bit *= 2
    return value


def gradient(grad, own, other, order):
    chips, features, tokens = grad.shape
    parts = len(own)
    width = sum(a.shape[1] for a in own)
    vmem_spec = pl.BlockSpec(memory_space=pltpu.VMEM)
    return pl.pallas_call(
        functools.partial(gradient_kernel, parts, order),
        out_shape=(jax.ShapeDtypeStruct((chips // 2, features, width), BF),) * 2,
        in_specs=[vmem_spec] * (1 + 2 * parts),
        out_specs=(vmem_spec,) * 2,
        compiler_params=pltpu.CompilerParams(vmem_limit_bytes=VMEM_LIMIT),
        cost_estimate=pl.CostEstimate(
            flops=2 * chips * features * tokens * width, bytes_accessed=8 * 1024 * 1024, transcendentals=0
        ),
        name="gradient",
    )(grad, *own, *other)


def place_kernel(count, axis, size, *refs):
    where_ref = refs[0]
    out = refs[-1]
    for i in range(count):
        start = pl.multiple_of(where_ref[i] * size, size)
        piece = refs[1 + i][...].astype(out.dtype)
        if axis == 0:
            out[pl.ds(start, size), :] = piece
        else:
            out[:, pl.ds(start, size)] = piece


def place(slots, pieces, axis, dtype):
    shape = list(pieces[0].shape)
    size = shape[axis]
    if axis == 1 and size % HD:
        order = jnp.argsort(slots)
        stacked = jnp.take(jnp.stack(pieces, 0), order, axis=0, mode="clip")
        return jnp.concatenate([stacked[i] for i in range(len(pieces))], 1).astype(dtype)
    shape[axis] *= len(pieces)
    vmem_spec = pl.BlockSpec(memory_space=pltpu.VMEM)
    return pl.pallas_call(
        functools.partial(place_kernel, len(pieces), axis, size),
        out_shape=jax.ShapeDtypeStruct(tuple(shape), dtype),
        in_specs=[pl.BlockSpec(memory_space=pltpu.SMEM)] + [vmem_spec] * len(pieces),
        out_specs=vmem_spec,
        compiler_params=pltpu.CompilerParams(vmem_limit_bytes=VMEM_LIMIT),
        cost_estimate=pl.CostEstimate(flops=0, bytes_accessed=6 * 1024 * 1024, transcendentals=0),
        name="place",
    )(slots.astype(jnp.int32), *pieces)


def place_rows_kernel(count, *refs):
    where_ref, pieces = refs[0], refs[1 : 1 + count]
    out, wide, sem = refs[-3:]
    size = wide.shape[1]
    copies = []
    for i in range(count):
        wide[i] = pieces[i][...].astype(F32)
        start = pl.multiple_of(where_ref[i] * size, size)
        copies.append(pltpu.make_async_copy(wide.at[i], out.at[pl.ds(start, size), :], sem.at[i]))
        copies[-1].start()
    for copy in copies:
        copy.wait()


def place_rows(slots, pieces, shape, before=None):
    count = len(pieces)
    extra = [] if before is None else [before]
    any_spec = pl.BlockSpec(memory_space=pl.ANY)
    return pl.pallas_call(
        functools.partial(place_rows_kernel, count),
        out_shape=jax.ShapeDtypeStruct(shape, F32),
        in_specs=[pl.BlockSpec(memory_space=pltpu.SMEM)]
        + [pl.BlockSpec(memory_space=pltpu.VMEM)] * count
        + [any_spec] * len(extra),
        out_specs=any_spec,
        scratch_shapes=[pltpu.VMEM((count, *pieces[0].shape), F32), pltpu.SemaphoreType.DMA((count,))],
        input_output_aliases={1 + count: 0} if extra else {},
        compiler_params=pltpu.CompilerParams(vmem_limit_bytes=VMEM_LIMIT),
        cost_estimate=pl.CostEstimate(flops=0, bytes_accessed=count * 1572864, transcendentals=0),
        name="place_rows",
    )(slots.astype(jnp.int32), *pieces, *extra)


def local(n_seq, n_head, prefix_k, prefix_v, queries, suffix_k, suffix_v, residual, out_weight,
          norm_gain, value_weight, prompt_of, suffix_len, return_table, return_index):
    chips = n_seq // 2
    bits = [1 << b for b in range(chips.bit_length() - 1)]
    rows = queries.shape[0]
    local_width = residual.shape[1]
    model = local_width * n_head
    kv_heads = prefix_k.shape[2] // HD
    group = queries.shape[1] // (kv_heads * HD)
    positions = prefix_k.shape[1]
    block_len = positions // n_seq
    seq = lax.axis_index("seq")
    plane = lax.axis_index("head")
    chip, core = seq // 2, seq % 2

    def seq_send(x, mask):
        return lax.ppermute(x, "seq", xor_perm(n_seq, mask))

    def partner(x):
        return seq_send(x, 1)

    def chip_send(x, bit):
        return seq_send(x, 2 * bit)

    def plane_send(x, step):
        return lax.ppermute(x, "head", shift_perm(n_head, step))

    def next_plane(step):
        return (plane + step) % n_head

    def plane_send(x, step):
        return lax.ppermute(x, "head", shift_perm(n_head, step))

    def next_plane(step):
        return (plane + step) % n_head

    weight_rows = out_weight.shape[0] // n_head
    w_own = []
    for t in range(n_head):
        piece = lax.dynamic_slice_in_dim(out_weight, next_plane(t) * weight_rows, weight_rows, 0)
        w_own.append(plane_send(piece, t) if t else piece)

    res = residual.reshape(rows, 2, n_head, weight_rows)
    mine = lax.dynamic_index_in_dim(res, core, 1, keepdims=False)
    yours = lax.dynamic_index_in_dim(res, 1 - core, 1, keepdims=False)
    theirs = partner(yours)
    res = []
    for t in range(n_head):
        piece = jnp.stack(
            [lax.dynamic_index_in_dim(x, next_plane(t), 1, keepdims=False) for x in (mine, theirs)], 0
        )
        res.append(plane_send(piece, t) if t else piece)

    gain_weight = norm_gain * value_weight
    gain = gain_weight.reshape(chips, 2, n_head, weight_rows)
    gain = lax.dynamic_index_in_dim(gain, core, 1, keepdims=False)
    gain = lax.dynamic_index_in_dim(gain, plane, 1, keepdims=False)

    bins = return_table.shape[0]
    one_hot = return_index[:, None] == jnp.arange(bins)[None, :]
    target = jnp.sum(jnp.where(one_hot, return_table[None, :], 0.0), 1)
    target_other = partner(target)

    pick = prompt_of.astype(jnp.int32)
    attn = []
    caches = ()
    for head in range(kv_heads):
        cut = slice(head * HD, (head + 1) * HD)
        both = jnp.stack([x[0, :, cut].reshape(n_seq, block_len, HD) for x in (prefix_k, prefix_v)], 1)
        if head:
            both = tie(both, kv)
        came = lax.all_to_all(both, "seq", split_axis=0, concat_axis=0, tiled=True)
        if head:
            came = tie(came, attn[-1])
        chosen, caches = route(pick, came, head, kv_heads, caches)
        kv = lax.all_to_all(chosen, "seq", split_axis=0, concat_axis=0, tiled=True)
        last = head == kv_heads - 1
        count = max(group // 2, 1) if last else group
        for step, first in enumerate(range(0, group, count)):
            if last and first + count == group:
                kv, *res = lax.optimization_barrier((kv, *res))
            attn.append(attention(queries, kv, suffix_k, suffix_v, head, group, first, count))
    cache_k, cache_v = caches

    half = n_head // 2
    w_own = list(lax.optimization_barrier((*w_own, attn[0]))[:-1])
    w_late = list(lax.optimization_barrier((*w_own, chosen))[:-1])
    weights = [w_own] + [None] * (chips - 1)
    for e in sorted(range(1, chips), key=lambda v: bin(v).count("1")):
        low, high = e & -e, 1 << (e.bit_length() - 1)
        got = [None] * n_head
        turn = [*range(half, n_head), *range(half)] if low == 1 else [*range(n_head)]
        for k, t in enumerate(turn):
            if low == high:
                got[t] = chip_send((w_late if k else w_own)[t], e)
            else:
                bit = low if t < half else high
                got[t] = chip_send(weights[e ^ bit][t], bit)
        weights[e] = got

    parts = len(attn)
    own = [[None] * parts for _ in range(n_head)]
    other = [[None] * parts for _ in range(n_head)]
    for g in range(parts):
        for t in range(n_head):
            if not t:
                own[t][g] = attn[g]
            elif g + 2 < parts or parts == 3 and not g:
                own[t][g] = plane_send(own[t - 1][g], 1)
            else:
                own[t][g] = plane_send(attn[g], t)
            other[t][g] = partner(own[t][g])

    where = jnp.stack([chip, plane]).astype(jnp.int32)
    weights = sum(weights, [])
    *h_outs, h_flip, sums = project(where, own, other, weights, res, gain[:, :, None])

    back = []
    for t in range(n_head):
        back.append(plane_send(h_outs[t], t) if t else h_outs[0])
    rest = partner(jnp.stack([piece[1] for piece in back], 0))
    pieces = [piece[0] for piece in back] + list(rest)
    slots = [side * n_head + next_plane(-t) for side in (core, 1 - core) for t in range(n_head)]
    hidden = place(jnp.stack(slots), pieces, 1, BF)

    yours = partner(sums[:4])
    totals = sums[:4] + jnp.concatenate([yours[2:], yours[:2]], 0)
    step = 1
    while step < n_head:
        totals = totals + lax.ppermute(totals, "head", xor_perm(n_head, step))
        step *= 2
    square_sum = jnp.concatenate([totals[0], totals[2]])
    weighted_sum = jnp.concatenate([totals[1], totals[3]])
    inverse = lax.rsqrt(square_sum / model + EPSILON)
    value_rows = weighted_sum * inverse
    targets = jnp.concatenate([target, target_other])
    position = jnp.arange(rows)
    live = jnp.concatenate([position < suffix_len[seq], position < suffix_len[seq ^ 1]])
    error = jnp.where(live, value_rows - targets, 0.0)
    first_term = error * inverse
    second_term = error * (weighted_sum * inverse * inverse * inverse) / model
    gain_near = jnp.take(gain, chip ^ jnp.arange(chips), axis=0, mode="clip")
    grad = (
        first_term[None, None, :] * gain_near[:, :, None] - second_term[None, None, :] * h_flip.astype(F32)
    ).astype(BF)

    final = []
    turns = sorted(range(n_head), key=lambda t: (t == 0, abs(2 * t - n_head), t))
    for t in turns:
        turn = bits if t % 2 else bits[::-1]
        order = [sum(bit for k, bit in enumerate(turn[::-1]) if i >> k & 1) for i in range(chips)]
        send, keep = gradient(grad, own[t], other[t], order)
        for bit in turn:
            got = chip_send(send, bit)
            half = keep.shape[0] // 2
            if half:
                send = (keep[half:].astype(F32) + got[half:].astype(F32)).astype(BF)
                keep = (keep[:half].astype(F32) + got[:half].astype(F32)).astype(BF)
            else:
                keep = (keep.astype(F32) + got.astype(F32)).astype(BF)
        final.append(plane_send(keep[0], -t) if t else keep[0])
    late = turns.index(n_head - 1)
    early = [i for i in range(n_head) if i != late]
    shape = (n_head * weight_rows, out_weight.shape[1])
    grad_out = place_rows(jnp.stack([next_plane(turns[i]) for i in early]), [final[i] for i in early], shape)
    grad_out = place_rows(next_plane(turns[late])[None], [final[late]], shape, grad_out)
    return (cache_k, cache_v, hidden, value_rows[:rows], grad_out)


def solution(mesh):
    in_specs = (
        P("seq", None, "head"),
        P("seq", None, "head"),
        P("seq", "head"),
        P("seq", "head"),
        P("seq", "head"),
        P("seq", "head"),
        P("seq", "head"),
        P(),
        P(),
        P(),
        P(),
        P(),
        P("seq"),
    )
    out_specs = (
        P(None, "seq", "head"),
        P(None, "seq", "head"),
        P("seq", "head"),
        P("seq"),
        P("seq", "head"),
    )
    body = functools.partial(local, mesh.shape["seq"], mesh.shape["head"])

    return jax.shard_map(body, mesh=mesh, in_specs=in_specs, out_specs=out_specs, check_vma=False)
```

time: 516 us -> 494 us (0.957)
  waiting for transfers between devices: 243 us -> 146 us
  starting transfers between devices: 79.5 us -> 143 us
  blocking collectives: 0 us -> 31.7 us
  other arithmetic: 36.1 us -> 20.9 us
  local copies, waits for them, and re-layouts: 34.7 us -> 28.4 us
    ppermute x58 -> x36, waiting for transfers between devices: 111 us -> 49.7 us  [seq_send(): return lax.ppermute(x, 'seq', xor_perm(n_seq, mask))]
    ppermute x21, waiting for transfers between devices: 130 us -> 71.2 us  [plane_send(): return lax.ppermute(x, 'head', shift_perm(n_head, step))]
    ppermute x21, starting transfers between devices: 29 us -> 86.5 us  [plane_send(): return lax.ppermute(x, 'head', shift_perm(n_head, step))]
    all_to_all x0 -> x1, blocking collectives: none -> 31.7 us  [local(): came = lax.all_to_all(both, 'seq', split_axis=0, concat_axis=0, tiled=True)]
    all_to_all x0 -> x3, waiting for transfers between devices: none -> 25.1 us  [the longest x2 25.1 us: local(): kv = lax.all_to_all(chosen, 'seq', split_axis=0, concat_axis=0, tiled=True)]
    ppermute x58 -> x36, starting transfers between devices: 47.3 us -> 27.6 us  [seq_send(): return lax.ppermute(x, 'seq', xor_perm(n_seq, mask))]
    another operation x24 -> x8, other arithmetic: 23 us -> 6.2 us  [the longest x4 3.77 us: local(): jnp.stack([lax.dynamic_index_in_dim(x, next_plane(t), 1, keepdims=False)...]
    all_to_all x0 -> x3, starting transfers between devices: none -> 12.7 us  [the longest x2 8.34 us: local(): kv = lax.all_to_all(chosen, 'seq', split_axis=0, concat_axis=0, tiled=True)]
  transfers between devices with their start and end apart: 81 -> 62, of which waited for: 24 -> 19; matrix products, arithmetic and copies ran while one was open for 12% -> 9% of each run, Pallas kernels for 21% -> 22%
where the time goes in v2:
time: 494 us; the launch traced here: 485 us
  waiting for transfers between devices  146 us (30%)
  starting transfers between devices  143 us (29%)
  Pallas kernels  114 us (23%)
  blocking collectives  31.7 us (6%)
  local copies, waits for them, and re-layouts  28.4 us (6%)
  other arithmetic  20.9 us (4%)
    ppermute x21, starting transfers between devices, plane_send(): return lax.ppermute(x, 'head', shift_perm(n_head, step))  86.5 us
    ppermute x21, waiting for transfers between devices, plane_send(): return lax.ppermute(x, 'head', shift_perm(n_head, step))  71.2 us
    pallas_call x3, Pallas kernels, attention(): pl.pallas_call(attention_kernel, out_shape=jax.ShapeDtypeStruct((rows, co...  53 us
    ppermute x36, waiting for transfers between devices, seq_send(): return lax.ppermute(x, 'seq', xor_perm(n_seq, mask))  49.7 us
    all_to_all x1, blocking collectives, local(): came = lax.all_to_all(both, 'seq', split_axis=0, concat_axis=0, tiled=True)  31.7 us
    ppermute x36, starting transfers between devices, seq_send(): return lax.ppermute(x, 'seq', xor_perm(n_seq, mask))  27.6 us
    all_to_all x2, waiting for transfers between devices, local(): kv = lax.all_to_all(chosen, 'seq', split_axis=0, concat_axis=0, tiled=True)  25.1 us
    pallas_call x4, Pallas kernels, gradient(): pl.pallas_call(functools.partial(gradient_kernel, parts, order), out_shap...  23.8 us
  transfers between devices with their start and end apart: 62, of which 19 were waited for; matrix products, arithmetic and copies ran while one was open for 9% of the time, Pallas kernels for 22%

profile of v2, /device:TPU:0, one launch (start us, length us, event | category | flops | bytes accessed | tf_op | source)
XLA Modules:
  0.0 484.9 jit_solution(2311665104184550253)
XLA Ops:
  3.2 31.7 %all_to_all.20.refs_1_ = bf16[8,2,512,128]{3,2,1,0:T(8,128)(2,1)} all-to-all(bf16[8,2,512,128]{3,2,1,0:T(8,128)(2,1)S(1)} %pad_maximum_fusion.1), channel_id=1, replica_groups=mesh['seq'=8,'head'=4] {'seq'}, dimensions={0} | all-to-all | bytes 4194304 | tf_op jit(solution)/shard_map/all_to_all | solution.py:447
  45.1 25.1 %all-to-all-done.1.kv = bf16[8,2,512,128]{3,2,1,0:T(8,128)(2,1)} async-done(((bf16[8,2,512,128]{3,2,1,0:T(8,128)(2,1)}), bf16[8,2,512,128]{3,2,1,0:T(8,128)(2,1)}, u32[]{:S(2)}, u32[]{:S(2)}) %all-to-all-start.1) | async-done | bytes 2097184 | tf_op jit(solution)/shard_map/all_to_all | solution.py:451
  90.4 25.0 %attend.3.refs_1_ = bf16[512,512]{1,0:T(8,128)(2,1)} custom-call(bf16[512,1024]{1,0:T(8,128)(2,1)} %q_ref.5, bf16[8,2,512,128]{3,2,1,0:T(8,128)(2,1)} %all-to-all-done.1.kv, bf16[512,256]{1,0:T(8,128)(2,1)} %sk_ref.5, bf16[512,256]{1,0:T(8,128)(2,1)} %sv_ref.5), custom_call_target="tpu_custom_call" | custom-call | flops 4831838208 | bytes 2359296 | tf_op jit(solution)/shard_map/attend/pallas_call | solution.py:84
  135.0 30.4 %collective-permute-start.7 = (bf16[512,512]{1,0:T(8,128)(2,1)}, bf16[512,512]{1,0:T(8,128)(2,1)S(1)}, u32[]{:S(2)}, u32[]{:S(2)}) collective-permute-start(bf16[512,512]{1,0:T(8,128)(2,1)} %collective-permute-done.4.refs_4_.refs_1_), channel_id=1, source_target_pairs={{0,1},{1,2},{2,3},{3,0},{4,5},{5,6},{6,7},{7,4},{8,9},{9,10},{10,1... | collective-permute-start | bytes 1572872 | tf_op jit(solution)/shard_map/ppermute | solution.py:407
  168.6 20.2 %collective-permute-done.2.refs_43_ = bf16[2,512,256]{2,1,0:T(8,128)(2,1)S(1)} collective-permute-done((bf16[2,512,256]{2,1,0:T(8,128)(2,1)S(1)}, bf16[2,512,256]{2,1,0:T(8,128)(2,1)S(1)}, u32[]{:S(2)}, u32[]{:S(2)}) %collective-permute-start.2) | collective-permute-done | bytes 524320 | tf_op jit(solution)/shard_map/ppermute | solution.py:407
  188.8 10.0 %collective-permute-start.10 = (bf16[512,512]{1,0:T(8,128)(2,1)S(1)}, bf16[512,512]{1,0:T(8,128)(2,1)S(1)}, u32[]{:S(2)}, u32[]{:S(2)}) collective-permute-start(bf16[512,512]{1,0:T(8,128)(2,1)S(1)} %collective-permute-done.7.refs_7_.refs_1_), channel_id=1, source_target_pairs={{0,1},{1,2},{2,3},{3,0},{4,5},{5,6},{6,7},{7,4},{8,9},{9,10},{10,1... | collective-permute-start | bytes 1572872 | tf_op jit(solution)/shard_map/ppermute | solution.py:407
  202.4 7.1 %collective-permute-done.10.refs_10_.refs_1_ = bf16[512,512]{1,0:T(8,128)(2,1)S(1)} collective-permute-done((bf16[512,512]{1,0:T(8,128)(2,1)S(1)}, bf16[512,512]{1,0:T(8,128)(2,1)S(1)}, u32[]{:S(2)}, u32[]{:S(2)}) %collective-permute-start.10) | collective-permute-done | bytes 524320 | tf_op jit(solution)/shard_map/ppermute | solution.py:407
  218.5 6.5 %collective-permute-done.28.refs_29_ = bf16[256,1024]{1,0:T(8,128)(2,1)S(1)} collective-permute-done((bf16[256,1024]{1,0:T(8,128)(2,1)S(1)}, bf16[256,1024]{1,0:T(8,128)(2,1)S(1)}, u32[]{:S(2)}, u32[]{:S(2)}) %collective-permute-start.28) | collective-permute-done | bytes 524320 | tf_op jit(solution)/shard_map/ppermute | solution.py:392
  238.1 13.9 %attend.5.refs_3_ = bf16[512,256]{1,0:T(8,128)(2,1)} custom-call(bf16[512,1024]{1,0:T(8,128)(2,1)} %q_ref.5, bf16[8,2,512,128]{3,2,1,0:T(8,128)(2,1)} %copy-done.1, bf16[512,256]{1,0:T(8,128)(2,1)} %sk_ref.5, bf16[512,256]{1,0:T(8,128)(2,1)} %sv_ref.5), custom_call_target="tpu_custom_call" | custom-call | flops 2415919104 | bytes 2359296 | tf_op jit(solution)/shard_map/attend/pallas_call | solution.py:84
  252.1 14.0 %attend.4.refs_2_ = bf16[512,256]{1,0:T(8,128)(2,1)} custom-call(bf16[512,1024]{1,0:T(8,128)(2,1)} %q_ref.5, bf16[8,2,512,128]{3,2,1,0:T(8,128)(2,1)} %copy-done.1, bf16[512,256]{1,0:T(8,128)(2,1)} %sk_ref.5, bf16[512,256]{1,0:T(8,128)(2,1)} %sv_ref.5), custom_call_target="tpu_custom_call" | custom-call | flops 2415919104 | bytes 2359296 | tf_op jit(solution)/shard_map/attend/pallas_call | solution.py:84
  266.2 13.0 %collective-permute-start.5 = (bf16[512,256]{1,0:T(8,128)(2,1)}, bf16[512,256]{1,0:T(8,128)(2,1)S(1)}, u32[]{:S(2)}, u32[]{:S(2)}) collective-permute-start(bf16[512,256]{1,0:T(8,128)(2,1)} %attend.4.refs_2_), channel_id=1, source_target_pairs={{0,1},{1,2},{2,3},{3,0},{4,5},{5,6},{6,7},{7,4},{8,9},{9,10},{10,1... | collective-permute-start | bytes 786440 | tf_op jit(solution)/shard_map/ppermute | solution.py:407
  291.7 13.0 %collective-permute-done.8.refs_8_.refs_2_ = bf16[512,256]{1,0:T(8,128)(2,1)S(1)} collective-permute-done((bf16[512,256]{1,0:T(8,128)(2,1)}, bf16[512,256]{1,0:T(8,128)(2,1)S(1)}, u32[]{:S(2)}, u32[]{:S(2)}) %collective-permute-start.8) | collective-permute-done | bytes 262176 | tf_op jit(solution)/shard_map/ppermute | solution.py:407
  304.6 5.6 %collective-permute-done.9.refs_9_.refs_3_ = bf16[512,256]{1,0:T(8,128)(2,1)S(1)} collective-permute-done((bf16[512,256]{1,0:T(8,128)(2,1)S(1)}, bf16[512,256]{1,0:T(8,128)(2,1)S(1)}, u32[]{:S(2)}, u32[]{:S(2)}) %collective-permute-start.9) | collective-permute-done | bytes 262176 | tf_op jit(solution)/shard_map/ppermute | solution.py:407
  316.4 20.0 %project.1 = (bf16[2,512,256]{2,1,0:T(8,128)(2,1)}, bf16[2,512,256]{2,1,0:T(8,128)(2,1)}, bf16[2,512,256]{2,1,0:T(8,128)(2,1)}, bf16[2,512,256]{2,1,0:T(8,128)(2...) custom-call(s32[2]{0:T(128)} %pad_add_fusion.refs_0_, bf16[512,512]{1,0:T(8,128)(2,1)} %attend.3.refs_1_, ...), custom_call_target="tpu_custom_call" | custom-call | flops 8589934592 | bytes 16777216 | tf_op jit(solution)/shard_map/project/pallas_call | solution.py:240
  339.7 12.3 %collective-permute-start.45 = (f32[4,512]{1,0:T(4,128)S(1)}, f32[4,512]{1,0:T(4,128)S(1)}, u32[]{:S(2)}, u32[]{:S(2)}) collective-permute-start(f32[4,512]{1,0:T(4,128)S(1)} %maximum_add_fusion), channel_id=1, source_target_pairs={{0,1},{1,0},{2,3},{3,2},{4,5},{5,4},{6,7},{7,6},{8,9},{9,8},{10,11... | collective-permute-start | bytes 24584 | tf_op jit(solution)/shard_map/ppermute | solution.py:505
  367.3 5.9 %gradient.4 = (bf16[2,256,1024]{2,1,0:T(8,128)(2,1)}, bf16[2,256,1024]{2,1,0:T(8,128)(2,1)}) custom-call(bf16[4,256,1024]{2,1,0:T(8,128)(2,1)} %subtract_convert_fusion.refs_0_, bf16[512,512]{1,0:T(8,128)(2,1)} %copy-done.21, bf16[512,256]{1,0:T(8,128)(2,1)} %copy-done.40, bf16[512,256]{1,0:T(8,128)(2,1)} %collective-permute-done.12.refs_12_.refs_3_, ...), custom_call_target="tpu_custom_call" | custom-call | flops 2147483648 | bytes 8388608 | tf_op jit(solution)/shard_map/gradient/pallas_call | solution.py:298
  374.7 5.9 %gradient.5 = (bf16[2,256,1024]{2,1,0:T(8,128)(2,1)}, bf16[2,256,1024]{2,1,0:T(8,128)(2,1)}) custom-call(bf16[4,256,1024]{2,1,0:T(8,128)(2,1)} %subtract_convert_fusion.refs_0_, bf16[512,512]{1,0:T(8,128)(2,1)} %copy-done.18, bf16[512,256]{1,0:T(8,128)(2,1)} %copy-done.36, bf16[512,256]{1,0:T(8,128)(2,1)} %copy-done.38, bf16[512,512]{1,0:T(8,128)(2,1)} %copy-done.22, ...), custom_call_target="tpu_custom_call" | custom-call | flops 2147483648 | bytes 8388608 | tf_op jit(solution)/shard_map/gradient/pallas_call | solution.py:298
  381.2 5.9 %gradient.6 = (bf16[2,256,1024]{2,1,0:T(8,128)(2,1)}, bf16[2,256,1024]{2,1,0:T(8,128)(2,1)}) custom-call(bf16[4,256,1024]{2,1,0:T(8,128)(2,1)} %subtract_convert_fusion.refs_0_, bf16[512,512]{1,0:T(8,128)(2,1)} %collective-permute-done.4.refs_4_.refs_1_, bf16[512,256]{1,0:T(8,128)(2,1)} %copy-done.34, bf16[512,256]{1,0:T(8,128)(2,1)} %copy-done.35, ...), custom_call_target="tpu_custom_call" | custom-call | flops 2147483648 | bytes 8388608 | tf_op jit(solution)/shard_map/gradient/pallas_call | solution.py:298
  387.2 5.9 %gradient.7 = (bf16[2,256,1024]{2,1,0:T(8,128)(2,1)}, bf16[2,256,1024]{2,1,0:T(8,128)(2,1)}) custom-call(bf16[4,256,1024]{2,1,0:T(8,128)(2,1)} %subtract_convert_fusion.refs_0_, bf16[512,512]{1,0:T(8,128)(2,1)} %attend.3.refs_1_, bf16[512,256]{1,0:T(8,128)(2,1)} %attend.4.refs_2_, bf16[512,256]{1,0:T(8,128)(2,1)} %attend.5.refs_3_, ...), custom_call_target="tpu_custom_call" | custom-call | flops 2147483648 | bytes 8388608 | tf_op jit(solution)/shard_map/gradient/pallas_call | solution.py:298
  408.9 13.1 %collective-permute-done.54 = bf16[2,256,1024]{2,1,0:T(8,128)(2,1)S(1)} collective-permute-done((bf16[2,256,1024]{2,1,0:T(8,128)(2,1)}, bf16[2,256,1024]{2,1,0:T(8,128)(2,1)S(1)}, u32[]{:S(2)}, u32[]{:S(2)}) %collective-permute-start.54) | collective-permute-done | bytes 1048608 | tf_op jit(solution)/shard_map/ppermute | solution.py:392
  422.6 6.7 %collective-permute-done.57 = bf16[2,256,1024]{2,1,0:T(8,128)(2,1)S(1)} collective-permute-done((bf16[2,256,1024]{2,1,0:T(8,128)(2,1)}, bf16[2,256,1024]{2,1,0:T(8,128)(2,1)S(1)}, u32[]{:S(2)}, u32[]{:S(2)}) %collective-permute-start.57) | collective-permute-done | bytes 1048608 | tf_op jit(solution)/shard_map/ppermute | solution.py:392
  430.2 10.4 %collective-permute-done.49 = bf16[1,256,1024]{2,1,0:T(8,128)(2,1)S(1)} collective-permute-done((bf16[1,256,1024]{2,1,0:T(8,128)(2,1)S(1)}, bf16[1,256,1024]{2,1,0:T(8,128)(2,1)S(1)}, u32[]{:S(2)}, u32[]{:S(2)}) %collective-permute-start.49) | collective-permute-done | bytes 524320 | tf_op jit(solution)/shard_map/ppermute | solution.py:392
  451.2 4.9 %collective-permute-start.56 = (bf16[256,1024]{1,0:T(8,128)(2,1)}, bf16[256,1024]{1,0:T(8,128)(2,1)}, u32[]{:S(2)}, u32[]{:S(2)}) collective-permute-start(bf16[256,1024]{1,0:T(8,128)(2,1)} %fusion.2), channel_id=1, source_target_pairs={{0,3},{1,0},{2,1},{3,2},{4,7},{5,4},{6,5},{7,6},{8,11},{9,8},{10,9... | collective-permute-start | bytes 1572872 | tf_op jit(solution)/shard_map/ppermute | solution.py:407
  462.3 15.0 %collective-permute-done.53.refs_1_ = bf16[256,1024]{1,0:T(8,128)(2,1)S(1)} collective-permute-done((bf16[256,1024]{1,0:T(8,128)(2,1)}, bf16[256,1024]{1,0:T(8,128)(2,1)S(1)}, u32[]{:S(2)}, u32[]{:S(2)}) %collective-permute-start.53) | collective-permute-done | bytes 524320 | tf_op jit(solution)/shard_map/ppermute | solution.py:407
  (254 shorter events, 161.7 us)
Async XLA Ops:
  70.2 50.6 %all-to-all-start.2 = ((bf16[8,2,512,128]{3,2,1,0:T(8,128)(2,1)}), bf16[8,2,512,128]{3,2,1,0:T(8,128)(2,1)}, u32[]{:S(2)}, u32[]{:S(2)}) async-start(bf16[8,2,512,128]{3,2,1,0:T(8,128)(2,1)} %pad_maximum_fusion), calls=%async_computation.2 | async-start | bytes 4194304 | tf_op jit(solution)/shard_map/all_to_all | solution.py:447
  79.4 36.7 %collective-permute-start = (bf16[512,4,256]{2,0,1:T(8,128)(2,1)}, bf16[512,4,256]{2,0,1:T(8,128)(2,1)}, u32[]{:S(2)}, u32[]{:S(2)}) collective-permute-start(bf16[512,4,256]{2,0,1:T(8,128)(2,1)} %bitcast.70), channel_id=1, source_target_pairs={{0,4},{4,0},{8,12},{12,8},{16,20},{20,16},{24,28},{28,24},{1,5},{5... | collective-permute-start | bytes 3145736 | tf_op jit(solution)/shard_map/ppermute | solution.py:392
  82.7 48.6 %collective-permute-start.25 = (bf16[256,1024]{1,0:T(8,128)(2,1)}, bf16[256,1024]{1,0:T(8,128)(2,1)}, u32[]{:S(2)}, u32[]{:S(2)}) collective-permute-start(bf16[256,1024]{1,0:T(8,128)(2,1)} %get-tuple-element.78), channel_id=1, source_target_pairs={{0,1},{1,2},{2,3},{3,0},{4,5},{5,6},{6,7},{7,4},{8,9},{9,10},{10,1... | collective-permute-start | bytes 1572872 | tf_op jit(solution)/shard_map/ppermute | solution.py:407
  84.3 50.6 %collective-permute-start.26 = (bf16[256,1024]{1,0:T(8,128)(2,1)}, bf16[256,1024]{1,0:T(8,128)(2,1)}, u32[]{:S(2)}, u32[]{:S(2)}) collective-permute-start(bf16[256,1024]{1,0:T(8,128)(2,1)} %get-tuple-element.80), channel_id=1, source_target_pairs={{0,2},{1,3},{2,0},{3,1},{4,6},{5,7},{6,4},{7,5},{8,10},{9,11},{10,... | collective-permute-start | bytes 1572872 | tf_op jit(solution)/shard_map/ppermute | solution.py:407
  86.9 78.6 %collective-permute-start.27 = (bf16[256,1024]{1,0:T(8,128)(2,1)}, bf16[256,1024]{1,0:T(8,128)(2,1)}, u32[]{:S(2)}, u32[]{:S(2)}) collective-permute-start(bf16[256,1024]{1,0:T(8,128)(2,1)} %get-tuple-element.77), channel_id=1, source_target_pairs={{0,3},{1,0},{2,1},{3,2},{4,7},{5,4},{6,5},{7,6},{8,11},{9,8},{10,9... | collective-permute-start | bytes 1572872 | tf_op jit(solution)/shard_map/ppermute | solution.py:407
  119.1 48.0 %collective-permute-start.1 = (bf16[2,512,256]{2,1,0:T(8,128)(2,1)}, bf16[2,512,256]{2,1,0:T(8,128)(2,1)}, u32[]{:S(2)}, u32[]{:S(2)}) collective-permute-start(bf16[2,512,256]{2,1,0:T(8,128)(2,1)} %pad_maximum_fusion.4), channel_id=1, source_target_pairs={{0,1},{1,2},{2,3},{3,0},{4,5},{5,6},{6,7},{7,4},{8,9},{9,10},{10,1... | collective-permute-start | bytes 1572872 | tf_op jit(solution)/shard_map/ppermute | solution.py:407
  125.1 106.4 %all-to-all-start.3 = ((bf16[8,2,512,128]{3,2,1,0:T(8,128)(2,1)}), bf16[8,2,512,128]{3,2,1,0:T(8,128)(2,1)S(1)}, u32[]{:S(2)}, u32[]{:S(2)}) async-start(bf16[8,2,512,128]{3,2,1,0:T(8,128)(2,1)} %get-tuple-element.47), calls=%async_computation.3 | async-start | bytes 4194304 | tf_op jit(solution)/shard_map/all_to_all | solution.py:451
  131.3 57.5 %collective-permute-start.2 = (bf16[2,512,256]{2,1,0:T(8,128)(2,1)S(1)}, bf16[2,512,256]{2,1,0:T(8,128)(2,1)S(1)}, u32[]{:S(2)}, u32[]{:S(2)}) collective-permute-start(bf16[2,512,256]{2,1,0:T(8,128)(2,1)S(1)} %pad_maximum_fusion.5), channel_id=1, source_target_pairs={{0,2},{1,3},{2,0},{3,1},{4,6},{5,7},{6,4},{7,5},{8,10},{9,11},{10,... | collective-permute-start | bytes 1572872 | tf_op jit(solution)/shard_map/ppermute | solution.py:407
  134.8 64.0 %collective-permute-start.3 = (bf16[2,512,256]{2,1,0:T(8,128)(2,1)S(1)}, bf16[2,512,256]{2,1,0:T(8,128)(2,1)S(1)}, u32[]{:S(2)}, u32[]{:S(2)}) collective-permute-start(bf16[2,512,256]{2,1,0:T(8,128)(2,1)S(1)} %pad_maximum_fusion.6), channel_id=1, source_target_pairs={{0,3},{1,0},{2,1},{3,2},{4,7},{5,4},{6,5},{7,6},{8,11},{9,8},{10,9... | collective-permute-start | bytes 1572872 | tf_op jit(solution)/shard_map/ppermute | solution.py:407
  135.0 53.7 %collective-permute-start.7 = (bf16[512,512]{1,0:T(8,128)(2,1)}, bf16[512,512]{1,0:T(8,128)(2,1)S(1)}, u32[]{:S(2)}, u32[]{:S(2)}) collective-permute-start(bf16[512,512]{1,0:T(8,128)(2,1)} %collective-permute-done.4.refs_4_.refs_1_), channel_id=1, source_target_pairs={{0,1},{1,2},{2,3},{3,0},{4,5},{5,6},{6,7},{7,4},{8,9},{9,10},{10,1... | collective-permute-start | bytes 1572872 | tf_op jit(solution)/shard_map/ppermute | solution.py:407
  167.1 33.8 %collective-permute-start.30 = (bf16[256,1024]{1,0:T(8,128)(2,1)}, bf16[256,1024]{1,0:T(8,128)(2,1)S(1)}, u32[]{:S(2)}, u32[]{:S(2)}) collective-permute-start(bf16[256,1024]{1,0:T(8,128)(2,1)} %collective-permute-done.26.refs_27_), channel_id=1, source_target_pairs={{0,8},{4,12},{8,0},{12,4},{16,24},{20,28},{24,16},{28,20},{1,9},{5... | collective-permute-start | bytes 1572872 | tf_op jit(solution)/shard_map/ppermute | solution.py:392
  217.1 49.0 %collective-permute-start.29 = (bf16[256,1024]{1,0:T(8,128)(2,1)}, bf16[256,1024]{1,0:T(8,128)(2,1)S(1)}, u32[]{:S(2)}, u32[]{:S(2)}) collective-permute-start(bf16[256,1024]{1,0:T(8,128)(2,1)} %collective-permute-done.25.refs_26_), channel_id=1, source_target_pairs={{0,8},{4,12},{8,0},{12,4},{16,24},{20,28},{24,16},{28,20},{1,9},{5... | collective-permute-start | bytes 1572872 | tf_op jit(solution)/shard_map/ppermute | solution.py:392
  218.0 61.3 %collective-permute-start.35 = (bf16[256,1024]{1,0:T(8,128)(2,1)}, bf16[256,1024]{1,0:T(8,128)(2,1)}, u32[]{:S(2)}, u32[]{:S(2)}) collective-permute-start(bf16[256,1024]{1,0:T(8,128)(2,1)} %collective-permute-done.27.refs_28_), channel_id=1, source_target_pairs={{0,16},{4,20},{8,24},{12,28},{16,0},{20,4},{24,8},{28,12},{1,17},{... | collective-permute-start | bytes 1572872 | tf_op jit(solution)/shard_map/ppermute | solution.py:392
  225.0 54.1 %collective-permute-start.34 = (bf16[256,1024]{1,0:T(8,128)(2,1)}, bf16[256,1024]{1,0:T(8,128)(2,1)}, u32[]{:S(2)}, u32[]{:S(2)}) collective-permute-start(bf16[256,1024]{1,0:T(8,128)(2,1)} %collective-permute-done.26.refs_27_), channel_id=1, source_target_pairs={{0,16},{4,20},{8,24},{12,28},{16,0},{20,4},{24,8},{28,12},{1,17},{... | collective-permute-start | bytes 1572872 | tf_op jit(solution)/shard_map/ppermute | solution.py:392
  228.9 50.4 %collective-permute-start.37 = (bf16[256,1024]{1,0:T(8,128)(2,1)}, bf16[256,1024]{1,0:T(8,128)(2,1)}, u32[]{:S(2)}, u32[]{:S(2)}) collective-permute-start(bf16[256,1024]{1,0:T(8,128)(2,1)} %collective-permute-done.33.refs_34_), channel_id=1, source_target_pairs={{0,8},{4,12},{8,0},{12,4},{16,24},{20,28},{24,16},{28,20},{1,9},{5... | collective-permute-start | bytes 1572872 | tf_op jit(solution)/shard_map/ppermute | solution.py:392
  236.4 45.8 %collective-permute-start.39 = (bf16[256,1024]{1,0:T(8,128)(2,1)}, bf16[256,1024]{1,0:T(8,128)(2,1)S(1)}, u32[]{:S(2)}, u32[]{:S(2)}) collective-permute-start(bf16[256,1024]{1,0:T(8,128)(2,1)} %collective-permute-done.31.refs_32_), channel_id=1, source_target_pairs={{0,16},{4,20},{8,24},{12,28},{16,0},{20,4},{24,8},{28,12},{1,17},{... | collective-permute-start | bytes 1572872 | tf_op jit(solution)/shard_map/ppermute | solution.py:392
  315.6 48.2 %collective-permute-start.47 = (f32[512]{0:T(512)S(1)}, f32[512]{0:T(512)S(1)}, u32[]{:S(2)}, u32[]{:S(2)}) collective-permute-start(f32[512]{0:T(512)S(1)} %select_reduce_fusion), channel_id=1, source_target_pairs={{0,4},{4,0},{8,12},{12,8},{16,20},{20,16},{24,28},{28,24},{1,5},{5... | collective-permute-start | bytes 6152 | tf_op jit(solution)/shard_map/ppermute | solution.py:392
  359.0 34.1 %collective-permute-start.40 = (bf16[2,512,256]{2,1,0:T(8,128)(2,1)}, bf16[2,512,256]{2,1,0:T(8,128)(2,1)S(1)}, u32[]{:S(2)}, u32[]{:S(2)}) collective-permute-start(bf16[2,512,256]{2,1,0:T(8,128)(2,1)} %get-tuple-element.62), channel_id=1, source_target_pairs={{0,1},{1,2},{2,3},{3,0},{4,5},{5,6},{6,7},{7,4},{8,9},{9,10},{10,1... | collective-permute-start | bytes 1572872 | tf_op jit(solution)/shard_map/ppermute | solution.py:407
  360.8 36.4 %collective-permute-start.41 = (bf16[2,512,256]{2,1,0:T(8,128)(2,1)}, bf16[2,512,256]{2,1,0:T(8,128)(2,1)S(1)}, u32[]{:S(2)}, u32[]{:S(2)}) collective-permute-start(bf16[2,512,256]{2,1,0:T(8,128)(2,1)} %get-tuple-element.63), channel_id=1, source_target_pairs={{0,2},{1,3},{2,0},{3,1},{4,6},{5,7},{6,4},{7,5},{8,10},{9,11},{10,... | collective-permute-start | bytes 1572872 | tf_op jit(solution)/shard_map/ppermute | solution.py:407
  360.8 39.4 %collective-permute-start.42 = (bf16[2,512,256]{2,1,0:T(8,128)(2,1)}, bf16[2,512,256]{2,1,0:T(8,128)(2,1)S(1)}, u32[]{:S(2)}, u32[]{:S(2)}) collective-permute-start(bf16[2,512,256]{2,1,0:T(8,128)(2,1)} %get-tuple-element.64), channel_id=1, source_target_pairs={{0,3},{1,0},{2,1},{3,2},{4,7},{5,4},{6,5},{7,6},{8,11},{9,8},{10,9... | collective-permute-start | bytes 1572872 | tf_op jit(solution)/shard_map/ppermute | solution.py:407
  401.1 55.0 %collective-permute-start.43 = (bf16[4,512,256]{2,1,0:T(8,128)(2,1)S(1)}, bf16[4,512,256]{2,1,0:T(8,128)(2,1)S(1)}, u32[]{:S(2)}, u32[]{:S(2)}) collective-permute-start(bf16[4,512,256]{2,1,0:T(8,128)(2,1)S(1)} %pad_maximum_fusion.2), channel_id=1, source_target_pairs={{0,4},{4,0},{8,12},{12,8},{16,20},{20,16},{24,28},{28,24},{1,5},{5... | collective-permute-start | bytes 3145736 | tf_op jit(solution)/shard_map/ppermute | solution.py:392
  401.4 39.2 %collective-permute-start.49 = (bf16[1,256,1024]{2,1,0:T(8,128)(2,1)S(1)}, bf16[1,256,1024]{2,1,0:T(8,128)(2,1)S(1)}, u32[]{:S(2)}, u32[]{:S(2)}) collective-permute-start(bf16[1,256,1024]{2,1,0:T(8,128)(2,1)S(1)} %add_convert_fusion.10), channel_id=1, source_target_pairs={{0,16},{4,20},{8,24},{12,28},{16,0},{20,4},{24,8},{28,12},{1,17},{... | collective-permute-start | bytes 1572872 | tf_op jit(solution)/shard_map/ppermute | solution.py:392
  408.2 36.5 %collective-permute-start.52 = (bf16[1,256,1024]{2,1,0:T(8,128)(2,1)S(1)}, bf16[1,256,1024]{2,1,0:T(8,128)(2,1)S(1)}, u32[]{:S(2)}, u32[]{:S(2)}) collective-permute-start(bf16[1,256,1024]{2,1,0:T(8,128)(2,1)S(1)} %add_convert_fusion.7), channel_id=1, source_target_pairs={{0,8},{4,12},{8,0},{12,4},{16,24},{20,28},{24,16},{28,20},{1,9},{5... | collective-permute-start | bytes 1572872 | tf_op jit(solution)/shard_map/ppermute | solution.py:392
  441.6 40.1 %collective-permute-start.50 = (bf16[256,1024]{1,0:T(8,128)(2,1)}, bf16[256,1024]{1,0:T(8,128)(2,1)S(1)}, u32[]{:S(2)}, u32[]{:S(2)}) collective-permute-start(bf16[256,1024]{1,0:T(8,128)(2,1)} %fusion), channel_id=1, source_target_pairs={{0,1},{1,2},{2,3},{3,0},{4,5},{5,6},{6,7},{7,4},{8,9},{9,10},{10,1... | collective-permute-start | bytes 1572872 | tf_op jit(solution)/shard_map/ppermute | solution.py:407
  (80 other events, 1554.5 us)

commit v3 on v2

--- a/solution.py
+++ b/solution.py
@@ -177,7 +177,7 @@
         pltpu.make_async_copy(landed, landed, w_sem.at[e, t]).wait()
 
 
-def project_kernel(planes, widths, chips, *refs):
+def project_kernel(planes, widths, chips, sends, *refs):
     pieces = planes * len(widths)
     where_ref, refs = refs[0], refs[1:]
     sides, refs = (refs[:pieces], refs[pieces : 2 * pieces]), refs[2 * pieces :]
@@ -185,7 +185,8 @@
     res, refs = refs[:planes], refs[planes:]
     gain, refs = refs[0], refs[1:]
     h_outs, refs = refs[:planes], refs[planes:]
-    h_flip, sums, a_buf, w_buf, r_buf, h_buf, a_sem, w_sem, r_sem, h_sem = refs
+    flips, refs = refs[: len(sends)], refs[len(sends) :]
+    h_flip, sums, a_buf, w_buf, r_buf, h_buf, a_sem, w_sem, r_sem, h_sem, f_sem = refs
     rows = a_buf.shape[1]
     chip = where_ref[0]
     plane = where_ref[1]
@@ -216,11 +217,21 @@
             def _(r=r):
                 pltpu.make_async_copy(h_buf.at[e], h_outs[r], h_sem.at[r]).start()
 
+        for j, chosen in enumerate(sends):
+            for i, value in enumerate(chosen):
+
+                @pl.when(e == value)
+                def _(j=j, i=i):
+                    pltpu.make_async_copy(h_flip.at[e], flips[j].at[i], f_sem.at[j, i]).start()
+
     for r in range(planes):
         pltpu.make_async_copy(h_buf.at[0], h_outs[r], h_sem.at[r]).wait()
-
-
-def project(where, own, other, weights, res, gain):
+    for j, chosen in enumerate(sends):
+        for i in range(len(chosen)):
+            pltpu.make_async_copy(h_flip.at[0], flips[j].at[i], f_sem.at[j, i]).wait()
+
+
+def project(where, own, other, weights, res, gain, sends):
     planes = len(own)
     widths = tuple(a.shape[1] for a in own[0])
     chips = len(weights) // planes
@@ -238,23 +249,25 @@
         flops=4 * rows * features * chips * depth, bytes_accessed=16 * 1024 * 1024, transcendentals=0
     )
     return pl.pallas_call(
-        functools.partial(project_kernel, planes, widths, chips),
+        functools.partial(project_kernel, planes, widths, chips, sends),
         out_shape=(
             *(shape((2, rows, features), BF),) * planes,
+            *(shape((len(chosen), features, 2 * rows), BF) for chosen in sends),
             shape((chips, features, 2 * rows), BF),
             shape((8, rows), F32),
         ),
         in_specs=[pl.BlockSpec(memory_space=pltpu.SMEM)]
         + [any_spec] * (2 * len(own) + planes * chips + planes)
         + [vmem_spec],
-        out_specs=(any_spec,) * planes + (vmem_spec,) * 2,
+        out_specs=(any_spec,) * (planes + len(sends)) + (vmem_spec,) * 2,
         scratch_shapes=buffers
         + [
             pltpu.VMEM((planes, 2, rows, features), BF),
             pltpu.VMEM((chips, 2, rows, features), BF),
         ]
         + semaphores
-        + [pltpu.SemaphoreType.DMA((n,)) for n in (planes, planes)],
+        + [pltpu.SemaphoreType.DMA((n,)) for n in (planes, planes)]
+        + [pltpu.SemaphoreType.DMA((max(len(sends), 1), 2))],
         compiler_params=params,
         cost_estimate=cost,
         name="project",
@@ -308,35 +321,62 @@
     )(grad, *own, *other)
 
 
-def place_kernel(count, axis, size, *refs):
-    where_ref = refs[0]
-    out = refs[-1]
+def joint_kernel(parts, rest, *refs):
+    grad, near = refs[:2]
+    pieces, outs = refs[2 : 2 + 4 * parts], refs[2 + 4 * parts :]
+    rows = pieces[0].shape[0]
+    for out, e, i in ((outs[0], rest, 1), (outs[1], 0, 0)):
+        start = 0
+        for g in range(parts):
+            own, other, near_own, near_other = (pieces[k * parts + g] for k in range(4))
+            total = dot(grad[e, :, :rows], own[...]) + dot(grad[e, :, rows:], other[...])
+            total += dot(near[i, :, :rows], near_own[...]) + dot(near[i, :, rows:], near_other[...])
+            out[0, :, start : start + own.shape[1]] = total.astype(BF)
+            start += own.shape[1]
+
+
+def joint_gradient(grad, near, pieces, rest):
+    chips, features, tokens = grad.shape
+    width = sum(a.shape[1] for a in pieces[0])
+    vmem_spec = pl.BlockSpec(memory_space=pltpu.VMEM)
+    return pl.pallas_call(
+        functools.partial(joint_kernel, len(pieces[0]), rest),
+        out_shape=(jax.ShapeDtypeStruct((1, features, width), BF),) * 2,
+        in_specs=[vmem_spec] * (2 + 4 * len(pieces[0])),
+        out_specs=(vmem_spec,) * 2,
+        compiler_params=pltpu.CompilerParams(vmem_limit_bytes=VMEM_LIMIT),
+        cost_estimate=pl.CostEstimate(
+            flops=2 * chips * features * tokens * width, bytes_accessed=8 * 1024 * 1024, transcendentals=0
+        ),
+        name="joint",
+    )(grad, near, *sum(pieces, []))
+
+
+def place_columns_kernel(count, *refs):
+    where_ref, out = refs[0], refs[-1]
+    size = refs[1].shape[2]
     for i in range(count):
         start = pl.multiple_of(where_ref[i] * size, size)
-        piece = refs[1 + i][...].astype(out.dtype)
-        if axis == 0:
-            out[pl.ds(start, size), :] = piece
-        else:
-            out[:, pl.ds(start, size)] = piece
-
-
-def place(slots, pieces, axis, dtype):
-    shape = list(pieces[0].shape)
-    size = shape[axis]
-    if axis == 1 and size % HD:
-        order = jnp.argsort(slots)
-        stacked = jnp.take(jnp.stack(pieces, 0), order, axis=0, mode="clip")
-        return jnp.concatenate([stacked[i] for i in range(len(pieces))], 1).astype(dtype)
-    shape[axis] *= len(pieces)
+        out[:, pl.ds(start, size)] = refs[1 + i][2 * i // count]
+
+
+def place_columns(slots, front, rear):
+    pieces = list(front) + list(rear)
+    count = len(pieces)
+    _, rows, size = pieces[0].shape
+    if size % HD:
+        flat = jnp.stack([p[2 * i // count] for i, p in enumerate(pieces)], 0)
+        flat = jnp.take(flat, jnp.argsort(slots), axis=0, mode="clip")
+        return jnp.concatenate([flat[i] for i in range(count)], 1)
     vmem_spec = pl.BlockSpec(memory_space=pltpu.VMEM)
     return pl.pallas_call(
-        functools.partial(place_kernel, len(pieces), axis, size),
-        out_shape=jax.ShapeDtypeStruct(tuple(shape), dtype),
-        in_specs=[pl.BlockSpec(memory_space=pltpu.SMEM)] + [vmem_spec] * len(pieces),
+        functools.partial(place_columns_kernel, count),
+        out_shape=jax.ShapeDtypeStruct((rows, count * size), BF),
+        in_specs=[pl.BlockSpec(memory_space=pltpu.SMEM)] + [vmem_spec] * count,
         out_specs=vmem_spec,
         compiler_params=pltpu.CompilerParams(vmem_limit_bytes=VMEM_LIMIT),
         cost_estimate=pl.CostEstimate(flops=0, bytes_accessed=6 * 1024 * 1024, transcendentals=0),
-        name="place",
+        name="place_columns",
     )(slots.astype(jnp.int32), *pieces)
 
 
@@ -486,17 +526,31 @@
                 own[t][g] = plane_send(attn[g], t)
             other[t][g] = partner(own[t][g])
 
+    early = {1: bits[0], 2: bits[1]} if len(bits) == 2 and n_head == 4 else {}
+    near_attn = {}
+    for t, bit in early.items():
+        mine, theirs = [], []
+        for g in range(parts):
+            mine.append(chip_send(own[t][g], bit))
+            theirs.append(partner(mine[-1]))
+        near_attn[t] = mine, theirs
+
     where = jnp.stack([chip, plane]).astype(jnp.int32)
     weights = sum(weights, [])
-    *h_outs, h_flip, sums = project(where, own, other, weights, res, gain[:, :, None])
+    sends = [(bit, sum(bits)) for bit in early.values()]
+    *h_outs, h_flip, sums = project(where, own, other, weights, res, gain[:, :, None], sends)
+    h_outs, flips = h_outs[:n_head], h_outs[n_head:]
+
+    near_flip = {}
+    for (t, bit), flip in zip(early.items(), flips):
+        near_flip[t] = chip_send(flip, bit)
 
     back = []
     for t in range(n_head):
         back.append(plane_send(h_outs[t], t) if t else h_outs[0])
-    rest = partner(jnp.stack([piece[1] for piece in back], 0))
-    pieces = [piece[0] for piece in back] + list(rest)
+    rest = [partner(piece) for piece in back]
     slots = [side * n_head + next_plane(-t) for side in (core, 1 - core) for t in range(n_head)]
-    hidden = place(jnp.stack(slots), pieces, 1, BF)
+    hidden = place_columns(jnp.stack(slots), back, rest)
 
     yours = partner(sums[:4])
     totals = sums[:4] + jnp.concatenate([yours[2:], yours[:2]], 0)
@@ -515,17 +569,33 @@
     first_term = error * inverse
     second_term = error * (weighted_sum * inverse * inverse * inverse) / model
     gain_near = jnp.take(gain, chip ^ jnp.arange(chips), axis=0, mode="clip")
-    grad = (
-        first_term[None, None, :] * gain_near[:, :, None] - second_term[None, None, :] * h_flip.astype(F32)
-    ).astype(BF)
+
+    def hidden_grad(terms, gains, flip):
+        return (
+            terms[0][None, None, :] * gains[:, :, None] - terms[1][None, None, :] * flip.astype(F32)
+        ).astype(BF)
+
+    terms = jnp.stack([first_term, second_term], 0)
+    grad = hidden_grad(terms, gain_near, h_flip)
+    near_grad = {}
+    for t, bit in early.items():
+        near_terms = chip_send(terms, bit)
+        gains = jnp.stack([gain_near[0], gain_near[sum(bits) ^ bit]], 0)
+        near_grad[t] = hidden_grad(near_terms, gains, near_flip[t])
 
     final = []
-    turns = sorted(range(n_head), key=lambda t: (t == 0, abs(2 * t - n_head), t))
+    turns = sorted(range(n_head), key=lambda t: (t != 0, t not in early, -t))
     for t in turns:
         turn = bits if t % 2 else bits[::-1]
         order = [sum(bit for k, bit in enumerate(turn[::-1]) if i >> k & 1) for i in range(chips)]
-        send, keep = gradient(grad, own[t], other[t], order)
-        for bit in turn:
+        if t in early:
+            pieces = [own[t], other[t], *near_attn[t]]
+            send, keep = joint_gradient(grad, near_grad[t], pieces, turn[1])
+        else:
+            send, keep = gradient(grad, own[t], other[t], order)
+        for stage, bit in enumerate(turn):
+            if t in early and not stage:
+                continue
             got = chip_send(send, bit)
             half = keep.shape[0] // 2
             if half:

time: 494 us -> 542 us (1.097)
  waiting for transfers between devices: 146 us -> 173 us
  starting transfers between devices: 143 us -> 162 us
    ppermute x36 -> x53, starting transfers between devices: 27.6 us -> 41.4 us  [seq_send(): return lax.ppermute(x, 'seq', xor_perm(n_seq, mask))]
    ppermute x21, waiting for transfers between devices: 71.2 us -> 85 us  [plane_send(): return lax.ppermute(x, 'head', shift_perm(n_head, step))]
    pallas_call x2 -> x4, Pallas kernels: 23.1 us -> 36.6 us  [the longest x1 20.4 us: project(): pl.pallas_call(functools.partial(project_kernel, planes, widths, chips, s...]
    ppermute x36 -> x53, waiting for transfers between devices: 49.7 us -> 62.3 us  [seq_send(): return lax.ppermute(x, 'seq', xor_perm(n_seq, mask))]
    pallas_call x4 -> x2, Pallas kernels: 23.8 us -> 12 us  [gradient(): pl.pallas_call(functools.partial(gradient_kernel, parts, order), out_shap...]
    ppermute x21, starting transfers between devices: 86.5 us -> 92.4 us  [plane_send(): return lax.ppermute(x, 'head', shift_perm(n_head, step))]
  transfers between devices with their start and end apart: 62 -> 79, of which waited for: 19 -> 21; matrix products, arithmetic and copies ran while one was open for 9% -> 8% of each run, Pallas kernels for 22% -> 20%
where the time goes in v3:
time: 542 us; the launch traced here: 533 us
  waiting for transfers between devices  173 us (32%)
  starting transfers between devices  162 us (30%)
  Pallas kernels  116 us (21%)
  blocking collectives  31.7 us (6%)
  local copies, waits for them, and re-layouts  24.2 us (4%)
  other arithmetic  24 us (4%)
    ppermute x21, starting transfers between devices, plane_send(): return lax.ppermute(x, 'head', shift_perm(n_head, step))  92.4 us
    ppermute x21, waiting for transfers between devices, plane_send(): return lax.ppermute(x, 'head', shift_perm(n_head, step))  85 us
    ppermute x53, waiting for transfers between devices, seq_send(): return lax.ppermute(x, 'seq', xor_perm(n_seq, mask))  62.3 us
    pallas_call x3, Pallas kernels, attention(): pl.pallas_call(attention_kernel, out_shape=jax.ShapeDtypeStruct((rows, co...  53 us
    ppermute x53, starting transfers between devices, seq_send(): return lax.ppermute(x, 'seq', xor_perm(n_seq, mask))  41.4 us
    all_to_all x1, blocking collectives, local(): came = lax.all_to_all(both, 'seq', split_axis=0, concat_axis=0, tiled=True)  31.7 us
    all_to_all x2, waiting for transfers between devices, local(): kv = lax.all_to_all(chosen, 'seq', split_axis=0, concat_axis=0, tiled=True)  25.1 us
    pallas_call x1, Pallas kernels, project(): pl.pallas_call(functools.partial(project_kernel, planes, widths, chips, s...  20.4 us
  transfers between devices with their start and end apart: 79, of which 21 were waited for; matrix products, arithmetic and copies ran while one was open for 8% of the time, Pallas kernels for 20%

profile of v3, /device:TPU:0, one launch (start us, length us, event | category | flops | bytes accessed | tf_op | source)
XLA Modules:
  0.0 532.7 jit_solution(12121512104401666230)
XLA Ops:
  3.2 31.7 %all_to_all.20.refs_1_ = bf16[8,2,512,128]{3,2,1,0:T(8,128)(2,1)} all-to-all(bf16[8,2,512,128]{3,2,1,0:T(8,128)(2,1)S(1)} %pad_maximum_fusion.1), channel_id=1, replica_groups=mesh['seq'=8,'head'=4] {'seq'}, dimensions={0} | all-to-all | bytes 4194304 | tf_op jit(solution)/shard_map/all_to_all | solution.py:487
  45.1 25.1 %all-to-all-done.1.kv = bf16[8,2,512,128]{3,2,1,0:T(8,128)(2,1)} async-done(((bf16[8,2,512,128]{3,2,1,0:T(8,128)(2,1)}), bf16[8,2,512,128]{3,2,1,0:T(8,128)(2,1)}, u32[]{:S(2)}, u32[]{:S(2)}) %all-to-all-start.1) | async-done | bytes 2097184 | tf_op jit(solution)/shard_map/all_to_all | solution.py:491
  90.4 25.1 %attend.3.refs_1_ = bf16[512,512]{1,0:T(8,128)(2,1)} custom-call(bf16[512,1024]{1,0:T(8,128)(2,1)} %q_ref.5, bf16[8,2,512,128]{3,2,1,0:T(8,128)(2,1)} %all-to-all-done.1.kv, bf16[512,256]{1,0:T(8,128)(2,1)} %sk_ref.5, bf16[512,256]{1,0:T(8,128)(2,1)} %sv_ref.5), custom_call_target="tpu_custom_call" | custom-call | flops 4831838208 | bytes 2359296 | tf_op jit(solution)/shard_map/attend/pallas_call | solution.py:84
  135.0 30.4 %collective-permute-start.7 = (bf16[512,512]{1,0:T(8,128)(2,1)}, bf16[512,512]{1,0:T(8,128)(2,1)S(1)}, u32[]{:S(2)}, u32[]{:S(2)}) collective-permute-start(bf16[512,512]{1,0:T(8,128)(2,1)} %collective-permute-done.4.refs_4_.refs_2_), channel_id=1, source_target_pairs={{0,1},{1,2},{2,3},{3,0},{4,5},{5,6},{6,7},{7,4},{8,9},{9,10},{10,1... | collective-permute-start | bytes 1572872 | tf_op jit(solution)/shard_map/ppermute | solution.py:447
  168.5 20.2 %collective-permute-done.2.refs_43_ = bf16[2,512,256]{2,1,0:T(8,128)(2,1)S(1)} collective-permute-done((bf16[2,512,256]{2,1,0:T(8,128)(2,1)S(1)}, bf16[2,512,256]{2,1,0:T(8,128)(2,1)S(1)}, u32[]{:S(2)}, u32[]{:S(2)}) %collective-permute-start.2) | collective-permute-done | bytes 524320 | tf_op jit(solution)/shard_map/ppermute | solution.py:447
  188.7 10.0 %collective-permute-start.10 = (bf16[512,512]{1,0:T(8,128)(2,1)S(1)}, bf16[512,512]{1,0:T(8,128)(2,1)S(1)}, u32[]{:S(2)}, u32[]{:S(2)}) collective-permute-start(bf16[512,512]{1,0:T(8,128)(2,1)S(1)} %collective-permute-done.7.refs_7_.refs_2_), channel_id=1, source_target_pairs={{0,1},{1,2},{2,3},{3,0},{4,5},{5,6},{6,7},{7,4},{8,9},{9,10},{10,1... | collective-permute-start | bytes 1572872 | tf_op jit(solution)/shard_map/ppermute | solution.py:447
  202.3 7.1 %collective-permute-done.10.refs_10_.refs_1_ = bf16[512,512]{1,0:T(8,128)(2,1)S(1)} collective-permute-done((bf16[512,512]{1,0:T(8,128)(2,1)S(1)}, bf16[512,512]{1,0:T(8,128)(2,1)S(1)}, u32[]{:S(2)}, u32[]{:S(2)}) %collective-permute-start.10) | collective-permute-done | bytes 524320 | tf_op jit(solution)/shard_map/ppermute | solution.py:447
  218.5 6.5 %collective-permute-done.28.refs_29_ = bf16[256,1024]{1,0:T(8,128)(2,1)S(1)} collective-permute-done((bf16[256,1024]{1,0:T(8,128)(2,1)S(1)}, bf16[256,1024]{1,0:T(8,128)(2,1)S(1)}, u32[]{:S(2)}, u32[]{:S(2)}) %collective-permute-start.28) | collective-permute-done | bytes 524320 | tf_op jit(solution)/shard_map/ppermute | solution.py:432
  238.1 13.9 %attend.5.refs_3_ = bf16[512,256]{1,0:T(8,128)(2,1)} custom-call(bf16[512,1024]{1,0:T(8,128)(2,1)} %q_ref.5, bf16[8,2,512,128]{3,2,1,0:T(8,128)(2,1)} %copy-done.1, bf16[512,256]{1,0:T(8,128)(2,1)} %sk_ref.5, bf16[512,256]{1,0:T(8,128)(2,1)} %sv_ref.5), custom_call_target="tpu_custom_call" | custom-call | flops 2415919104 | bytes 2359296 | tf_op jit(solution)/shard_map/attend/pallas_call | solution.py:84
  252.0 14.0 %attend.4.refs_2_ = bf16[512,256]{1,0:T(8,128)(2,1)} custom-call(bf16[512,1024]{1,0:T(8,128)(2,1)} %q_ref.5, bf16[8,2,512,128]{3,2,1,0:T(8,128)(2,1)} %copy-done.1, bf16[512,256]{1,0:T(8,128)(2,1)} %sk_ref.5, bf16[512,256]{1,0:T(8,128)(2,1)} %sv_ref.5), custom_call_target="tpu_custom_call" | custom-call | flops 2415919104 | bytes 2359296 | tf_op jit(solution)/shard_map/attend/pallas_call | solution.py:84
  266.1 12.9 %collective-permute-start.5 = (bf16[512,256]{1,0:T(8,128)(2,1)}, bf16[512,256]{1,0:T(8,128)(2,1)S(1)}, u32[]{:S(2)}, u32[]{:S(2)}) collective-permute-start(bf16[512,256]{1,0:T(8,128)(2,1)} %attend.4.refs_2_), channel_id=1, source_target_pairs={{0,1},{1,2},{2,3},{3,0},{4,5},{5,6},{6,7},{7,4},{8,9},{9,10},{10,1... | collective-permute-start | bytes 786440 | tf_op jit(solution)/shard_map/ppermute | solution.py:447
  291.5 13.0 %collective-permute-done.8.refs_8_.refs_3_ = bf16[512,256]{1,0:T(8,128)(2,1)S(1)} collective-permute-done((bf16[512,256]{1,0:T(8,128)(2,1)}, bf16[512,256]{1,0:T(8,128)(2,1)S(1)}, u32[]{:S(2)}, u32[]{:S(2)}) %collective-permute-start.8) | collective-permute-done | bytes 262176 | tf_op jit(solution)/shard_map/ppermute | solution.py:447
  316.4 20.4 %project.1 = (bf16[2,512,256]{2,1,0:T(8,128)(2,1)}, bf16[2,512,256]{2,1,0:T(8,128)(2,1)}, bf16[2,512,256]{2,1,0:T(8,128)(2,1)}, bf16[2,512,256]{2,1,0:T(8,128)(2...) custom-call(s32[2]{0:T(128)} %pad_add_fusion.refs_0_, ...), custom_call_target="tpu_custom_call" | custom-call | flops 8589934592 | bytes 16777216 | tf_op jit(solution)/shard_map/project/pallas_call | solution.py:251
  339.5 12.3 %collective-permute-start.48 = (f32[4,512]{1,0:T(4,128)S(1)}, f32[4,512]{1,0:T(4,128)S(1)}, u32[]{:S(2)}, u32[]{:S(2)}) collective-permute-start(f32[4,512]{1,0:T(4,128)S(1)} %maximum_add_fusion), channel_id=1, source_target_pairs={{0,1},{1,0},{2,3},{3,2},{4,5},{5,4},{6,7},{7,6},{8,9},{9,8},{10,11... | collective-permute-start | bytes 24584 | tf_op jit(solution)/shard_map/ppermute | solution.py:559
  376.5 6.0 %gradient.3 = (bf16[2,256,1024]{2,1,0:T(8,128)(2,1)}, bf16[2,256,1024]{2,1,0:T(8,128)(2,1)}) custom-call(bf16[4,256,1024]{2,1,0:T(8,128)(2,1)} %subtract_convert_fusion.refs_0_, bf16[512,512]{1,0:T(8,128)(2,1)} %attend.3.refs_1_, bf16[512,256]{1,0:T(8,128)(2,1)} %attend.4.refs_2_, bf16[512,256]{1,0:T(8,128)(2,1)} %attend.5.refs_3_, ...), custom_call_target="tpu_custom_call" | custom-call | flops 2147483648 | bytes 8388608 | tf_op jit(solution)/shard_map/gradient/pallas_call | solution.py:311
  383.1 13.8 %collective-permute-done.56 = f32[2,1024]{1,0:T(2,128)S(1)} collective-permute-done((f32[2,1024]{1,0:T(2,128)S(1)}, f32[2,1024]{1,0:T(2,128)S(1)}, u32[]{:S(2)}, u32[]{:S(2)}) %collective-permute-start.56) | collective-permute-done | bytes 8224 | tf_op jit(solution)/shard_map/ppermute | solution.py:432
  407.7 6.2 %joint.2 = (bf16[1,256,1024]{2,1,0:T(8,128)(2,1)}, bf16[1,256,1024]{2,1,0:T(8,128)(2,1)}) custom-call(bf16[4,256,1024]{2,1,0:T(8,128)(2,1)} %subtract_convert_fusion.refs_0_, bf16[2,256,1024]{2,1,0:T(8,128)(2,1)} %subtract_convert_fusion.2.refs_1_, bf16[512,512]{1,0:T(8,128)(2,1)} %copy-done.23, bf16[512,256]{1,0:T(8,128)(2,1)} %copy-done.44, ...), custom_call_target="tpu_custom_call" | custom-call | flops 2147483648 | bytes 8388608 | tf_op jit(solution)/shard_map/joint/pallas_call | solution.py:342
  414.0 18.9 %collective-permute-done.70.refs_10_ = bf16[512,256]{1,0:T(8,128)(2,1)} collective-permute-done((bf16[512,256]{1,0:T(8,128)(2,1)S(1)}, bf16[512,256]{1,0:T(8,128)(2,1)}, u32[]{:S(2)}, u32[]{:S(2)}) %collective-permute-start.70) | collective-permute-done | bytes 262176 | tf_op jit(solution)/shard_map/ppermute | solution.py:432
  442.7 6.3 %joint.3 = (bf16[1,256,1024]{2,1,0:T(8,128)(2,1)}, bf16[1,256,1024]{2,1,0:T(8,128)(2,1)}) custom-call(bf16[4,256,1024]{2,1,0:T(8,128)(2,1)} %subtract_convert_fusion.refs_0_, bf16[2,256,1024]{2,1,0:T(8,128)(2,1)} %subtract_convert_fusion.1.refs_1_, bf16[512,512]{1,0:T(8,128)(2,1)} %collective-permute-done.4.refs_4_.refs_2_, bf16[512,256]{1,0:T(8,128)(2,1)} %copy-done.39, ...), custom_call_target="tpu_custom_call" | custom-call | flops 2147483648 | bytes 8388608 | tf_op jit(solution)/shard_map/joint/pallas_call | solution.py:342
  454.8 7.9 %collective-permute-done.64 = bf16[1,256,1024]{2,1,0:T(8,128)(2,1)S(1)} collective-permute-done((bf16[1,256,1024]{2,1,0:T(8,128)(2,1)}, bf16[1,256,1024]{2,1,0:T(8,128)(2,1)S(1)}, u32[]{:S(2)}, u32[]{:S(2)}) %collective-permute-start.64) | collective-permute-done | bytes 524320 | tf_op jit(solution)/shard_map/ppermute | solution.py:432
  465.4 11.1 %collective-permute-done.41.refs_3_ = bf16[2,512,256]{2,1,0:T(8,128)(2,1)} collective-permute-done((bf16[2,512,256]{2,1,0:T(8,128)(2,1)}, bf16[2,512,256]{2,1,0:T(8,128)(2,1)}, u32[]{:S(2)}, u32[]{:S(2)}) %collective-permute-start.41) | collective-permute-done | bytes 524320 | tf_op jit(solution)/shard_map/ppermute | solution.py:447
  481.9 10.7 %collective-permute-start.65 = (bf16[256,1024]{1,0:T(8,128)(2,1)}, bf16[256,1024]{1,0:T(8,128)(2,1)S(1)}, u32[]{:S(2)}, u32[]{:S(2)}) collective-permute-start(bf16[256,1024]{1,0:T(8,128)(2,1)} %fusion.2), channel_id=1, source_target_pairs={{0,2},{1,3},{2,0},{3,1},{4,6},{5,7},{6,4},{7,5},{8,10},{9,11},{10,... | collective-permute-start | bytes 1572872 | tf_op jit(solution)/shard_map/ppermute | solution.py:447
  504.5 12.2 %collective-permute-done.65.refs_2_ = bf16[256,1024]{1,0:T(8,128)(2,1)S(1)} collective-permute-done((bf16[256,1024]{1,0:T(8,128)(2,1)}, bf16[256,1024]{1,0:T(8,128)(2,1)S(1)}, u32[]{:S(2)}, u32[]{:S(2)}) %collective-permute-start.65) | collective-permute-done | bytes 524320 | tf_op jit(solution)/shard_map/ppermute | solution.py:447
  520.7 9.7 %collective-permute-done.53.refs_1_ = bf16[256,1024]{1,0:T(8,128)(2,1)} collective-permute-done((bf16[256,1024]{1,0:T(8,128)(2,1)}, bf16[256,1024]{1,0:T(8,128)(2,1)}, u32[]{:S(2)}, u32[]{:S(2)}) %collective-permute-start.53) | collective-permute-done | bytes 524320 | tf_op jit(solution)/shard_map/ppermute | solution.py:447
  (327 shorter events, 185.6 us)
Async XLA Ops:
  70.2 50.5 %all-to-all-start.2 = ((bf16[8,2,512,128]{3,2,1,0:T(8,128)(2,1)}), bf16[8,2,512,128]{3,2,1,0:T(8,128)(2,1)}, u32[]{:S(2)}, u32[]{:S(2)}) async-start(bf16[8,2,512,128]{3,2,1,0:T(8,128)(2,1)} %pad_maximum_fusion), calls=%async_computation.2 | async-start | bytes 4194304 | tf_op jit(solution)/shard_map/all_to_all | solution.py:487
  79.4 36.7 %collective-permute-start = (bf16[512,4,256]{2,0,1:T(8,128)(2,1)}, bf16[512,4,256]{2,0,1:T(8,128)(2,1)}, u32[]{:S(2)}, u32[]{:S(2)}) collective-permute-start(bf16[512,4,256]{2,0,1:T(8,128)(2,1)} %bitcast.60), channel_id=1, source_target_pairs={{0,4},{4,0},{8,12},{12,8},{16,20},{20,16},{24,28},{28,24},{1,5},{5... | collective-permute-start | bytes 3145736 | tf_op jit(solution)/shard_map/ppermute | solution.py:432
  82.6 48.6 %collective-permute-start.25 = (bf16[256,1024]{1,0:T(8,128)(2,1)}, bf16[256,1024]{1,0:T(8,128)(2,1)}, u32[]{:S(2)}, u32[]{:S(2)}) collective-permute-start(bf16[256,1024]{1,0:T(8,128)(2,1)} %get-tuple-element.85), channel_id=1, source_target_pairs={{0,1},{1,2},{2,3},{3,0},{4,5},{5,6},{6,7},{7,4},{8,9},{9,10},{10,1... | collective-permute-start | bytes 1572872 | tf_op jit(solution)/shard_map/ppermute | solution.py:447
  84.2 50.6 %collective-permute-start.26 = (bf16[256,1024]{1,0:T(8,128)(2,1)}, bf16[256,1024]{1,0:T(8,128)(2,1)}, u32[]{:S(2)}, u32[]{:S(2)}) collective-permute-start(bf16[256,1024]{1,0:T(8,128)(2,1)} %get-tuple-element.87), channel_id=1, source_target_pairs={{0,2},{1,3},{2,0},{3,1},{4,6},{5,7},{6,4},{7,5},{8,10},{9,11},{10,... | collective-permute-start | bytes 1572872 | tf_op jit(solution)/shard_map/ppermute | solution.py:447
  86.8 78.6 %collective-permute-start.27 = (bf16[256,1024]{1,0:T(8,128)(2,1)}, bf16[256,1024]{1,0:T(8,128)(2,1)}, u32[]{:S(2)}, u32[]{:S(2)}) collective-permute-start(bf16[256,1024]{1,0:T(8,128)(2,1)} %get-tuple-element.84), channel_id=1, source_target_pairs={{0,3},{1,0},{2,1},{3,2},{4,7},{5,4},{6,5},{7,6},{8,11},{9,8},{10,9... | collective-permute-start | bytes 1572872 | tf_op jit(solution)/shard_map/ppermute | solution.py:447
  119.0 48.0 %collective-permute-start.1 = (bf16[2,512,256]{2,1,0:T(8,128)(2,1)}, bf16[2,512,256]{2,1,0:T(8,128)(2,1)}, u32[]{:S(2)}, u32[]{:S(2)}) collective-permute-start(bf16[2,512,256]{2,1,0:T(8,128)(2,1)} %pad_maximum_fusion.3), channel_id=1, source_target_pairs={{0,1},{1,2},{2,3},{3,0},{4,5},{5,6},{6,7},{7,4},{8,9},{9,10},{10,1... | collective-permute-start | bytes 1572872 | tf_op jit(solution)/shard_map/ppermute | solution.py:447
  125.1 106.4 %all-to-all-start.3 = ((bf16[8,2,512,128]{3,2,1,0:T(8,128)(2,1)}), bf16[8,2,512,128]{3,2,1,0:T(8,128)(2,1)S(1)}, u32[]{:S(2)}, u32[]{:S(2)}) async-start(bf16[8,2,512,128]{3,2,1,0:T(8,128)(2,1)} %get-tuple-element.49), calls=%async_computation.3 | async-start | bytes 4194304 | tf_op jit(solution)/shard_map/all_to_all | solution.py:491
  131.2 57.5 %collective-permute-start.2 = (bf16[2,512,256]{2,1,0:T(8,128)(2,1)S(1)}, bf16[2,512,256]{2,1,0:T(8,128)(2,1)S(1)}, u32[]{:S(2)}, u32[]{:S(2)}) collective-permute-start(bf16[2,512,256]{2,1,0:T(8,128)(2,1)S(1)} %pad_maximum_fusion.4), channel_id=1, source_target_pairs={{0,2},{1,3},{2,0},{3,1},{4,6},{5,7},{6,4},{7,5},{8,10},{9,11},{10,... | collective-permute-start | bytes 1572872 | tf_op jit(solution)/shard_map/ppermute | solution.py:447
  134.8 64.0 %collective-permute-start.3 = (bf16[2,512,256]{2,1,0:T(8,128)(2,1)S(1)}, bf16[2,512,256]{2,1,0:T(8,128)(2,1)S(1)}, u32[]{:S(2)}, u32[]{:S(2)}) collective-permute-start(bf16[2,512,256]{2,1,0:T(8,128)(2,1)S(1)} %pad_maximum_fusion.5), channel_id=1, source_target_pairs={{0,3},{1,0},{2,1},{3,2},{4,7},{5,4},{6,5},{7,6},{8,11},{9,8},{10,9... | collective-permute-start | bytes 1572872 | tf_op jit(solution)/shard_map/ppermute | solution.py:447
  135.0 53.7 %collective-permute-start.7 = (bf16[512,512]{1,0:T(8,128)(2,1)}, bf16[512,512]{1,0:T(8,128)(2,1)S(1)}, u32[]{:S(2)}, u32[]{:S(2)}) collective-permute-start(bf16[512,512]{1,0:T(8,128)(2,1)} %collective-permute-done.4.refs_4_.refs_2_), channel_id=1, source_target_pairs={{0,1},{1,2},{2,3},{3,0},{4,5},{5,6},{6,7},{7,4},{8,9},{9,10},{10,1... | collective-permute-start | bytes 1572872 | tf_op jit(solution)/shard_map/ppermute | solution.py:447
  167.0 33.8 %collective-permute-start.30 = (bf16[256,1024]{1,0:T(8,128)(2,1)}, bf16[256,1024]{1,0:T(8,128)(2,1)S(1)}, u32[]{:S(2)}, u32[]{:S(2)}) collective-permute-start(bf16[256,1024]{1,0:T(8,128)(2,1)} %collective-permute-done.26.refs_27_), channel_id=1, source_target_pairs={{0,8},{4,12},{8,0},{12,4},{16,24},{20,28},{24,16},{28,20},{1,9},{5... | collective-permute-start | bytes 1572872 | tf_op jit(solution)/shard_map/ppermute | solution.py:432
  217.1 49.0 %collective-permute-start.29 = (bf16[256,1024]{1,0:T(8,128)(2,1)}, bf16[256,1024]{1,0:T(8,128)(2,1)}, u32[]{:S(2)}, u32[]{:S(2)}) collective-permute-start(bf16[256,1024]{1,0:T(8,128)(2,1)} %collective-permute-done.25.refs_26_), channel_id=1, source_target_pairs={{0,8},{4,12},{8,0},{12,4},{16,24},{20,28},{24,16},{28,20},{1,9},{5... | collective-permute-start | bytes 1572872 | tf_op jit(solution)/shard_map/ppermute | solution.py:432
  217.9 61.2 %collective-permute-start.35 = (bf16[256,1024]{1,0:T(8,128)(2,1)}, bf16[256,1024]{1,0:T(8,128)(2,1)}, u32[]{:S(2)}, u32[]{:S(2)}) collective-permute-start(bf16[256,1024]{1,0:T(8,128)(2,1)} %collective-permute-done.27.refs_28_), channel_id=1, source_target_pairs={{0,16},{4,20},{8,24},{12,28},{16,0},{20,4},{24,8},{28,12},{1,17},{... | collective-permute-start | bytes 1572872 | tf_op jit(solution)/shard_map/ppermute | solution.py:432
  225.0 54.1 %collective-permute-start.34 = (bf16[256,1024]{1,0:T(8,128)(2,1)}, bf16[256,1024]{1,0:T(8,128)(2,1)}, u32[]{:S(2)}, u32[]{:S(2)}) collective-permute-start(bf16[256,1024]{1,0:T(8,128)(2,1)} %collective-permute-done.26.refs_27_), channel_id=1, source_target_pairs={{0,16},{4,20},{8,24},{12,28},{16,0},{20,4},{24,8},{28,12},{1,17},{... | collective-permute-start | bytes 1572872 | tf_op jit(solution)/shard_map/ppermute | solution.py:432
  228.8 50.3 %collective-permute-start.37 = (bf16[256,1024]{1,0:T(8,128)(2,1)}, bf16[256,1024]{1,0:T(8,128)(2,1)}, u32[]{:S(2)}, u32[]{:S(2)}) collective-permute-start(bf16[256,1024]{1,0:T(8,128)(2,1)} %collective-permute-done.33.refs_34_), channel_id=1, source_target_pairs={{0,8},{4,12},{8,0},{12,4},{16,24},{20,28},{24,16},{28,20},{1,9},{5... | collective-permute-start | bytes 1572872 | tf_op jit(solution)/shard_map/ppermute | solution.py:432
  236.3 45.7 %collective-permute-start.39 = (bf16[256,1024]{1,0:T(8,128)(2,1)}, bf16[256,1024]{1,0:T(8,128)(2,1)S(1)}, u32[]{:S(2)}, u32[]{:S(2)}) collective-permute-start(bf16[256,1024]{1,0:T(8,128)(2,1)} %collective-permute-done.31.refs_32_), channel_id=1, source_target_pairs={{0,16},{4,20},{8,24},{12,28},{16,0},{20,4},{24,8},{28,12},{1,17},{... | collective-permute-start | bytes 1572872 | tf_op jit(solution)/shard_map/ppermute | solution.py:432
  315.4 46.4 %collective-permute-start.50 = (f32[512]{0:T(512)S(1)}, f32[512]{0:T(512)S(1)}, u32[]{:S(2)}, u32[]{:S(2)}) collective-permute-start(f32[512]{0:T(512)S(1)} %select_reduce_fusion), channel_id=1, source_target_pairs={{0,4},{4,0},{8,12},{12,8},{16,20},{20,16},{24,28},{28,24},{1,5},{5... | collective-permute-start | bytes 6152 | tf_op jit(solution)/shard_map/ppermute | solution.py:432
  361.8 43.5 %collective-permute-start.57 = (bf16[2,256,1024]{2,1,0:T(8,128)(2,1)}, bf16[2,256,1024]{2,1,0:T(8,128)(2,1)S(1)}, u32[]{:S(2)}, u32[]{:S(2)}) collective-permute-start(bf16[2,256,1024]{2,1,0:T(8,128)(2,1)} %get-tuple-element.73), channel_id=1, source_target_pairs={{0,16},{4,20},{8,24},{12,28},{16,0},{20,4},{24,8},{28,12},{1,17},{... | collective-permute-start | bytes 3145736 | tf_op jit(solution)/shard_map/ppermute | solution.py:432
  374.0 58.9 %collective-permute-start.67 = (bf16[2,256,1024]{2,1,0:T(8,128)(2,1)}, bf16[2,256,1024]{2,1,0:T(8,128)(2,1)S(1)}, u32[]{:S(2)}, u32[]{:S(2)}) collective-permute-start(bf16[2,256,1024]{2,1,0:T(8,128)(2,1)} %get-tuple-element.76), channel_id=1, source_target_pairs={{0,8},{4,12},{8,0},{12,4},{16,24},{20,28},{24,16},{28,20},{1,9},{5... | collective-permute-start | bytes 3145736 | tf_op jit(solution)/shard_map/ppermute | solution.py:432
  403.1 45.9 %collective-permute-start.51 = (bf16[2,256,1024]{2,1,0:T(8,128)(2,1)}, bf16[2,256,1024]{2,1,0:T(8,128)(2,1)}, u32[]{:S(2)}, u32[]{:S(2)}) collective-permute-start(bf16[2,256,1024]{2,1,0:T(8,128)(2,1)} %get-tuple-element.70), channel_id=1, source_target_pairs={{0,8},{4,12},{8,0},{12,4},{16,24},{20,28},{24,16},{28,20},{1,9},{5... | collective-permute-start | bytes 3145736 | tf_op jit(solution)/shard_map/ppermute | solution.py:432
  405.4 46.8 %collective-permute-start.54 = (bf16[2,256,1024]{2,1,0:T(8,128)(2,1)}, bf16[2,256,1024]{2,1,0:T(8,128)(2,1)S(1)}, u32[]{:S(2)}, u32[]{:S(2)}) collective-permute-start(bf16[2,256,1024]{2,1,0:T(8,128)(2,1)} %get-tuple-element.72), channel_id=1, source_target_pairs={{0,16},{4,20},{8,24},{12,28},{16,0},{20,4},{24,8},{28,12},{1,17},{... | collective-permute-start | bytes 3145736 | tf_op jit(solution)/shard_map/ppermute | solution.py:432
  438.6 37.9 %collective-permute-start.41 = (bf16[2,512,256]{2,1,0:T(8,128)(2,1)}, bf16[2,512,256]{2,1,0:T(8,128)(2,1)}, u32[]{:S(2)}, u32[]{:S(2)}) collective-permute-start(bf16[2,512,256]{2,1,0:T(8,128)(2,1)} %get-tuple-element.65), channel_id=1, source_target_pairs={{0,2},{1,3},{2,0},{3,1},{4,6},{5,7},{6,4},{7,5},{8,10},{9,11},{10,... | collective-permute-start | bytes 1572872 | tf_op jit(solution)/shard_map/ppermute | solution.py:447
  442.7 33.8 %collective-permute-start.42 = (bf16[2,512,256]{2,1,0:T(8,128)(2,1)}, bf16[2,512,256]{2,1,0:T(8,128)(2,1)}, u32[]{:S(2)}, u32[]{:S(2)}) collective-permute-start(bf16[2,512,256]{2,1,0:T(8,128)(2,1)} %get-tuple-element.66), channel_id=1, source_target_pairs={{0,3},{1,0},{2,1},{3,2},{4,7},{5,4},{6,5},{7,6},{8,11},{9,8},{10,9... | collective-permute-start | bytes 1572872 | tf_op jit(solution)/shard_map/ppermute | solution.py:447
  481.9 34.9 %collective-permute-start.65 = (bf16[256,1024]{1,0:T(8,128)(2,1)}, bf16[256,1024]{1,0:T(8,128)(2,1)S(1)}, u32[]{:S(2)}, u32[]{:S(2)}) collective-permute-start(bf16[256,1024]{1,0:T(8,128)(2,1)} %fusion.2), channel_id=1, source_target_pairs={{0,2},{1,3},{2,0},{3,1},{4,6},{5,7},{6,4},{7,5},{8,10},{9,11},{10,... | collective-permute-start | bytes 1572872 | tf_op jit(solution)/shard_map/ppermute | solution.py:447
  (115 other events, 2020.1 us)

commit v4 on v3

--- a/solution.py
+++ b/solution.py
@@ -10,6 +10,7 @@
 
 
 HD = 128
+SEQ, HEAD = "seq", "head"
 EPSILON = 1e-05
 MASKED = -1e30
 BF = jnp.bfloat16
@@ -143,6 +144,7 @@
     parts = len(widths)
     block = sum(widths)
     chips = len(weights) // planes
+    rows = a_buf.shape[0] // 2
     copies = []
     for side in range(2):
         for t in range(planes):
@@ -151,7 +153,7 @@
                 copies.append(
                     pltpu.make_async_copy(
                         sides[side][t * parts + g],
-                        a_buf.at[side, :, start : start + widths[g]],
+                        a_buf.at[pl.ds(side * rows, rows), start : start + widths[g]],
                         a_sem.at[side, t * parts + g],
                     )
                 )
@@ -187,7 +189,7 @@
     h_outs, refs = refs[:planes], refs[planes:]
     flips, refs = refs[: len(sends)], refs[len(sends) :]
     h_flip, sums, a_buf, w_buf, r_buf, h_buf, a_sem, w_sem, r_sem, h_sem, f_sem = refs
-    rows = a_buf.shape[1]
+    rows = a_buf.shape[0] // 2
     chip = where_ref[0]
     plane = where_ref[1]
     more = [pltpu.make_async_copy(res[r], r_buf.at[r], r_sem.at[r]) for r in range(planes)]
@@ -203,8 +205,9 @@
         gain_col = gain[home]
         came = lax.rem(plane - home + planes, planes)
         goes = lax.rem(home - plane + planes, planes)
+        both = dot_t(a_buf[...], w_buf[e])
         for side in range(2):
-            total = dot_t(a_buf[side], w_buf[e])
+            total = both[side * rows : (side + 1) * rows]
             h = (r_buf[came, side].astype(F32) + total).astype(BF)
             h_buf[e, side] = h
             flip = h.astype(F32).T
@@ -242,7 +245,7 @@
     any_spec = pl.BlockSpec(memory_space=pl.ANY)
     vmem_spec = pl.BlockSpec(memory_space=pltpu.VMEM)
     own, other = sum(own, []), sum(other, [])
-    buffers = [pltpu.VMEM((2, rows, depth), BF), pltpu.VMEM((chips, features, depth), BF)]
+    buffers = [pltpu.VMEM((2 * rows, depth), BF), pltpu.VMEM((chips, features, depth), BF)]
     semaphores = [pltpu.SemaphoreType.DMA((2, len(own))), pltpu.SemaphoreType.DMA((chips, planes))]
     params = pltpu.CompilerParams(vmem_limit_bytes=VMEM_LIMIT)
     cost = pl.CostEstimate(
@@ -424,12 +427,12 @@
     group = queries.shape[1] // (kv_heads * HD)
     positions = prefix_k.shape[1]
     block_len = positions // n_seq
-    seq = lax.axis_index("seq")
-    plane = lax.axis_index("head")
+    seq = lax.axis_index(SEQ)
+    plane = lax.axis_index(HEAD)
     chip, core = seq // 2, seq % 2
 
     def seq_send(x, mask):
-        return lax.ppermute(x, "seq", xor_perm(n_seq, mask))
+        return lax.ppermute(x, SEQ, xor_perm(n_seq, mask))
 
     def partner(x):
         return seq_send(x, 1)
@@ -438,13 +441,13 @@
         return seq_send(x, 2 * bit)
 
     def plane_send(x, step):
-        return lax.ppermute(x, "head", shift_perm(n_head, step))
+        return lax.ppermute(x, HEAD, shift_perm(n_head, step))
 
     def next_plane(step):
         return (plane + step) % n_head
 
     def plane_send(x, step):
-        return lax.ppermute(x, "head", shift_perm(n_head, step))
+        return lax.ppermute(x, HEAD, shift_perm(n_head, step))
 
     def next_plane(step):
         return (plane + step) % n_head
@@ -484,11 +487,11 @@
         both = jnp.stack([x[0, :, cut].reshape(n_seq, block_len, HD) for x in (prefix_k, prefix_v)], 1)
         if head:
             both = tie(both, kv)
-        came = lax.all_to_all(both, "seq", split_axis=0, concat_axis=0, tiled=True)
+        came = lax.all_to_all(both, SEQ, split_axis=0, concat_axis=0, tiled=True)
         if head:
             came = tie(came, attn[-1])
         chosen, caches = route(pick, came, head, kv_heads, caches)
-        kv = lax.all_to_all(chosen, "seq", split_axis=0, concat_axis=0, tiled=True)
+        kv = lax.all_to_all(chosen, SEQ, split_axis=0, concat_axis=0, tiled=True)
         last = head == kv_heads - 1
         count = max(group // 2, 1) if last else group
         for step, first in enumerate(range(0, group, count)):
@@ -556,7 +559,7 @@
     totals = sums[:4] + jnp.concatenate([yours[2:], yours[:2]], 0)
     step = 1
     while step < n_head:
-        totals = totals + lax.ppermute(totals, "head", xor_perm(n_head, step))
+        totals = totals + lax.ppermute(totals, HEAD, xor_perm(n_head, step))
         step *= 2
     square_sum = jnp.concatenate([totals[0], totals[2]])
     weighted_sum = jnp.concatenate([totals[1], totals[3]])
@@ -614,27 +617,27 @@
 
 def solution(mesh):
     in_specs = (
-        P("seq", None, "head"),
-        P("seq", None, "head"),
-        P("seq", "head"),
-        P("seq", "head"),
-        P("seq", "head"),
-        P("seq", "head"),
-        P("seq", "head"),
+        P(SEQ, None, HEAD),
+        P(SEQ, None, HEAD),
+        P(SEQ, HEAD),
+        P(SEQ, HEAD),
+        P(SEQ, HEAD),
+        P(SEQ, HEAD),
+        P(SEQ, HEAD),
         P(),
         P(),
         P(),
         P(),
         P(),
-        P("seq"),
+        P(SEQ),
     )
     out_specs = (
-        P(None, "seq", "head"),
-        P(None, "seq", "head"),
-        P("seq", "head"),
-        P("seq"),
-        P("seq", "head"),
+        P(None, SEQ, HEAD),
+        P(None, SEQ, HEAD),
+        P(SEQ, HEAD),
+        P(SEQ),
+        P(SEQ, HEAD),
     )
-    body = functools.partial(local, mesh.shape["seq"], mesh.shape["head"])
+    body = functools.partial(local, mesh.shape[SEQ], mesh.shape[HEAD])
 
     return jax.shard_map(body, mesh=mesh, in_specs=in_specs, out_specs=out_specs, check_vma=False)

time: 542 us -> 542 us (level)
  no operation moved by 1% of the time
where the time goes in v4:
time: 542 us; the launch traced here: 533 us
  waiting for transfers between devices  173 us (32%)
  starting transfers between devices  162 us (30%)
  Pallas kernels  116 us (21%)
  blocking collectives  31.7 us (6%)
  local copies, waits for them, and re-layouts  24.2 us (4%)
  other arithmetic  24 us (4%)
    ppermute x21, starting transfers between devices, plane_send(): return lax.ppermute(x, HEAD, shift_perm(n_head, step))  92.5 us
    ppermute x21, waiting for transfers between devices, plane_send(): return lax.ppermute(x, HEAD, shift_perm(n_head, step))  85 us
    ppermute x53, waiting for transfers between devices, seq_send(): return lax.ppermute(x, SEQ, xor_perm(n_seq, mask))  62.3 us
    pallas_call x3, Pallas kernels, attention(): pl.pallas_call(attention_kernel, out_shape=jax.ShapeDtypeStruct((rows, co...  53 us
    ppermute x53, starting transfers between devices, seq_send(): return lax.ppermute(x, SEQ, xor_perm(n_seq, mask))  41.4 us
    all_to_all x1, blocking collectives, local(): came = lax.all_to_all(both, SEQ, split_axis=0, concat_axis=0, tiled=True)  31.7 us
    all_to_all x2, waiting for transfers between devices, local(): kv = lax.all_to_all(chosen, SEQ, split_axis=0, concat_axis=0, tiled=True)  25.1 us
    pallas_call x1, Pallas kernels, project(): pl.pallas_call(functools.partial(project_kernel, planes, widths, chips, s...  20.3 us
  transfers between devices with their start and end apart: 79, of which 21 were waited for; matrix products, arithmetic and copies ran while one was open for 8% of the time, Pallas kernels for 20%

profile of v4, /device:TPU:0, one launch (start us, length us, event | category | flops | bytes accessed | tf_op | source)
XLA Modules:
  0.0 532.6 jit_solution(16435802484059314084)
XLA Ops:
  3.2 31.7 %all_to_all.20.refs_1_ = bf16[8,2,512,128]{3,2,1,0:T(8,128)(2,1)} all-to-all(bf16[8,2,512,128]{3,2,1,0:T(8,128)(2,1)S(1)} %pad_maximum_fusion.1), channel_id=1, replica_groups=mesh['seq'=8,'head'=4] {'seq'}, dimensions={0} | all-to-all | bytes 4194304 | tf_op jit(solution)/shard_map/all_to_all | solution.py:490
  45.1 25.1 %all-to-all-done.1.kv = bf16[8,2,512,128]{3,2,1,0:T(8,128)(2,1)} async-done(((bf16[8,2,512,128]{3,2,1,0:T(8,128)(2,1)}), bf16[8,2,512,128]{3,2,1,0:T(8,128)(2,1)}, u32[]{:S(2)}, u32[]{:S(2)}) %all-to-all-start.1) | async-done | bytes 2097184 | tf_op jit(solution)/shard_map/all_to_all | solution.py:494
  90.4 25.1 %attend.3.refs_1_ = bf16[512,512]{1,0:T(8,128)(2,1)} custom-call(bf16[512,1024]{1,0:T(8,128)(2,1)} %q_ref.5, bf16[8,2,512,128]{3,2,1,0:T(8,128)(2,1)} %all-to-all-done.1.kv, bf16[512,256]{1,0:T(8,128)(2,1)} %sk_ref.5, bf16[512,256]{1,0:T(8,128)(2,1)} %sv_ref.5), custom_call_target="tpu_custom_call" | custom-call | flops 4831838208 | bytes 2359296 | tf_op jit(solution)/shard_map/attend/pallas_call | solution.py:85
  135.0 30.4 %collective-permute-start.7 = (bf16[512,512]{1,0:T(8,128)(2,1)}, bf16[512,512]{1,0:T(8,128)(2,1)S(1)}, u32[]{:S(2)}, u32[]{:S(2)}) collective-permute-start(bf16[512,512]{1,0:T(8,128)(2,1)} %collective-permute-done.4.refs_4_.refs_2_), channel_id=1, source_target_pairs={{0,1},{1,2},{2,3},{3,0},{4,5},{5,6},{6,7},{7,4},{8,9},{9,10},{10,1... | collective-permute-start | bytes 1572872 | tf_op jit(solution)/shard_map/ppermute | solution.py:450
  168.5 20.2 %collective-permute-done.2.refs_43_ = bf16[2,512,256]{2,1,0:T(8,128)(2,1)S(1)} collective-permute-done((bf16[2,512,256]{2,1,0:T(8,128)(2,1)S(1)}, bf16[2,512,256]{2,1,0:T(8,128)(2,1)S(1)}, u32[]{:S(2)}, u32[]{:S(2)}) %collective-permute-start.2) | collective-permute-done | bytes 524320 | tf_op jit(solution)/shard_map/ppermute | solution.py:450
  188.7 10.0 %collective-permute-start.10 = (bf16[512,512]{1,0:T(8,128)(2,1)S(1)}, bf16[512,512]{1,0:T(8,128)(2,1)S(1)}, u32[]{:S(2)}, u32[]{:S(2)}) collective-permute-start(bf16[512,512]{1,0:T(8,128)(2,1)S(1)} %collective-permute-done.7.refs_7_.refs_2_), channel_id=1, source_target_pairs={{0,1},{1,2},{2,3},{3,0},{4,5},{5,6},{6,7},{7,4},{8,9},{9,10},{10,1... | collective-permute-start | bytes 1572872 | tf_op jit(solution)/shard_map/ppermute | solution.py:450
  202.3 7.1 %collective-permute-done.10.refs_10_.refs_1_ = bf16[512,512]{1,0:T(8,128)(2,1)S(1)} collective-permute-done((bf16[512,512]{1,0:T(8,128)(2,1)S(1)}, bf16[512,512]{1,0:T(8,128)(2,1)S(1)}, u32[]{:S(2)}, u32[]{:S(2)}) %collective-permute-start.10) | collective-permute-done | bytes 524320 | tf_op jit(solution)/shard_map/ppermute | solution.py:450
  218.5 6.5 %collective-permute-done.28.refs_29_ = bf16[256,1024]{1,0:T(8,128)(2,1)S(1)} collective-permute-done((bf16[256,1024]{1,0:T(8,128)(2,1)S(1)}, bf16[256,1024]{1,0:T(8,128)(2,1)S(1)}, u32[]{:S(2)}, u32[]{:S(2)}) %collective-permute-start.28) | collective-permute-done | bytes 524320 | tf_op jit(solution)/shard_map/ppermute | solution.py:435
  238.1 13.9 %attend.5.refs_3_ = bf16[512,256]{1,0:T(8,128)(2,1)} custom-call(bf16[512,1024]{1,0:T(8,128)(2,1)} %q_ref.5, bf16[8,2,512,128]{3,2,1,0:T(8,128)(2,1)} %copy-done.1, bf16[512,256]{1,0:T(8,128)(2,1)} %sk_ref.5, bf16[512,256]{1,0:T(8,128)(2,1)} %sv_ref.5), custom_call_target="tpu_custom_call" | custom-call | flops 2415919104 | bytes 2359296 | tf_op jit(solution)/shard_map/attend/pallas_call | solution.py:85
  252.0 14.0 %attend.4.refs_2_ = bf16[512,256]{1,0:T(8,128)(2,1)} custom-call(bf16[512,1024]{1,0:T(8,128)(2,1)} %q_ref.5, bf16[8,2,512,128]{3,2,1,0:T(8,128)(2,1)} %copy-done.1, bf16[512,256]{1,0:T(8,128)(2,1)} %sk_ref.5, bf16[512,256]{1,0:T(8,128)(2,1)} %sv_ref.5), custom_call_target="tpu_custom_call" | custom-call | flops 2415919104 | bytes 2359296 | tf_op jit(solution)/shard_map/attend/pallas_call | solution.py:85
  266.1 12.9 %collective-permute-start.5 = (bf16[512,256]{1,0:T(8,128)(2,1)}, bf16[512,256]{1,0:T(8,128)(2,1)S(1)}, u32[]{:S(2)}, u32[]{:S(2)}) collective-permute-start(bf16[512,256]{1,0:T(8,128)(2,1)} %attend.4.refs_2_), channel_id=1, source_target_pairs={{0,1},{1,2},{2,3},{3,0},{4,5},{5,6},{6,7},{7,4},{8,9},{9,10},{10,1... | collective-permute-start | bytes 786440 | tf_op jit(solution)/shard_map/ppermute | solution.py:450
  291.5 13.0 %collective-permute-done.8.refs_8_.refs_3_ = bf16[512,256]{1,0:T(8,128)(2,1)S(1)} collective-permute-done((bf16[512,256]{1,0:T(8,128)(2,1)}, bf16[512,256]{1,0:T(8,128)(2,1)S(1)}, u32[]{:S(2)}, u32[]{:S(2)}) %collective-permute-start.8) | collective-permute-done | bytes 262176 | tf_op jit(solution)/shard_map/ppermute | solution.py:450
  316.4 20.3 %project.1 = (bf16[2,512,256]{2,1,0:T(8,128)(2,1)}, bf16[2,512,256]{2,1,0:T(8,128)(2,1)}, bf16[2,512,256]{2,1,0:T(8,128)(2,1)}, bf16[2,512,256]{2,1,0:T(8,128)(2...) custom-call(s32[2]{0:T(128)} %pad_add_fusion.refs_0_, ...), custom_call_target="tpu_custom_call" | custom-call | flops 8589934592 | bytes 16777216 | tf_op jit(solution)/shard_map/project/pallas_call | solution.py:254
  339.4 12.3 %collective-permute-start.48 = (f32[4,512]{1,0:T(4,128)S(1)}, f32[4,512]{1,0:T(4,128)S(1)}, u32[]{:S(2)}, u32[]{:S(2)}) collective-permute-start(f32[4,512]{1,0:T(4,128)S(1)} %maximum_add_fusion), channel_id=1, source_target_pairs={{0,1},{1,0},{2,3},{3,2},{4,5},{5,4},{6,7},{7,6},{8,9},{9,8},{10,11... | collective-permute-start | bytes 24584 | tf_op jit(solution)/shard_map/ppermute | solution.py:562
  376.4 6.0 %gradient.3 = (bf16[2,256,1024]{2,1,0:T(8,128)(2,1)}, bf16[2,256,1024]{2,1,0:T(8,128)(2,1)}) custom-call(bf16[4,256,1024]{2,1,0:T(8,128)(2,1)} %subtract_convert_fusion.refs_0_, bf16[512,512]{1,0:T(8,128)(2,1)} %attend.3.refs_1_, bf16[512,256]{1,0:T(8,128)(2,1)} %attend.4.refs_2_, bf16[512,256]{1,0:T(8,128)(2,1)} %attend.5.refs_3_, ...), custom_call_target="tpu_custom_call" | custom-call | flops 2147483648 | bytes 8388608 | tf_op jit(solution)/shard_map/gradient/pallas_call | solution.py:314
  383.1 13.8 %collective-permute-done.56 = f32[2,1024]{1,0:T(2,128)S(1)} collective-permute-done((f32[2,1024]{1,0:T(2,128)S(1)}, f32[2,1024]{1,0:T(2,128)S(1)}, u32[]{:S(2)}, u32[]{:S(2)}) %collective-permute-start.56) | collective-permute-done | bytes 8224 | tf_op jit(solution)/shard_map/ppermute | solution.py:435
  407.7 6.2 %joint.2 = (bf16[1,256,1024]{2,1,0:T(8,128)(2,1)}, bf16[1,256,1024]{2,1,0:T(8,128)(2,1)}) custom-call(bf16[4,256,1024]{2,1,0:T(8,128)(2,1)} %subtract_convert_fusion.refs_0_, bf16[2,256,1024]{2,1,0:T(8,128)(2,1)} %subtract_convert_fusion.2.refs_1_, bf16[512,512]{1,0:T(8,128)(2,1)} %copy-done.23, bf16[512,256]{1,0:T(8,128)(2,1)} %copy-done.44, ...), custom_call_target="tpu_custom_call" | custom-call | flops 2147483648 | bytes 8388608 | tf_op jit(solution)/shard_map/joint/pallas_call | solution.py:345
  413.9 18.9 %collective-permute-done.70.refs_10_ = bf16[512,256]{1,0:T(8,128)(2,1)} collective-permute-done((bf16[512,256]{1,0:T(8,128)(2,1)S(1)}, bf16[512,256]{1,0:T(8,128)(2,1)}, u32[]{:S(2)}, u32[]{:S(2)}) %collective-permute-start.70) | collective-permute-done | bytes 262176 | tf_op jit(solution)/shard_map/ppermute | solution.py:435
  442.7 6.3 %joint.3 = (bf16[1,256,1024]{2,1,0:T(8,128)(2,1)}, bf16[1,256,1024]{2,1,0:T(8,128)(2,1)}) custom-call(bf16[4,256,1024]{2,1,0:T(8,128)(2,1)} %subtract_convert_fusion.refs_0_, bf16[2,256,1024]{2,1,0:T(8,128)(2,1)} %subtract_convert_fusion.1.refs_1_, bf16[512,512]{1,0:T(8,128)(2,1)} %collective-permute-done.4.refs_4_.refs_2_, bf16[512,256]{1,0:T(8,128)(2,1)} %copy-done.39, ...), custom_call_target="tpu_custom_call" | custom-call | flops 2147483648 | bytes 8388608 | tf_op jit(solution)/shard_map/joint/pallas_call | solution.py:345
  454.7 7.9 %collective-permute-done.64 = bf16[1,256,1024]{2,1,0:T(8,128)(2,1)S(1)} collective-permute-done((bf16[1,256,1024]{2,1,0:T(8,128)(2,1)}, bf16[1,256,1024]{2,1,0:T(8,128)(2,1)S(1)}, u32[]{:S(2)}, u32[]{:S(2)}) %collective-permute-start.64) | collective-permute-done | bytes 524320 | tf_op jit(solution)/shard_map/ppermute | solution.py:435
  465.3 11.1 %collective-permute-done.41.refs_3_ = bf16[2,512,256]{2,1,0:T(8,128)(2,1)} collective-permute-done((bf16[2,512,256]{2,1,0:T(8,128)(2,1)}, bf16[2,512,256]{2,1,0:T(8,128)(2,1)}, u32[]{:S(2)}, u32[]{:S(2)}) %collective-permute-start.41) | collective-permute-done | bytes 524320 | tf_op jit(solution)/shard_map/ppermute | solution.py:450
  481.8 10.7 %collective-permute-start.65 = (bf16[256,1024]{1,0:T(8,128)(2,1)}, bf16[256,1024]{1,0:T(8,128)(2,1)S(1)}, u32[]{:S(2)}, u32[]{:S(2)}) collective-permute-start(bf16[256,1024]{1,0:T(8,128)(2,1)} %fusion.2), channel_id=1, source_target_pairs={{0,2},{1,3},{2,0},{3,1},{4,6},{5,7},{6,4},{7,5},{8,10},{9,11},{10,... | collective-permute-start | bytes 1572872 | tf_op jit(solution)/shard_map/ppermute | solution.py:450
  504.5 12.2 %collective-permute-done.65.refs_2_ = bf16[256,1024]{1,0:T(8,128)(2,1)S(1)} collective-permute-done((bf16[256,1024]{1,0:T(8,128)(2,1)}, bf16[256,1024]{1,0:T(8,128)(2,1)S(1)}, u32[]{:S(2)}, u32[]{:S(2)}) %collective-permute-start.65) | collective-permute-done | bytes 524320 | tf_op jit(solution)/shard_map/ppermute | solution.py:450
  520.7 9.7 %collective-permute-done.53.refs_1_ = bf16[256,1024]{1,0:T(8,128)(2,1)} collective-permute-done((bf16[256,1024]{1,0:T(8,128)(2,1)}, bf16[256,1024]{1,0:T(8,128)(2,1)}, u32[]{:S(2)}, u32[]{:S(2)}) %collective-permute-start.53) | collective-permute-done | bytes 524320 | tf_op jit(solution)/shard_map/ppermute | solution.py:450
  (327 shorter events, 185.6 us)
Async XLA Ops:
  70.2 50.5 %all-to-all-start.2 = ((bf16[8,2,512,128]{3,2,1,0:T(8,128)(2,1)}), bf16[8,2,512,128]{3,2,1,0:T(8,128)(2,1)}, u32[]{:S(2)}, u32[]{:S(2)}) async-start(bf16[8,2,512,128]{3,2,1,0:T(8,128)(2,1)} %pad_maximum_fusion), calls=%async_computation.2 | async-start | bytes 4194304 | tf_op jit(solution)/shard_map/all_to_all | solution.py:490
  79.4 36.7 %collective-permute-start = (bf16[512,4,256]{2,0,1:T(8,128)(2,1)}, bf16[512,4,256]{2,0,1:T(8,128)(2,1)}, u32[]{:S(2)}, u32[]{:S(2)}) collective-permute-start(bf16[512,4,256]{2,0,1:T(8,128)(2,1)} %bitcast.60), channel_id=1, source_target_pairs={{0,4},{4,0},{8,12},{12,8},{16,20},{20,16},{24,28},{28,24},{1,5},{5... | collective-permute-start | bytes 3145736 | tf_op jit(solution)/shard_map/ppermute | solution.py:435
  82.6 48.6 %collective-permute-start.25 = (bf16[256,1024]{1,0:T(8,128)(2,1)}, bf16[256,1024]{1,0:T(8,128)(2,1)}, u32[]{:S(2)}, u32[]{:S(2)}) collective-permute-start(bf16[256,1024]{1,0:T(8,128)(2,1)} %get-tuple-element.85), channel_id=1, source_target_pairs={{0,1},{1,2},{2,3},{3,0},{4,5},{5,6},{6,7},{7,4},{8,9},{9,10},{10,1... | collective-permute-start | bytes 1572872 | tf_op jit(solution)/shard_map/ppermute | solution.py:450
  84.2 50.6 %collective-permute-start.26 = (bf16[256,1024]{1,0:T(8,128)(2,1)}, bf16[256,1024]{1,0:T(8,128)(2,1)}, u32[]{:S(2)}, u32[]{:S(2)}) collective-permute-start(bf16[256,1024]{1,0:T(8,128)(2,1)} %get-tuple-element.87), channel_id=1, source_target_pairs={{0,2},{1,3},{2,0},{3,1},{4,6},{5,7},{6,4},{7,5},{8,10},{9,11},{10,... | collective-permute-start | bytes 1572872 | tf_op jit(solution)/shard_map/ppermute | solution.py:450
  86.8 78.6 %collective-permute-start.27 = (bf16[256,1024]{1,0:T(8,128)(2,1)}, bf16[256,1024]{1,0:T(8,128)(2,1)}, u32[]{:S(2)}, u32[]{:S(2)}) collective-permute-start(bf16[256,1024]{1,0:T(8,128)(2,1)} %get-tuple-element.84), channel_id=1, source_target_pairs={{0,3},{1,0},{2,1},{3,2},{4,7},{5,4},{6,5},{7,6},{8,11},{9,8},{10,9... | collective-permute-start | bytes 1572872 | tf_op jit(solution)/shard_map/ppermute | solution.py:450
  119.0 48.0 %collective-permute-start.1 = (bf16[2,512,256]{2,1,0:T(8,128)(2,1)}, bf16[2,512,256]{2,1,0:T(8,128)(2,1)}, u32[]{:S(2)}, u32[]{:S(2)}) collective-permute-start(bf16[2,512,256]{2,1,0:T(8,128)(2,1)} %pad_maximum_fusion.3), channel_id=1, source_target_pairs={{0,1},{1,2},{2,3},{3,0},{4,5},{5,6},{6,7},{7,4},{8,9},{9,10},{10,1... | collective-permute-start | bytes 1572872 | tf_op jit(solution)/shard_map/ppermute | solution.py:450
  125.1 106.4 %all-to-all-start.3 = ((bf16[8,2,512,128]{3,2,1,0:T(8,128)(2,1)}), bf16[8,2,512,128]{3,2,1,0:T(8,128)(2,1)S(1)}, u32[]{:S(2)}, u32[]{:S(2)}) async-start(bf16[8,2,512,128]{3,2,1,0:T(8,128)(2,1)} %get-tuple-element.49), calls=%async_computation.3 | async-start | bytes 4194304 | tf_op jit(solution)/shard_map/all_to_all | solution.py:494
  131.2 57.5 %collective-permute-start.2 = (bf16[2,512,256]{2,1,0:T(8,128)(2,1)S(1)}, bf16[2,512,256]{2,1,0:T(8,128)(2,1)S(1)}, u32[]{:S(2)}, u32[]{:S(2)}) collective-permute-start(bf16[2,512,256]{2,1,0:T(8,128)(2,1)S(1)} %pad_maximum_fusion.4), channel_id=1, source_target_pairs={{0,2},{1,3},{2,0},{3,1},{4,6},{5,7},{6,4},{7,5},{8,10},{9,11},{10,... | collective-permute-start | bytes 1572872 | tf_op jit(solution)/shard_map/ppermute | solution.py:450
  134.8 64.0 %collective-permute-start.3 = (bf16[2,512,256]{2,1,0:T(8,128)(2,1)S(1)}, bf16[2,512,256]{2,1,0:T(8,128)(2,1)S(1)}, u32[]{:S(2)}, u32[]{:S(2)}) collective-permute-start(bf16[2,512,256]{2,1,0:T(8,128)(2,1)S(1)} %pad_maximum_fusion.5), channel_id=1, source_target_pairs={{0,3},{1,0},{2,1},{3,2},{4,7},{5,4},{6,5},{7,6},{8,11},{9,8},{10,9... | collective-permute-start | bytes 1572872 | tf_op jit(solution)/shard_map/ppermute | solution.py:450
  135.0 53.7 %collective-permute-start.7 = (bf16[512,512]{1,0:T(8,128)(2,1)}, bf16[512,512]{1,0:T(8,128)(2,1)S(1)}, u32[]{:S(2)}, u32[]{:S(2)}) collective-permute-start(bf16[512,512]{1,0:T(8,128)(2,1)} %collective-permute-done.4.refs_4_.refs_2_), channel_id=1, source_target_pairs={{0,1},{1,2},{2,3},{3,0},{4,5},{5,6},{6,7},{7,4},{8,9},{9,10},{10,1... | collective-permute-start | bytes 1572872 | tf_op jit(solution)/shard_map/ppermute | solution.py:450
  167.0 33.8 %collective-permute-start.30 = (bf16[256,1024]{1,0:T(8,128)(2,1)}, bf16[256,1024]{1,0:T(8,128)(2,1)S(1)}, u32[]{:S(2)}, u32[]{:S(2)}) collective-permute-start(bf16[256,1024]{1,0:T(8,128)(2,1)} %collective-permute-done.26.refs_27_), channel_id=1, source_target_pairs={{0,8},{4,12},{8,0},{12,4},{16,24},{20,28},{24,16},{28,20},{1,9},{5... | collective-permute-start | bytes 1572872 | tf_op jit(solution)/shard_map/ppermute | solution.py:435
  217.1 49.0 %collective-permute-start.29 = (bf16[256,1024]{1,0:T(8,128)(2,1)}, bf16[256,1024]{1,0:T(8,128)(2,1)}, u32[]{:S(2)}, u32[]{:S(2)}) collective-permute-start(bf16[256,1024]{1,0:T(8,128)(2,1)} %collective-permute-done.25.refs_26_), channel_id=1, source_target_pairs={{0,8},{4,12},{8,0},{12,4},{16,24},{20,28},{24,16},{28,20},{1,9},{5... | collective-permute-start | bytes 1572872 | tf_op jit(solution)/shard_map/ppermute | solution.py:435
  217.9 61.2 %collective-permute-start.35 = (bf16[256,1024]{1,0:T(8,128)(2,1)}, bf16[256,1024]{1,0:T(8,128)(2,1)}, u32[]{:S(2)}, u32[]{:S(2)}) collective-permute-start(bf16[256,1024]{1,0:T(8,128)(2,1)} %collective-permute-done.27.refs_28_), channel_id=1, source_target_pairs={{0,16},{4,20},{8,24},{12,28},{16,0},{20,4},{24,8},{28,12},{1,17},{... | collective-permute-start | bytes 1572872 | tf_op jit(solution)/shard_map/ppermute | solution.py:435
  225.0 54.1 %collective-permute-start.34 = (bf16[256,1024]{1,0:T(8,128)(2,1)}, bf16[256,1024]{1,0:T(8,128)(2,1)}, u32[]{:S(2)}, u32[]{:S(2)}) collective-permute-start(bf16[256,1024]{1,0:T(8,128)(2,1)} %collective-permute-done.26.refs_27_), channel_id=1, source_target_pairs={{0,16},{4,20},{8,24},{12,28},{16,0},{20,4},{24,8},{28,12},{1,17},{... | collective-permute-start | bytes 1572872 | tf_op jit(solution)/shard_map/ppermute | solution.py:435
  228.8 50.3 %collective-permute-start.37 = (bf16[256,1024]{1,0:T(8,128)(2,1)}, bf16[256,1024]{1,0:T(8,128)(2,1)}, u32[]{:S(2)}, u32[]{:S(2)}) collective-permute-start(bf16[256,1024]{1,0:T(8,128)(2,1)} %collective-permute-done.33.refs_34_), channel_id=1, source_target_pairs={{0,8},{4,12},{8,0},{12,4},{16,24},{20,28},{24,16},{28,20},{1,9},{5... | collective-permute-start | bytes 1572872 | tf_op jit(solution)/shard_map/ppermute | solution.py:435
  236.3 45.7 %collective-permute-start.39 = (bf16[256,1024]{1,0:T(8,128)(2,1)}, bf16[256,1024]{1,0:T(8,128)(2,1)S(1)}, u32[]{:S(2)}, u32[]{:S(2)}) collective-permute-start(bf16[256,1024]{1,0:T(8,128)(2,1)} %collective-permute-done.31.refs_32_), channel_id=1, source_target_pairs={{0,16},{4,20},{8,24},{12,28},{16,0},{20,4},{24,8},{28,12},{1,17},{... | collective-permute-start | bytes 1572872 | tf_op jit(solution)/shard_map/ppermute | solution.py:435
  315.4 46.4 %collective-permute-start.50 = (f32[512]{0:T(512)S(1)}, f32[512]{0:T(512)S(1)}, u32[]{:S(2)}, u32[]{:S(2)}) collective-permute-start(f32[512]{0:T(512)S(1)} %select_reduce_fusion), channel_id=1, source_target_pairs={{0,4},{4,0},{8,12},{12,8},{16,20},{20,16},{24,28},{28,24},{1,5},{5... | collective-permute-start | bytes 6152 | tf_op jit(solution)/shard_map/ppermute | solution.py:435
  361.8 43.5 %collective-permute-start.57 = (bf16[2,256,1024]{2,1,0:T(8,128)(2,1)}, bf16[2,256,1024]{2,1,0:T(8,128)(2,1)S(1)}, u32[]{:S(2)}, u32[]{:S(2)}) collective-permute-start(bf16[2,256,1024]{2,1,0:T(8,128)(2,1)} %get-tuple-element.73), channel_id=1, source_target_pairs={{0,16},{4,20},{8,24},{12,28},{16,0},{20,4},{24,8},{28,12},{1,17},{... | collective-permute-start | bytes 3145736 | tf_op jit(solution)/shard_map/ppermute | solution.py:435
  374.0 58.8 %collective-permute-start.67 = (bf16[2,256,1024]{2,1,0:T(8,128)(2,1)}, bf16[2,256,1024]{2,1,0:T(8,128)(2,1)S(1)}, u32[]{:S(2)}, u32[]{:S(2)}) collective-permute-start(bf16[2,256,1024]{2,1,0:T(8,128)(2,1)} %get-tuple-element.76), channel_id=1, source_target_pairs={{0,8},{4,12},{8,0},{12,4},{16,24},{20,28},{24,16},{28,20},{1,9},{5... | collective-permute-start | bytes 3145736 | tf_op jit(solution)/shard_map/ppermute | solution.py:435
  403.1 45.9 %collective-permute-start.51 = (bf16[2,256,1024]{2,1,0:T(8,128)(2,1)}, bf16[2,256,1024]{2,1,0:T(8,128)(2,1)}, u32[]{:S(2)}, u32[]{:S(2)}) collective-permute-start(bf16[2,256,1024]{2,1,0:T(8,128)(2,1)} %get-tuple-element.70), channel_id=1, source_target_pairs={{0,8},{4,12},{8,0},{12,4},{16,24},{20,28},{24,16},{28,20},{1,9},{5... | collective-permute-start | bytes 3145736 | tf_op jit(solution)/shard_map/ppermute | solution.py:435
  405.3 46.8 %collective-permute-start.54 = (bf16[2,256,1024]{2,1,0:T(8,128)(2,1)}, bf16[2,256,1024]{2,1,0:T(8,128)(2,1)S(1)}, u32[]{:S(2)}, u32[]{:S(2)}) collective-permute-start(bf16[2,256,1024]{2,1,0:T(8,128)(2,1)} %get-tuple-element.72), channel_id=1, source_target_pairs={{0,16},{4,20},{8,24},{12,28},{16,0},{20,4},{24,8},{28,12},{1,17},{... | collective-permute-start | bytes 3145736 | tf_op jit(solution)/shard_map/ppermute | solution.py:435
  438.6 37.9 %collective-permute-start.41 = (bf16[2,512,256]{2,1,0:T(8,128)(2,1)}, bf16[2,512,256]{2,1,0:T(8,128)(2,1)}, u32[]{:S(2)}, u32[]{:S(2)}) collective-permute-start(bf16[2,512,256]{2,1,0:T(8,128)(2,1)} %get-tuple-element.65), channel_id=1, source_target_pairs={{0,2},{1,3},{2,0},{3,1},{4,6},{5,7},{6,4},{7,5},{8,10},{9,11},{10,... | collective-permute-start | bytes 1572872 | tf_op jit(solution)/shard_map/ppermute | solution.py:450
  442.7 33.8 %collective-permute-start.42 = (bf16[2,512,256]{2,1,0:T(8,128)(2,1)}, bf16[2,512,256]{2,1,0:T(8,128)(2,1)}, u32[]{:S(2)}, u32[]{:S(2)}) collective-permute-start(bf16[2,512,256]{2,1,0:T(8,128)(2,1)} %get-tuple-element.66), channel_id=1, source_target_pairs={{0,3},{1,0},{2,1},{3,2},{4,7},{5,4},{6,5},{7,6},{8,11},{9,8},{10,9... | collective-permute-start | bytes 1572872 | tf_op jit(solution)/shard_map/ppermute | solution.py:450
  481.8 34.9 %collective-permute-start.65 = (bf16[256,1024]{1,0:T(8,128)(2,1)}, bf16[256,1024]{1,0:T(8,128)(2,1)S(1)}, u32[]{:S(2)}, u32[]{:S(2)}) collective-permute-start(bf16[256,1024]{1,0:T(8,128)(2,1)} %fusion.2), channel_id=1, source_target_pairs={{0,2},{1,3},{2,0},{3,1},{4,6},{5,7},{6,4},{7,5},{8,10},{9,11},{10,... | collective-permute-start | bytes 1572872 | tf_op jit(solution)/shard_map/ppermute | solution.py:450
  (115 other events, 2019.8 us)

commit v5 on v4

--- a/solution.py
+++ b/solution.py
@@ -77,9 +77,8 @@
     o_ref[...] = (mixed[:, :HD] / mixed[:, HD:]).astype(BF)
 
 
-def attention(queries, kv, suffix_k, suffix_v, head, group, first, count):
+def attention(queries, kv, suffix_k, suffix_v, head, group, first, count, tile):
     rows = queries.shape[0]
-    tile = TILE
     blocks, _, block_len, _ = kv.shape
     span = blocks * block_len + rows
     return pl.pallas_call(
@@ -497,7 +496,8 @@
         for step, first in enumerate(range(0, group, count)):
             if last and first + count == group:
                 kv, *res = lax.optimization_barrier((kv, *res))
-            attn.append(attention(queries, kv, suffix_k, suffix_v, head, group, first, count))
+            tile = 2 * TILE if last and first + count == group else TILE
+            attn.append(attention(queries, kv, suffix_k, suffix_v, head, group, first, count, tile))
     cache_k, cache_v = caches
 
     half = n_head // 2
@@ -508,9 +508,9 @@
         low, high = e & -e, 1 << (e.bit_length() - 1)
         got = [None] * n_head
         turn = [*range(half, n_head), *range(half)] if low == 1 else [*range(n_head)]
-        for k, t in enumerate(turn):
+        for t in turn:
             if low == high:
-                got[t] = chip_send((w_late if k else w_own)[t], e)
+                got[t] = chip_send(w_late[t], e)
             else:
                 bit = low if t < half else high
                 got[t] = chip_send(weights[e ^ bit][t], bit)

time: 542 us -> 578 us (1.066)
  waiting for transfers between devices: 173 us -> 216 us
    ppermute x21, waiting for transfers between devices: 85 us -> 108 us  [plane_send(): return lax.ppermute(x, HEAD, shift_perm(n_head, step))]
    ppermute x53, waiting for transfers between devices: 62.3 us -> 81.7 us  [seq_send(): return lax.ppermute(x, SEQ, xor_perm(n_seq, mask))]
  transfers between devices with their start and end apart: 79 -> 79, of which waited for: 21 -> 21; matrix products, arithmetic and copies ran while one was open for 8% -> 7% of each run, Pallas kernels for 20% -> 19%
where the time goes in v5:
time: 578 us; the launch traced here: 569 us
  waiting for transfers between devices  216 us (37%)
  starting transfers between devices  157 us (27%)
  Pallas kernels  115 us (20%)
  blocking collectives  31.7 us (5%)
  local copies, waits for them, and re-layouts  24 us (4%)
  other arithmetic  23.9 us (4%)
    ppermute x21, waiting for transfers between devices, plane_send(): return lax.ppermute(x, HEAD, shift_perm(n_head, step))  108 us
    ppermute x21, starting transfers between devices, plane_send(): return lax.ppermute(x, HEAD, shift_perm(n_head, step))  88.6 us
    ppermute x53, waiting for transfers between devices, seq_send(): return lax.ppermute(x, SEQ, xor_perm(n_seq, mask))  81.7 us
    pallas_call x3, Pallas kernels, attention(): pl.pallas_call(attention_kernel, out_shape=jax.ShapeDtypeStruct((rows, co...  52.2 us
    ppermute x53, starting transfers between devices, seq_send(): return lax.ppermute(x, SEQ, xor_perm(n_seq, mask))  38.9 us
    all_to_all x1, blocking collectives, local(): came = lax.all_to_all(both, SEQ, split_axis=0, concat_axis=0, tiled=True)  31.7 us
    all_to_all x2, waiting for transfers between devices, local(): kv = lax.all_to_all(chosen, SEQ, split_axis=0, concat_axis=0, tiled=True)  25.1 us
    pallas_call x1, Pallas kernels, project(): pl.pallas_call(functools.partial(project_kernel, planes, widths, chips, s...  20.3 us
  transfers between devices with their start and end apart: 79, of which 21 were waited for; matrix products, arithmetic and copies ran while one was open for 7% of the time, Pallas kernels for 19%

profile of v5, /device:TPU:0, one launch (start us, length us, event | category | flops | bytes accessed | tf_op | source)
XLA Modules:
  0.0 568.7 jit_solution(14512572036782548506)
XLA Ops:
  3.2 31.7 %all_to_all.20.refs_1_ = bf16[8,2,512,128]{3,2,1,0:T(8,128)(2,1)} all-to-all(bf16[8,2,512,128]{3,2,1,0:T(8,128)(2,1)S(1)} %pad_maximum_fusion.1), channel_id=1, replica_groups=mesh['seq'=8,'head'=4] {'seq'}, dimensions={0} | all-to-all | bytes 4194304 | tf_op jit(solution)/shard_map/all_to_all | solution.py:489
  45.1 25.1 %all-to-all-done.1.kv = bf16[8,2,512,128]{3,2,1,0:T(8,128)(2,1)} async-done(((bf16[8,2,512,128]{3,2,1,0:T(8,128)(2,1)}), bf16[8,2,512,128]{3,2,1,0:T(8,128)(2,1)}, u32[]{:S(2)}, u32[]{:S(2)}) %all-to-all-start.1) | async-done | bytes 2097184 | tf_op jit(solution)/shard_map/all_to_all | solution.py:493
  79.8 25.0 %attend.3.refs_1_ = bf16[512,512]{1,0:T(8,128)(2,1)} custom-call(bf16[512,1024]{1,0:T(8,128)(2,1)} %q_ref.5, bf16[8,2,512,128]{3,2,1,0:T(8,128)(2,1)} %all-to-all-done.1.kv, bf16[512,256]{1,0:T(8,128)(2,1)} %sk_ref.5, bf16[512,256]{1,0:T(8,128)(2,1)} %sv_ref.5), custom_call_target="tpu_custom_call" | custom-call | flops 4831838208 | bytes 2359296 | tf_op jit(solution)/shard_map/attend/pallas_call | solution.py:84
  138.7 17.6 %collective-permute-start.2 = (bf16[2,512,256]{2,1,0:T(8,128)(2,1)S(1)}, bf16[2,512,256]{2,1,0:T(8,128)(2,1)S(1)}, u32[]{:S(2)}, u32[]{:S(2)}) collective-permute-start(bf16[2,512,256]{2,1,0:T(8,128)(2,1)S(1)} %pad_maximum_fusion.4), channel_id=1, source_target_pairs={{0,2},{1,3},{2,0},{3,1},{4,6},{5,7},{6,4},{7,5},{8,10},{9,11},{10,... | collective-permute-start | bytes 1572872 | tf_op jit(solution)/shard_map/ppermute | solution.py:449
  156.3 10.6 %collective-permute-done.7.refs_7_.refs_2_ = bf16[512,512]{1,0:T(8,128)(2,1)} collective-permute-done((bf16[512,512]{1,0:T(8,128)(2,1)}, bf16[512,512]{1,0:T(8,128)(2,1)}, u32[]{:S(2)}, u32[]{:S(2)}) %collective-permute-start.7) | collective-permute-done | bytes 524320 | tf_op jit(solution)/shard_map/ppermute | solution.py:449
  166.8 20.7 %collective-permute-start.10 = (bf16[512,512]{1,0:T(8,128)(2,1)}, bf16[512,512]{1,0:T(8,128)(2,1)S(1)}, u32[]{:S(2)}, u32[]{:S(2)}) collective-permute-start(bf16[512,512]{1,0:T(8,128)(2,1)} %collective-permute-done.7.refs_7_.refs_2_), channel_id=1, source_target_pairs={{0,1},{1,2},{2,3},{3,0},{4,5},{5,6},{6,7},{7,4},{8,9},{9,10},{10,1... | collective-permute-start | bytes 1572872 | tf_op jit(solution)/shard_map/ppermute | solution.py:449
  188.2 33.9 %collective-permute-done.2.refs_43_ = bf16[2,512,256]{2,1,0:T(8,128)(2,1)S(1)} collective-permute-done((bf16[2,512,256]{2,1,0:T(8,128)(2,1)S(1)}, bf16[2,512,256]{2,1,0:T(8,128)(2,1)S(1)}, u32[]{:S(2)}, u32[]{:S(2)}) %collective-permute-start.2) | collective-permute-done | bytes 524320 | tf_op jit(solution)/shard_map/ppermute | solution.py:449
  229.0 8.8 %collective-permute-done.28.refs_29_ = bf16[256,1024]{1,0:T(8,128)(2,1)S(1)} collective-permute-done((bf16[256,1024]{1,0:T(8,128)(2,1)S(1)}, bf16[256,1024]{1,0:T(8,128)(2,1)S(1)}, u32[]{:S(2)}, u32[]{:S(2)}) %collective-permute-start.28) | collective-permute-done | bytes 524320 | tf_op jit(solution)/shard_map/ppermute | solution.py:434
  239.7 9.4 %collective-permute-done.29.refs_30_ = bf16[256,1024]{1,0:T(8,128)(2,1)S(1)} collective-permute-done((bf16[256,1024]{1,0:T(8,128)(2,1)}, bf16[256,1024]{1,0:T(8,128)(2,1)S(1)}, u32[]{:S(2)}, u32[]{:S(2)}) %collective-permute-start.29) | collective-permute-done | bytes 524320 | tf_op jit(solution)/shard_map/ppermute | solution.py:434
  251.0 9.4 %collective-permute-done.30.refs_31_ = bf16[256,1024]{1,0:T(8,128)(2,1)} collective-permute-done((bf16[256,1024]{1,0:T(8,128)(2,1)}, bf16[256,1024]{1,0:T(8,128)(2,1)}, u32[]{:S(2)}, u32[]{:S(2)}) %collective-permute-start.30) | collective-permute-done | bytes 524320 | tf_op jit(solution)/shard_map/ppermute | solution.py:434
  264.3 7.2 %collective-permute-done.31.refs_32_ = bf16[256,1024]{1,0:T(8,128)(2,1)S(1)} collective-permute-done((bf16[256,1024]{1,0:T(8,128)(2,1)}, bf16[256,1024]{1,0:T(8,128)(2,1)S(1)}, u32[]{:S(2)}, u32[]{:S(2)}) %collective-permute-start.31) | collective-permute-done | bytes 524320 | tf_op jit(solution)/shard_map/ppermute | solution.py:434
  275.6 13.1 %attend.5.refs_3_ = bf16[512,256]{1,0:T(8,128)(2,1)} custom-call(bf16[512,1024]{1,0:T(8,128)(2,1)} %q_ref.5, bf16[8,2,512,128]{3,2,1,0:T(8,128)(2,1)} %copy-done.1, bf16[512,256]{1,0:T(8,128)(2,1)} %sk_ref.5, bf16[512,256]{1,0:T(8,128)(2,1)} %sv_ref.5), custom_call_target="tpu_custom_call" | custom-call | flops 2415919104 | bytes 2359296 | tf_op jit(solution)/shard_map/attend/pallas_call | solution.py:84
  288.8 14.0 %attend.4.refs_2_ = bf16[512,256]{1,0:T(8,128)(2,1)} custom-call(bf16[512,1024]{1,0:T(8,128)(2,1)} %q_ref.5, bf16[8,2,512,128]{3,2,1,0:T(8,128)(2,1)} %copy-done.1, bf16[512,256]{1,0:T(8,128)(2,1)} %sk_ref.5, bf16[512,256]{1,0:T(8,128)(2,1)} %sv_ref.5), custom_call_target="tpu_custom_call" | custom-call | flops 2415919104 | bytes 2359296 | tf_op jit(solution)/shard_map/attend/pallas_call | solution.py:84
  302.8 10.8 %collective-permute-start.5 = (bf16[512,256]{1,0:T(8,128)(2,1)}, bf16[512,256]{1,0:T(8,128)(2,1)S(1)}, u32[]{:S(2)}, u32[]{:S(2)}) collective-permute-start(bf16[512,256]{1,0:T(8,128)(2,1)} %attend.4.refs_2_), channel_id=1, source_target_pairs={{0,1},{1,2},{2,3},{3,0},{4,5},{5,6},{6,7},{7,4},{8,9},{9,10},{10,1... | collective-permute-start | bytes 786440 | tf_op jit(solution)/shard_map/ppermute | solution.py:449
  326.1 12.2 %collective-permute-done.8.refs_8_.refs_3_ = bf16[512,256]{1,0:T(8,128)(2,1)S(1)} collective-permute-done((bf16[512,256]{1,0:T(8,128)(2,1)}, bf16[512,256]{1,0:T(8,128)(2,1)S(1)}, u32[]{:S(2)}, u32[]{:S(2)}) %collective-permute-start.8) | collective-permute-done | bytes 262176 | tf_op jit(solution)/shard_map/ppermute | solution.py:449
  350.3 20.3 %project.1 = (bf16[2,512,256]{2,1,0:T(8,128)(2,1)}, bf16[2,512,256]{2,1,0:T(8,128)(2,1)}, bf16[2,512,256]{2,1,0:T(8,128)(2,1)}, bf16[2,512,256]{2,1,0:T(8,128)(2...) custom-call(s32[2]{0:T(128)} %pad_add_fusion.refs_0_, ...), custom_call_target="tpu_custom_call" | custom-call | flops 8589934592 | bytes 16777216 | tf_op jit(solution)/shard_map/project/pallas_call | solution.py:253
  373.5 13.6 %collective-permute-start.48 = (f32[4,512]{1,0:T(4,128)S(1)}, f32[4,512]{1,0:T(4,128)S(1)}, u32[]{:S(2)}, u32[]{:S(2)}) collective-permute-start(f32[4,512]{1,0:T(4,128)S(1)} %maximum_add_fusion), channel_id=1, source_target_pairs={{0,1},{1,0},{2,3},{3,2},{4,5},{5,4},{6,7},{7,6},{8,9},{9,8},{10,11... | collective-permute-start | bytes 24584 | tf_op jit(solution)/shard_map/ppermute | solution.py:562
  418.5 13.8 %collective-permute-done.56 = f32[2,1024]{1,0:T(2,128)S(1)} collective-permute-done((f32[2,1024]{1,0:T(2,128)S(1)}, f32[2,1024]{1,0:T(2,128)S(1)}, u32[]{:S(2)}, u32[]{:S(2)}) %collective-permute-start.56) | collective-permute-done | bytes 8224 | tf_op jit(solution)/shard_map/ppermute | solution.py:434
  449.3 18.8 %collective-permute-done.70.refs_10_ = bf16[512,256]{1,0:T(8,128)(2,1)} collective-permute-done((bf16[512,256]{1,0:T(8,128)(2,1)S(1)}, bf16[512,256]{1,0:T(8,128)(2,1)}, u32[]{:S(2)}, u32[]{:S(2)}) %collective-permute-start.70) | collective-permute-done | bytes 262176 | tf_op jit(solution)/shard_map/ppermute | solution.py:434
  490.3 8.6 %collective-permute-done.64 = bf16[1,256,1024]{2,1,0:T(8,128)(2,1)S(1)} collective-permute-done((bf16[1,256,1024]{2,1,0:T(8,128)(2,1)}, bf16[1,256,1024]{2,1,0:T(8,128)(2,1)S(1)}, u32[]{:S(2)}, u32[]{:S(2)}) %collective-permute-start.64) | collective-permute-done | bytes 524320 | tf_op jit(solution)/shard_map/ppermute | solution.py:434
  500.9 11.8 %collective-permute-done.41.refs_3_ = bf16[2,512,256]{2,1,0:T(8,128)(2,1)} collective-permute-done((bf16[2,512,256]{2,1,0:T(8,128)(2,1)}, bf16[2,512,256]{2,1,0:T(8,128)(2,1)}, u32[]{:S(2)}, u32[]{:S(2)}) %collective-permute-start.41) | collective-permute-done | bytes 524320 | tf_op jit(solution)/shard_map/ppermute | solution.py:449
  517.9 10.7 %collective-permute-start.65 = (bf16[256,1024]{1,0:T(8,128)(2,1)}, bf16[256,1024]{1,0:T(8,128)(2,1)S(1)}, u32[]{:S(2)}, u32[]{:S(2)}) collective-permute-start(bf16[256,1024]{1,0:T(8,128)(2,1)} %fusion.2), channel_id=1, source_target_pairs={{0,2},{1,3},{2,0},{3,1},{4,6},{5,7},{6,4},{7,5},{8,10},{9,11},{10,... | collective-permute-start | bytes 1572872 | tf_op jit(solution)/shard_map/ppermute | solution.py:449
  540.6 12.2 %collective-permute-done.65.refs_2_ = bf16[256,1024]{1,0:T(8,128)(2,1)S(1)} collective-permute-done((bf16[256,1024]{1,0:T(8,128)(2,1)}, bf16[256,1024]{1,0:T(8,128)(2,1)S(1)}, u32[]{:S(2)}, u32[]{:S(2)}) %collective-permute-start.65) | collective-permute-done | bytes 524320 | tf_op jit(solution)/shard_map/ppermute | solution.py:449
  556.7 9.7 %collective-permute-done.53.refs_1_ = bf16[256,1024]{1,0:T(8,128)(2,1)} collective-permute-done((bf16[256,1024]{1,0:T(8,128)(2,1)}, bf16[256,1024]{1,0:T(8,128)(2,1)}, u32[]{:S(2)}, u32[]{:S(2)}) %collective-permute-start.53) | collective-permute-done | bytes 524320 | tf_op jit(solution)/shard_map/ppermute | solution.py:449
  (317 shorter events, 198.0 us)
Async XLA Ops:
  70.2 58.1 %all-to-all-start.2 = ((bf16[8,2,512,128]{3,2,1,0:T(8,128)(2,1)}), bf16[8,2,512,128]{3,2,1,0:T(8,128)(2,1)}, u32[]{:S(2)}, u32[]{:S(2)}) async-start(bf16[8,2,512,128]{3,2,1,0:T(8,128)(2,1)} %pad_maximum_fusion), calls=%async_computation.2 | async-start | bytes 4194304 | tf_op jit(solution)/shard_map/all_to_all | solution.py:489
  79.4 44.8 %collective-permute-start = (bf16[512,4,256]{2,0,1:T(8,128)(2,1)}, bf16[512,4,256]{2,0,1:T(8,128)(2,1)}, u32[]{:S(2)}, u32[]{:S(2)}) collective-permute-start(bf16[512,4,256]{2,0,1:T(8,128)(2,1)} %bitcast.60), channel_id=1, source_target_pairs={{0,4},{4,0},{8,12},{12,8},{16,20},{20,16},{24,28},{28,24},{1,5},{5... | collective-permute-start | bytes 3145736 | tf_op jit(solution)/shard_map/ppermute | solution.py:434
  110.8 76.7 %collective-permute-start.26 = (bf16[256,1024]{1,0:T(8,128)(2,1)}, bf16[256,1024]{1,0:T(8,128)(2,1)}, u32[]{:S(2)}, u32[]{:S(2)}) collective-permute-start(bf16[256,1024]{1,0:T(8,128)(2,1)} %get-tuple-element.87), channel_id=1, source_target_pairs={{0,2},{1,3},{2,0},{3,1},{4,6},{5,7},{6,4},{7,5},{8,10},{9,11},{10,... | collective-permute-start | bytes 1572872 | tf_op jit(solution)/shard_map/ppermute | solution.py:449
  112.1 75.5 %collective-permute-start.27 = (bf16[256,1024]{1,0:T(8,128)(2,1)}, bf16[256,1024]{1,0:T(8,128)(2,1)}, u32[]{:S(2)}, u32[]{:S(2)}) collective-permute-start(bf16[256,1024]{1,0:T(8,128)(2,1)} %get-tuple-element.84), channel_id=1, source_target_pairs={{0,3},{1,0},{2,1},{3,2},{4,7},{5,4},{6,5},{7,6},{8,11},{9,8},{10,9... | collective-permute-start | bytes 1572872 | tf_op jit(solution)/shard_map/ppermute | solution.py:449
  121.9 44.9 %collective-permute-start.7 = (bf16[512,512]{1,0:T(8,128)(2,1)}, bf16[512,512]{1,0:T(8,128)(2,1)}, u32[]{:S(2)}, u32[]{:S(2)}) collective-permute-start(bf16[512,512]{1,0:T(8,128)(2,1)} %collective-permute-done.4.refs_4_.refs_2_), channel_id=1, source_target_pairs={{0,1},{1,2},{2,3},{3,0},{4,5},{5,6},{6,7},{7,4},{8,9},{9,10},{10,1... | collective-permute-start | bytes 1572872 | tf_op jit(solution)/shard_map/ppermute | solution.py:449
  127.2 60.5 %collective-permute-start.1 = (bf16[2,512,256]{2,1,0:T(8,128)(2,1)}, bf16[2,512,256]{2,1,0:T(8,128)(2,1)}, u32[]{:S(2)}, u32[]{:S(2)}) collective-permute-start(bf16[2,512,256]{2,1,0:T(8,128)(2,1)} %pad_maximum_fusion.3), channel_id=1, source_target_pairs={{0,1},{1,2},{2,3},{3,0},{4,5},{5,6},{6,7},{7,4},{8,9},{9,10},{10,1... | collective-permute-start | bytes 1572872 | tf_op jit(solution)/shard_map/ppermute | solution.py:449
  132.7 141.6 %all-to-all-start.3 = ((bf16[8,2,512,128]{3,2,1,0:T(8,128)(2,1)}), bf16[8,2,512,128]{3,2,1,0:T(8,128)(2,1)S(1)}, u32[]{:S(2)}, u32[]{:S(2)}) async-start(bf16[8,2,512,128]{3,2,1,0:T(8,128)(2,1)} %get-tuple-element.49), calls=%async_computation.3 | async-start | bytes 4194304 | tf_op jit(solution)/shard_map/all_to_all | solution.py:493
  138.7 83.5 %collective-permute-start.2 = (bf16[2,512,256]{2,1,0:T(8,128)(2,1)S(1)}, bf16[2,512,256]{2,1,0:T(8,128)(2,1)S(1)}, u32[]{:S(2)}, u32[]{:S(2)}) collective-permute-start(bf16[2,512,256]{2,1,0:T(8,128)(2,1)S(1)} %pad_maximum_fusion.4), channel_id=1, source_target_pairs={{0,2},{1,3},{2,0},{3,1},{4,6},{5,7},{6,4},{7,5},{8,10},{9,11},{10,... | collective-permute-start | bytes 1572872 | tf_op jit(solution)/shard_map/ppermute | solution.py:449
  166.8 56.1 %collective-permute-start.10 = (bf16[512,512]{1,0:T(8,128)(2,1)}, bf16[512,512]{1,0:T(8,128)(2,1)S(1)}, u32[]{:S(2)}, u32[]{:S(2)}) collective-permute-start(bf16[512,512]{1,0:T(8,128)(2,1)} %collective-permute-done.7.refs_7_.refs_2_), channel_id=1, source_target_pairs={{0,1},{1,2},{2,3},{3,0},{4,5},{5,6},{6,7},{7,4},{8,9},{9,10},{10,1... | collective-permute-start | bytes 1572872 | tf_op jit(solution)/shard_map/ppermute | solution.py:449
  187.6 35.4 %collective-permute-start.3 = (bf16[2,512,256]{2,1,0:T(8,128)(2,1)S(1)}, bf16[2,512,256]{2,1,0:T(8,128)(2,1)S(1)}, u32[]{:S(2)}, u32[]{:S(2)}) collective-permute-start(bf16[2,512,256]{2,1,0:T(8,128)(2,1)S(1)} %pad_maximum_fusion.5), channel_id=1, source_target_pairs={{0,3},{1,0},{2,1},{3,2},{4,7},{5,4},{6,5},{7,6},{8,11},{9,8},{10,9... | collective-permute-start | bytes 1572872 | tf_op jit(solution)/shard_map/ppermute | solution.py:449
  187.6 37.3 %collective-permute-start.13 = (bf16[512,512]{1,0:T(8,128)(2,1)S(1)}, bf16[512,512]{1,0:T(8,128)(2,1)S(1)}, u32[]{:S(2)}, u32[]{:S(2)}) collective-permute-start(bf16[512,512]{1,0:T(8,128)(2,1)S(1)} %copy-done.19), channel_id=1, source_target_pairs={{0,4},{4,0},{8,12},{12,8},{16,20},{20,16},{24,28},{28,24},{1,5},{5... | collective-permute-start | bytes 1572872 | tf_op jit(solution)/shard_map/ppermute | solution.py:434
  187.7 37.4 %collective-permute-start.16 = (bf16[512,512]{1,0:T(8,128)(2,1)}, bf16[512,512]{1,0:T(8,128)(2,1)S(1)}, u32[]{:S(2)}, u32[]{:S(2)}) collective-permute-start(bf16[512,512]{1,0:T(8,128)(2,1)} %collective-permute-done.4.refs_4_.refs_2_), channel_id=1, source_target_pairs={{0,4},{4,0},{8,12},{12,8},{16,20},{20,16},{24,28},{28,24},{1,5},{5... | collective-permute-start | bytes 1572872 | tf_op jit(solution)/shard_map/ppermute | solution.py:434
  227.0 35.3 %collective-permute-start.32 = (bf16[256,1024]{1,0:T(8,128)(2,1)S(1)}, bf16[256,1024]{1,0:T(8,128)(2,1)}, u32[]{:S(2)}, u32[]{:S(2)}) collective-permute-start(bf16[256,1024]{1,0:T(8,128)(2,1)S(1)} %copy-done.12), channel_id=1, source_target_pairs={{0,16},{4,20},{8,24},{12,28},{16,0},{20,4},{24,8},{28,12},{1,17},{... | collective-permute-start | bytes 1572872 | tf_op jit(solution)/shard_map/ppermute | solution.py:434
  260.4 42.4 %collective-permute-start.35 = (bf16[256,1024]{1,0:T(8,128)(2,1)}, bf16[256,1024]{1,0:T(8,128)(2,1)}, u32[]{:S(2)}, u32[]{:S(2)}) collective-permute-start(bf16[256,1024]{1,0:T(8,128)(2,1)} %collective-permute-done.27.refs_28_), channel_id=1, source_target_pairs={{0,16},{4,20},{8,24},{12,28},{16,0},{20,4},{24,8},{28,12},{1,17},{... | collective-permute-start | bytes 1572872 | tf_op jit(solution)/shard_map/ppermute | solution.py:434
  262.3 51.3 %collective-permute-start.36 = (bf16[256,1024]{1,0:T(8,128)(2,1)}, bf16[256,1024]{1,0:T(8,128)(2,1)}, u32[]{:S(2)}, u32[]{:S(2)}) collective-permute-start(bf16[256,1024]{1,0:T(8,128)(2,1)} %collective-permute-done.32.refs_33_), channel_id=1, source_target_pairs={{0,8},{4,12},{8,0},{12,4},{16,24},{20,28},{24,16},{28,20},{1,9},{5... | collective-permute-start | bytes 1572872 | tf_op jit(solution)/shard_map/ppermute | solution.py:434
  263.8 50.6 %collective-permute-start.37 = (bf16[256,1024]{1,0:T(8,128)(2,1)}, bf16[256,1024]{1,0:T(8,128)(2,1)}, u32[]{:S(2)}, u32[]{:S(2)}) collective-permute-start(bf16[256,1024]{1,0:T(8,128)(2,1)} %collective-permute-done.33.refs_34_), channel_id=1, source_target_pairs={{0,8},{4,12},{8,0},{12,4},{16,24},{20,28},{24,16},{28,20},{1,9},{5... | collective-permute-start | bytes 1572872 | tf_op jit(solution)/shard_map/ppermute | solution.py:434
  271.5 42.9 %collective-permute-start.38 = (bf16[256,1024]{1,0:T(8,128)(2,1)}, bf16[256,1024]{1,0:T(8,128)(2,1)}, u32[]{:S(2)}, u32[]{:S(2)}) collective-permute-start(bf16[256,1024]{1,0:T(8,128)(2,1)} %collective-permute-done.30.refs_31_), channel_id=1, source_target_pairs={{0,16},{4,20},{8,24},{12,28},{16,0},{20,4},{24,8},{28,12},{1,17},{... | collective-permute-start | bytes 1572872 | tf_op jit(solution)/shard_map/ppermute | solution.py:434
  274.3 43.1 %collective-permute-start.39 = (bf16[256,1024]{1,0:T(8,128)(2,1)}, bf16[256,1024]{1,0:T(8,128)(2,1)}, u32[]{:S(2)}, u32[]{:S(2)}) collective-permute-start(bf16[256,1024]{1,0:T(8,128)(2,1)} %copy-done.29), channel_id=1, source_target_pairs={{0,16},{4,20},{8,24},{12,28},{16,0},{20,4},{24,8},{28,12},{1,17},{... | collective-permute-start | bytes 1572872 | tf_op jit(solution)/shard_map/ppermute | solution.py:434
  349.2 47.9 %collective-permute-start.50 = (f32[512]{0:T(512)S(1)}, f32[512]{0:T(512)S(1)}, u32[]{:S(2)}, u32[]{:S(2)}) collective-permute-start(f32[512]{0:T(512)S(1)} %select_reduce_fusion), channel_id=1, source_target_pairs={{0,4},{4,0},{8,12},{12,8},{16,20},{20,16},{24,28},{28,24},{1,5},{5... | collective-permute-start | bytes 6152 | tf_op jit(solution)/shard_map/ppermute | solution.py:434
  397.1 43.4 %collective-permute-start.57 = (bf16[2,256,1024]{2,1,0:T(8,128)(2,1)}, bf16[2,256,1024]{2,1,0:T(8,128)(2,1)S(1)}, u32[]{:S(2)}, u32[]{:S(2)}) collective-permute-start(bf16[2,256,1024]{2,1,0:T(8,128)(2,1)} %get-tuple-element.73), channel_id=1, source_target_pairs={{0,16},{4,20},{8,24},{12,28},{16,0},{20,4},{24,8},{28,12},{1,17},{... | collective-permute-start | bytes 3145736 | tf_op jit(solution)/shard_map/ppermute | solution.py:434
  409.3 58.8 %collective-permute-start.67 = (bf16[2,256,1024]{2,1,0:T(8,128)(2,1)}, bf16[2,256,1024]{2,1,0:T(8,128)(2,1)S(1)}, u32[]{:S(2)}, u32[]{:S(2)}) collective-permute-start(bf16[2,256,1024]{2,1,0:T(8,128)(2,1)} %get-tuple-element.76), channel_id=1, source_target_pairs={{0,8},{4,12},{8,0},{12,4},{16,24},{20,28},{24,16},{28,20},{1,9},{5... | collective-permute-start | bytes 3145736 | tf_op jit(solution)/shard_map/ppermute | solution.py:434
  438.4 46.8 %collective-permute-start.51 = (bf16[2,256,1024]{2,1,0:T(8,128)(2,1)}, bf16[2,256,1024]{2,1,0:T(8,128)(2,1)}, u32[]{:S(2)}, u32[]{:S(2)}) collective-permute-start(bf16[2,256,1024]{2,1,0:T(8,128)(2,1)} %get-tuple-element.70), channel_id=1, source_target_pairs={{0,8},{4,12},{8,0},{12,4},{16,24},{20,28},{24,16},{28,20},{1,9},{5... | collective-permute-start | bytes 3145736 | tf_op jit(solution)/shard_map/ppermute | solution.py:434
  440.6 47.6 %collective-permute-start.54 = (bf16[2,256,1024]{2,1,0:T(8,128)(2,1)}, bf16[2,256,1024]{2,1,0:T(8,128)(2,1)S(1)}, u32[]{:S(2)}, u32[]{:S(2)}) collective-permute-start(bf16[2,256,1024]{2,1,0:T(8,128)(2,1)} %get-tuple-element.72), channel_id=1, source_target_pairs={{0,16},{4,20},{8,24},{12,28},{16,0},{20,4},{24,8},{28,12},{1,17},{... | collective-permute-start | bytes 3145736 | tf_op jit(solution)/shard_map/ppermute | solution.py:434
  474.8 37.9 %collective-permute-start.41 = (bf16[2,512,256]{2,1,0:T(8,128)(2,1)}, bf16[2,512,256]{2,1,0:T(8,128)(2,1)}, u32[]{:S(2)}, u32[]{:S(2)}) collective-permute-start(bf16[2,512,256]{2,1,0:T(8,128)(2,1)} %get-tuple-element.65), channel_id=1, source_target_pairs={{0,2},{1,3},{2,0},{3,1},{4,6},{5,7},{6,4},{7,5},{8,10},{9,11},{10,... | collective-permute-start | bytes 1572872 | tf_op jit(solution)/shard_map/ppermute | solution.py:449
  (110 other events, 2105.7 us)
